TPU v7x, 256 devices: a whole 4x4x8 slice. The times are simulated.
256 devices in a mesh: area: 32 (over y, x, core), pop: 8 (over z).
Axes of the slice: x: 4, y: 4, z: 8, core: 2. Of those that a mesh axis runs over, the one named last changes fastest.
Arguments:
- history: bfloat16 [4, 32, 64, 32, 128], P(None, 'area', 'pop'), may hold values from -1 to 1
- external: bfloat16 [32, 64, 32, 128], P('area', 'pop'), may hold values from -6 to 6
- leak_rate: float32 [32, 64, 128], P('area', 'pop'), may hold values from 0.05 to 1
- intra_index: int32 [32, 64, 32], P('area', 'pop'), may hold values from 0 to 63
- intra_weight: bfloat16 [32, 64, 32, 128, 128], P('area', 'pop'), may hold values from -0.09375 to 0.09375
- inter_pick: int32 [32, 64, 12], P('area', 'pop'), may hold values from 0 to 1
- inter_weight: bfloat16 [32, 64, 12, 128, 128], P('area', 'pop'), may hold values from -0.15625 to 0.15625
- source_area: int32 [32, 12], replicated, may hold values from 0 to 31, as said below
- delays: int32 [32, 12], replicated, may hold values from 1 to 3
- live_blocks: int32 [32], replicated, may hold values from 8 to 64, as said below
Outputs:
- activity: float32 [32, 64, 32, 128], P('area', 'pop')
Inputs may be any that keep to these rules, and one draw needn't show every extreme that they name: `source_area`: the 12 source areas of an area are distinct and differ from the area itself. `live_blocks`: some area is fully populated and some has 8 populated blocks.
All inputs are finite; a program needn't handle non-finite values.
Results may differ from a plain program's by a relative error of at most 0.0014.
Values may be sent and summed in bfloat16 or wider, within the bound.
No kernel may reach another device: no remote copies, remote signals or barrier semaphores. Data moves between devices by JAX's collectives and lax.ppermute only.
A program may use at most 64 MiB of HBM per device.

v0:
```python
import jax
import jax.numpy as jnp
from jax import lax
from jax.sharding import PartitionSpec as P

SEND_DEV = 2
STEPS = 10


def shards(
    history,
    external,
    leak_rate,
    intra_index,
    intra_weight,
    inter_pick,
    inter_weight,
    source_area,
    delays,
    live_blocks,
):
    area_pos = lax.axis_index("area")
    pop_pos = lax.axis_index("pop")
    blk_local = history.shape[2]
    edge_count = inter_pick.shape[2]
    block_ids = pop_pos * blk_local + jnp.arange(blk_local, dtype=jnp.int32)
    alive_mask = (block_ids < live_blocks[area_pos]).astype(jnp.float32)[:, None, None]
    own_hist = (history[:, 0].astype(jnp.float32) * alive_mask[None]).astype(jnp.bfloat16)
    activity = own_hist[0].astype(jnp.float32)
    my_source = source_area[area_pos]
    tile_index = intra_index[0]
    w_inner = intra_weight[0]
    w_outer = inter_weight[0]
    flat_pick = jnp.arange(edge_count, dtype=jnp.int32)[None, :] * SEND_DEV + inter_pick[0]
    leak_cells = leak_rate[0][:, None, :]
    drive_ext = external[0].astype(jnp.float32)

    def advance(activity, rate_now, edge_rows):
        area_rates = lax.all_gather(rate_now, "pop", axis=0, tiled=True)
        tile_rows = jnp.take(area_rates, tile_index, axis=0)
        inner_term = jnp.einsum(
            "rkji,rktj->rti", w_inner, tile_rows, preferred_element_type=jnp.float32
        )
        flat_rows = edge_rows.reshape((edge_count * SEND_DEV,) + edge_rows.shape[2:])
        source_rows = jnp.take(flat_rows, flat_pick, axis=0)
        outer_term = jnp.einsum(
            "rkji,rktj->rti", w_outer, source_rows, preferred_element_type=jnp.float32
        )
        drive_term = jnp.tanh(inner_term + outer_term + drive_ext)
        return alive_mask * ((1.0 - leak_cells) * activity + leak_cells * drive_term)

    delay_to = jnp.sum(jnp.where(source_area == area_pos, delays, 0), axis=1)
    edge_flag = (delay_to > 0).astype(jnp.bfloat16)[:, None, None, None]

    def turn_slots(position, carried):
        activity, sent_hist, rate_now = carried
        chosen = jnp.take(sent_hist, delay_to, axis=0) * edge_flag
        received = lax.all_to_all(chosen, "area", split_axis=0, concat_axis=0, tiled=True)
        edge_rows = jnp.take(received, my_source, axis=0)
        activity = advance(activity, rate_now, edge_rows)
        rate_now = activity.astype(jnp.bfloat16)
        sent_hist = jnp.concatenate([rate_now[None, :SEND_DEV], sent_hist[:-1]], 0)
        return (activity, sent_hist, rate_now)

    activity, sent_hist, rate_now = lax.fori_loop(
        0, STEPS, turn_slots, (activity, own_hist[:, :SEND_DEV], own_hist[0])
    )
    return activity[None]


def solution(mesh):
    placed = (
        P(None, "area", "pop", None, None),
        P("area", "pop", None, None),
        P("area", "pop", None),
        P("area", "pop", None),
        P("area", "pop", None, None, None),
        P("area", "pop", None),
        P("area", "pop", None, None, None),
        P(),
        P(),
        P(),
    )
    return jax.shard_map(
        shards, mesh=mesh, in_specs=placed, out_specs=P("area", "pop", None, None), check_vma=False
    )
```

profile of v0, /device:TPU:4, one launch (start us, length us, event | category | flops | bytes accessed | tf_op | source)
XLA Modules:
  0.0 475.0 jit_solution(8111666128941133246)
XLA Ops:
  0.0 1.3 dynamic_slice.6
  1.9 1.1 fusion.23
  3.0 1.5 slice_bitcast_fusion.1
  6.8 467.5 %while.15 = (s32[]{:T(128)}, f32[8,32,128]{2,1,0:T(8,128)S(1)}, bf16[4,2,32,128]{3,2,1,0:T(8,128)(2,1)S(1)}, bf16[8,32,128]{2,1,0:T(8,128)(2,1)}, f32[8,1,128]{2...) while((s32[]{:T(128)}, f32[8,32,128]{2,1,0:T(8,128)S(1)}, ...), condition=%wide.region_2.3_spmd.clone, body=%wide.region_1.2_spmd.clone.sunk | while | flops 371433984 | bytes 26279644 | solution.py:65
  7.5 0.9 select_multiply_fusion.2
  8.5 7.6 %all-to-all-start = ((bf16[32,2,32,128]{3,2,1,0:T(8,128)(2,1)}), bf16[32,2,32,128]{3,2,1,0:T(8,128)(2,1)S(1)}, u32[]{:S(2)}, u32[]{:S(2)}) async-start(bf16[32,2,32,128]{3,2,1,0:T(8,128)(2,1)} %select_multiply_fusion.2), calls=%async_computation | async-start | bytes 1048576 | tf_op jit(solution)/shard_map/while/body/eval_jaxpr/all_to_all | solution.py:58
  16.2 29.3 %all_gather.5 = bf16[64,32,128]{2,1,0:T(8,128)(2,1)S(1)} all-gather(bf16[8,32,128]{2,1,0:T(8,128)(2,1)} %get-tuple-element.261), channel_id=1, replica_groups=mesh['area'=32,'pop'=8] {'pop'}, dimensions={0}, use_global_device_ids=true | all-gather | bytes 589824 | tf_op jit(solution)/shard_map/while/body/eval_jaxpr/all_gather | solution.py:39
  45.8 1.0 gather_fusion
  47.4 4.3 fusion.40
  53.2 3.2 fusion.44
  57.9 0.9 select_multiply_fusion.2
  58.8 7.2 %all-to-all-start = ((bf16[32,2,32,128]{3,2,1,0:T(8,128)(2,1)}), bf16[32,2,32,128]{3,2,1,0:T(8,128)(2,1)S(1)}, u32[]{:S(2)}, u32[]{:S(2)}) async-start(bf16[32,2,32,128]{3,2,1,0:T(8,128)(2,1)} %select_multiply_fusion.2), calls=%async_computation | async-start | bytes 1048576 | tf_op jit(solution)/shard_map/while/body/eval_jaxpr/all_to_all | solution.py:58
  66.1 25.6 %all_gather.5 = bf16[64,32,128]{2,1,0:T(8,128)(2,1)S(1)} all-gather(bf16[8,32,128]{2,1,0:T(8,128)(2,1)} %get-tuple-element.261), channel_id=1, replica_groups=mesh['area'=32,'pop'=8] {'pop'}, dimensions={0}, use_global_device_ids=true | all-gather | bytes 589824 | tf_op jit(solution)/shard_map/while/body/eval_jaxpr/all_gather | solution.py:39
  92.1 1.0 gather_fusion
  93.7 4.3 fusion.40
  99.5 3.2 fusion.44
  104.2 0.9 select_multiply_fusion.2
  105.1 7.3 %all-to-all-start = ((bf16[32,2,32,128]{3,2,1,0:T(8,128)(2,1)}), bf16[32,2,32,128]{3,2,1,0:T(8,128)(2,1)S(1)}, u32[]{:S(2)}, u32[]{:S(2)}) async-start(bf16[32,2,32,128]{3,2,1,0:T(8,128)(2,1)} %select_multiply_fusion.2), calls=%async_computation | async-start | bytes 1048576 | tf_op jit(solution)/shard_map/while/body/eval_jaxpr/all_to_all | solution.py:58
  112.5 25.6 %all_gather.5 = bf16[64,32,128]{2,1,0:T(8,128)(2,1)S(1)} all-gather(bf16[8,32,128]{2,1,0:T(8,128)(2,1)} %get-tuple-element.261), channel_id=1, replica_groups=mesh['area'=32,'pop'=8] {'pop'}, dimensions={0}, use_global_device_ids=true | all-gather | bytes 589824 | tf_op jit(solution)/shard_map/while/body/eval_jaxpr/all_gather | solution.py:39
  138.5 1.0 gather_fusion
  140.1 4.3 fusion.40
  145.9 3.2 fusion.44
  150.5 0.9 select_multiply_fusion.2
  151.5 7.3 %all-to-all-start = ((bf16[32,2,32,128]{3,2,1,0:T(8,128)(2,1)}), bf16[32,2,32,128]{3,2,1,0:T(8,128)(2,1)S(1)}, u32[]{:S(2)}, u32[]{:S(2)}) async-start(bf16[32,2,32,128]{3,2,1,0:T(8,128)(2,1)} %select_multiply_fusion.2), calls=%async_computation | async-start | bytes 1048576 | tf_op jit(solution)/shard_map/while/body/eval_jaxpr/all_to_all | solution.py:58
  158.9 25.6 %all_gather.5 = bf16[64,32,128]{2,1,0:T(8,128)(2,1)S(1)} all-gather(bf16[8,32,128]{2,1,0:T(8,128)(2,1)} %get-tuple-element.261), channel_id=1, replica_groups=mesh['area'=32,'pop'=8] {'pop'}, dimensions={0}, use_global_device_ids=true | all-gather | bytes 589824 | tf_op jit(solution)/shard_map/while/body/eval_jaxpr/all_gather | solution.py:39
  184.9 1.0 gather_fusion
  186.5 4.3 fusion.40
  192.3 3.2 fusion.44
  196.9 0.9 select_multiply_fusion.2
  197.9 7.3 %all-to-all-start = ((bf16[32,2,32,128]{3,2,1,0:T(8,128)(2,1)}), bf16[32,2,32,128]{3,2,1,0:T(8,128)(2,1)S(1)}, u32[]{:S(2)}, u32[]{:S(2)}) async-start(bf16[32,2,32,128]{3,2,1,0:T(8,128)(2,1)} %select_multiply_fusion.2), calls=%async_computation | async-start | bytes 1048576 | tf_op jit(solution)/shard_map/while/body/eval_jaxpr/all_to_all | solution.py:58
  205.2 25.6 %all_gather.5 = bf16[64,32,128]{2,1,0:T(8,128)(2,1)S(1)} all-gather(bf16[8,32,128]{2,1,0:T(8,128)(2,1)} %get-tuple-element.261), channel_id=1, replica_groups=mesh['area'=32,'pop'=8] {'pop'}, dimensions={0}, use_global_device_ids=true | all-gather | bytes 589824 | tf_op jit(solution)/shard_map/while/body/eval_jaxpr/all_gather | solution.py:39
  231.3 1.0 gather_fusion
  232.9 4.3 fusion.40
  238.6 3.2 fusion.44
  243.3 0.9 select_multiply_fusion.2
  244.2 7.2 %all-to-all-start = ((bf16[32,2,32,128]{3,2,1,0:T(8,128)(2,1)}), bf16[32,2,32,128]{3,2,1,0:T(8,128)(2,1)S(1)}, u32[]{:S(2)}, u32[]{:S(2)}) async-start(bf16[32,2,32,128]{3,2,1,0:T(8,128)(2,1)} %select_multiply_fusion.2), calls=%async_computation | async-start | bytes 1048576 | tf_op jit(solution)/shard_map/while/body/eval_jaxpr/all_to_all | solution.py:58
  251.6 25.6 %all_gather.5 = bf16[64,32,128]{2,1,0:T(8,128)(2,1)S(1)} all-gather(bf16[8,32,128]{2,1,0:T(8,128)(2,1)} %get-tuple-element.261), channel_id=1, replica_groups=mesh['area'=32,'pop'=8] {'pop'}, dimensions={0}, use_global_device_ids=true | all-gather | bytes 589824 | tf_op jit(solution)/shard_map/while/body/eval_jaxpr/all_gather | solution.py:39
  277.6 1.0 gather_fusion
  279.2 4.3 fusion.40
  285.0 3.2 fusion.44
  289.7 0.9 select_multiply_fusion.2
  290.6 7.2 %all-to-all-start = ((bf16[32,2,32,128]{3,2,1,0:T(8,128)(2,1)}), bf16[32,2,32,128]{3,2,1,0:T(8,128)(2,1)S(1)}, u32[]{:S(2)}, u32[]{:S(2)}) async-start(bf16[32,2,32,128]{3,2,1,0:T(8,128)(2,1)} %select_multiply_fusion.2), calls=%async_computation | async-start | bytes 1048576 | tf_op jit(solution)/shard_map/while/body/eval_jaxpr/all_to_all | solution.py:58
  297.9 25.7 %all_gather.5 = bf16[64,32,128]{2,1,0:T(8,128)(2,1)S(1)} all-gather(bf16[8,32,128]{2,1,0:T(8,128)(2,1)} %get-tuple-element.261), channel_id=1, replica_groups=mesh['area'=32,'pop'=8] {'pop'}, dimensions={0}, use_global_device_ids=true | all-gather | bytes 589824 | tf_op jit(solution)/shard_map/while/body/eval_jaxpr/all_gather | solution.py:39
  324.0 1.0 gather_fusion
  325.6 4.3 fusion.40
  331.3 3.2 fusion.44
  336.0 0.9 select_multiply_fusion.2
  337.0 7.2 %all-to-all-start = ((bf16[32,2,32,128]{3,2,1,0:T(8,128)(2,1)}), bf16[32,2,32,128]{3,2,1,0:T(8,128)(2,1)S(1)}, u32[]{:S(2)}, u32[]{:S(2)}) async-start(bf16[32,2,32,128]{3,2,1,0:T(8,128)(2,1)} %select_multiply_fusion.2), calls=%async_computation | async-start | bytes 1048576 | tf_op jit(solution)/shard_map/while/body/eval_jaxpr/all_to_all | solution.py:58
  344.3 25.7 %all_gather.5 = bf16[64,32,128]{2,1,0:T(8,128)(2,1)S(1)} all-gather(bf16[8,32,128]{2,1,0:T(8,128)(2,1)} %get-tuple-element.261), channel_id=1, replica_groups=mesh['area'=32,'pop'=8] {'pop'}, dimensions={0}, use_global_device_ids=true | all-gather | bytes 589824 | tf_op jit(solution)/shard_map/while/body/eval_jaxpr/all_gather | solution.py:39
  370.3 1.0 gather_fusion
  371.9 4.3 fusion.40
  377.7 3.2 fusion.44
  382.4 0.9 select_multiply_fusion.2
  383.3 7.2 %all-to-all-start = ((bf16[32,2,32,128]{3,2,1,0:T(8,128)(2,1)}), bf16[32,2,32,128]{3,2,1,0:T(8,128)(2,1)S(1)}, u32[]{:S(2)}, u32[]{:S(2)}) async-start(bf16[32,2,32,128]{3,2,1,0:T(8,128)(2,1)} %select_multiply_fusion.2), calls=%async_computation | async-start | bytes 1048576 | tf_op jit(solution)/shard_map/while/body/eval_jaxpr/all_to_all | solution.py:58
  390.6 25.7 %all_gather.5 = bf16[64,32,128]{2,1,0:T(8,128)(2,1)S(1)} all-gather(bf16[8,32,128]{2,1,0:T(8,128)(2,1)} %get-tuple-element.261), channel_id=1, replica_groups=mesh['area'=32,'pop'=8] {'pop'}, dimensions={0}, use_global_device_ids=true | all-gather | bytes 589824 | tf_op jit(solution)/shard_map/while/body/eval_jaxpr/all_gather | solution.py:39
  416.6 1.0 gather_fusion
  418.3 4.3 fusion.40
  424.0 3.2 fusion.44
  428.7 0.9 select_multiply_fusion.2
  429.6 7.2 %all-to-all-start = ((bf16[32,2,32,128]{3,2,1,0:T(8,128)(2,1)}), bf16[32,2,32,128]{3,2,1,0:T(8,128)(2,1)S(1)}, u32[]{:S(2)}, u32[]{:S(2)}) async-start(bf16[32,2,32,128]{3,2,1,0:T(8,128)(2,1)} %select_multiply_fusion.2), calls=%async_computation | async-start | bytes 1048576 | tf_op jit(solution)/shard_map/while/body/eval_jaxpr/all_to_all | solution.py:58
  436.9 25.7 %all_gather.5 = bf16[64,32,128]{2,1,0:T(8,128)(2,1)S(1)} all-gather(bf16[8,32,128]{2,1,0:T(8,128)(2,1)} %get-tuple-element.261), channel_id=1, replica_groups=mesh['area'=32,'pop'=8] {'pop'}, dimensions={0}, use_global_device_ids=true | all-gather | bytes 589824 | tf_op jit(solution)/shard_map/while/body/eval_jaxpr/all_gather | solution.py:39
  463.0 1.0 gather_fusion
  464.6 4.3 fusion.40
  470.3 3.2 fusion.44
  (309 shorter events, 41.6 us)
Async XLA Ops:
  6.8 9.3 %copy-start.1 = (s32[8,32]{1,0:T(8,128)S(1)}, s32[8,32]{1,0:T(8,128)}, u32[]{:S(2)}) copy-start(s32[8,32]{1,0:T(8,128)} %get-tuple-element.279) | copy-start | bytes 3076 | tf_op jit(solution)/shard_map/while
  6.8 39.0 %copy-start.2 = (f32[8,1,128]{2,0,1:T(8,128)S(1)}, f32[8,1,128]{2,0,1:T(8,128)}, u32[]{:S(2)}) copy-start(f32[8,1,128]{2,0,1:T(8,128)} %get-tuple-element.278) | copy-start | bytes 12292 | tf_op jit(solution)/shard_map/while
  8.5 43.3 %all-to-all-start = ((bf16[32,2,32,128]{3,2,1,0:T(8,128)(2,1)}), bf16[32,2,32,128]{3,2,1,0:T(8,128)(2,1)S(1)}, u32[]{:S(2)}, u32[]{:S(2)}) async-start(bf16[32,2,32,128]{3,2,1,0:T(8,128)(2,1)} %select_multiply_fusion.2), calls=%async_computation | async-start | bytes 1048576 | tf_op jit(solution)/shard_map/while/body/eval_jaxpr/all_to_all | solution.py:58
  57.1 8.9 %copy-start.1 = (s32[8,32]{1,0:T(8,128)S(1)}, s32[8,32]{1,0:T(8,128)}, u32[]{:S(2)}) copy-start(s32[8,32]{1,0:T(8,128)} %get-tuple-element.279) | copy-start | bytes 3076 | tf_op jit(solution)/shard_map/while
  57.1 34.9 %copy-start.2 = (f32[8,1,128]{2,0,1:T(8,128)S(1)}, f32[8,1,128]{2,0,1:T(8,128)}, u32[]{:S(2)}) copy-start(f32[8,1,128]{2,0,1:T(8,128)} %get-tuple-element.278) | copy-start | bytes 12292 | tf_op jit(solution)/shard_map/while
  58.8 39.3 %all-to-all-start = ((bf16[32,2,32,128]{3,2,1,0:T(8,128)(2,1)}), bf16[32,2,32,128]{3,2,1,0:T(8,128)(2,1)S(1)}, u32[]{:S(2)}, u32[]{:S(2)}) async-start(bf16[32,2,32,128]{3,2,1,0:T(8,128)(2,1)} %select_multiply_fusion.2), calls=%async_computation | async-start | bytes 1048576 | tf_op jit(solution)/shard_map/while/body/eval_jaxpr/all_to_all | solution.py:58
  103.4 9.0 %copy-start.1 = (s32[8,32]{1,0:T(8,128)S(1)}, s32[8,32]{1,0:T(8,128)}, u32[]{:S(2)}) copy-start(s32[8,32]{1,0:T(8,128)} %get-tuple-element.279) | copy-start | bytes 3076 | tf_op jit(solution)/shard_map/while
  103.5 35.0 %copy-start.2 = (f32[8,1,128]{2,0,1:T(8,128)S(1)}, f32[8,1,128]{2,0,1:T(8,128)}, u32[]{:S(2)}) copy-start(f32[8,1,128]{2,0,1:T(8,128)} %get-tuple-element.278) | copy-start | bytes 12292 | tf_op jit(solution)/shard_map/while
  105.1 39.4 %all-to-all-start = ((bf16[32,2,32,128]{3,2,1,0:T(8,128)(2,1)}), bf16[32,2,32,128]{3,2,1,0:T(8,128)(2,1)S(1)}, u32[]{:S(2)}, u32[]{:S(2)}) async-start(bf16[32,2,32,128]{3,2,1,0:T(8,128)(2,1)} %select_multiply_fusion.2), calls=%async_computation | async-start | bytes 1048576 | tf_op jit(solution)/shard_map/while/body/eval_jaxpr/all_to_all | solution.py:58
  149.8 9.0 %copy-start.1 = (s32[8,32]{1,0:T(8,128)S(1)}, s32[8,32]{1,0:T(8,128)}, u32[]{:S(2)}) copy-start(s32[8,32]{1,0:T(8,128)} %get-tuple-element.279) | copy-start | bytes 3076 | tf_op jit(solution)/shard_map/while
  149.8 35.0 %copy-start.2 = (f32[8,1,128]{2,0,1:T(8,128)S(1)}, f32[8,1,128]{2,0,1:T(8,128)}, u32[]{:S(2)}) copy-start(f32[8,1,128]{2,0,1:T(8,128)} %get-tuple-element.278) | copy-start | bytes 12292 | tf_op jit(solution)/shard_map/while
  151.5 39.4 %all-to-all-start = ((bf16[32,2,32,128]{3,2,1,0:T(8,128)(2,1)}), bf16[32,2,32,128]{3,2,1,0:T(8,128)(2,1)S(1)}, u32[]{:S(2)}, u32[]{:S(2)}) async-start(bf16[32,2,32,128]{3,2,1,0:T(8,128)(2,1)} %select_multiply_fusion.2), calls=%async_computation | async-start | bytes 1048576 | tf_op jit(solution)/shard_map/while/body/eval_jaxpr/all_to_all | solution.py:58
  196.2 8.9 %copy-start.1 = (s32[8,32]{1,0:T(8,128)S(1)}, s32[8,32]{1,0:T(8,128)}, u32[]{:S(2)}) copy-start(s32[8,32]{1,0:T(8,128)} %get-tuple-element.279) | copy-start | bytes 3076 | tf_op jit(solution)/shard_map/while
  196.2 35.0 %copy-start.2 = (f32[8,1,128]{2,0,1:T(8,128)S(1)}, f32[8,1,128]{2,0,1:T(8,128)}, u32[]{:S(2)}) copy-start(f32[8,1,128]{2,0,1:T(8,128)} %get-tuple-element.278) | copy-start | bytes 12292 | tf_op jit(solution)/shard_map/while
  197.9 39.3 %all-to-all-start = ((bf16[32,2,32,128]{3,2,1,0:T(8,128)(2,1)}), bf16[32,2,32,128]{3,2,1,0:T(8,128)(2,1)S(1)}, u32[]{:S(2)}, u32[]{:S(2)}) async-start(bf16[32,2,32,128]{3,2,1,0:T(8,128)(2,1)} %select_multiply_fusion.2), calls=%async_computation | async-start | bytes 1048576 | tf_op jit(solution)/shard_map/while/body/eval_jaxpr/all_to_all | solution.py:58
  242.6 8.9 %copy-start.1 = (s32[8,32]{1,0:T(8,128)S(1)}, s32[8,32]{1,0:T(8,128)}, u32[]{:S(2)}) copy-start(s32[8,32]{1,0:T(8,128)} %get-tuple-element.279) | copy-start | bytes 3076 | tf_op jit(solution)/shard_map/while
  242.6 35.0 %copy-start.2 = (f32[8,1,128]{2,0,1:T(8,128)S(1)}, f32[8,1,128]{2,0,1:T(8,128)}, u32[]{:S(2)}) copy-start(f32[8,1,128]{2,0,1:T(8,128)} %get-tuple-element.278) | copy-start | bytes 12292 | tf_op jit(solution)/shard_map/while
  244.2 39.3 %all-to-all-start = ((bf16[32,2,32,128]{3,2,1,0:T(8,128)(2,1)}), bf16[32,2,32,128]{3,2,1,0:T(8,128)(2,1)S(1)}, u32[]{:S(2)}, u32[]{:S(2)}) async-start(bf16[32,2,32,128]{3,2,1,0:T(8,128)(2,1)} %select_multiply_fusion.2), calls=%async_computation | async-start | bytes 1048576 | tf_op jit(solution)/shard_map/while/body/eval_jaxpr/all_to_all | solution.py:58
  289.0 8.9 %copy-start.1 = (s32[8,32]{1,0:T(8,128)S(1)}, s32[8,32]{1,0:T(8,128)}, u32[]{:S(2)}) copy-start(s32[8,32]{1,0:T(8,128)} %get-tuple-element.279) | copy-start | bytes 3076 | tf_op jit(solution)/shard_map/while
  289.0 35.0 %copy-start.2 = (f32[8,1,128]{2,0,1:T(8,128)S(1)}, f32[8,1,128]{2,0,1:T(8,128)}, u32[]{:S(2)}) copy-start(f32[8,1,128]{2,0,1:T(8,128)} %get-tuple-element.278) | copy-start | bytes 12292 | tf_op jit(solution)/shard_map/while
  290.6 39.3 %all-to-all-start = ((bf16[32,2,32,128]{3,2,1,0:T(8,128)(2,1)}), bf16[32,2,32,128]{3,2,1,0:T(8,128)(2,1)S(1)}, u32[]{:S(2)}, u32[]{:S(2)}) async-start(bf16[32,2,32,128]{3,2,1,0:T(8,128)(2,1)} %select_multiply_fusion.2), calls=%async_computation | async-start | bytes 1048576 | tf_op jit(solution)/shard_map/while/body/eval_jaxpr/all_to_all | solution.py:58
  335.3 8.9 %copy-start.1 = (s32[8,32]{1,0:T(8,128)S(1)}, s32[8,32]{1,0:T(8,128)}, u32[]{:S(2)}) copy-start(s32[8,32]{1,0:T(8,128)} %get-tuple-element.279) | copy-start | bytes 3076 | tf_op jit(solution)/shard_map/while
  335.3 35.0 %copy-start.2 = (f32[8,1,128]{2,0,1:T(8,128)S(1)}, f32[8,1,128]{2,0,1:T(8,128)}, u32[]{:S(2)}) copy-start(f32[8,1,128]{2,0,1:T(8,128)} %get-tuple-element.278) | copy-start | bytes 12292 | tf_op jit(solution)/shard_map/while
  337.0 39.3 %all-to-all-start = ((bf16[32,2,32,128]{3,2,1,0:T(8,128)(2,1)}), bf16[32,2,32,128]{3,2,1,0:T(8,128)(2,1)S(1)}, u32[]{:S(2)}, u32[]{:S(2)}) async-start(bf16[32,2,32,128]{3,2,1,0:T(8,128)(2,1)} %select_multiply_fusion.2), calls=%async_computation | async-start | bytes 1048576 | tf_op jit(solution)/shard_map/while/body/eval_jaxpr/all_to_all | solution.py:58
  381.6 8.9 %copy-start.1 = (s32[8,32]{1,0:T(8,128)S(1)}, s32[8,32]{1,0:T(8,128)}, u32[]{:S(2)}) copy-start(s32[8,32]{1,0:T(8,128)} %get-tuple-element.279) | copy-start | bytes 3076 | tf_op jit(solution)/shard_map/while
  381.6 35.0 %copy-start.2 = (f32[8,1,128]{2,0,1:T(8,128)S(1)}, f32[8,1,128]{2,0,1:T(8,128)}, u32[]{:S(2)}) copy-start(f32[8,1,128]{2,0,1:T(8,128)} %get-tuple-element.278) | copy-start | bytes 12292 | tf_op jit(solution)/shard_map/while
  383.3 39.3 %all-to-all-start = ((bf16[32,2,32,128]{3,2,1,0:T(8,128)(2,1)}), bf16[32,2,32,128]{3,2,1,0:T(8,128)(2,1)S(1)}, u32[]{:S(2)}, u32[]{:S(2)}) async-start(bf16[32,2,32,128]{3,2,1,0:T(8,128)(2,1)} %select_multiply_fusion.2), calls=%async_computation | async-start | bytes 1048576 | tf_op jit(solution)/shard_map/while/body/eval_jaxpr/all_to_all | solution.py:58
  428.0 8.9 %copy-start.1 = (s32[8,32]{1,0:T(8,128)S(1)}, s32[8,32]{1,0:T(8,128)}, u32[]{:S(2)}) copy-start(s32[8,32]{1,0:T(8,128)} %get-tuple-element.279) | copy-start | bytes 3076 | tf_op jit(solution)/shard_map/while
  428.0 35.0 %copy-start.2 = (f32[8,1,128]{2,0,1:T(8,128)S(1)}, f32[8,1,128]{2,0,1:T(8,128)}, u32[]{:S(2)}) copy-start(f32[8,1,128]{2,0,1:T(8,128)} %get-tuple-element.278) | copy-start | bytes 12292 | tf_op jit(solution)/shard_map/while
  429.6 39.3 %all-to-all-start = ((bf16[32,2,32,128]{3,2,1,0:T(8,128)(2,1)}), bf16[32,2,32,128]{3,2,1,0:T(8,128)(2,1)S(1)}, u32[]{:S(2)}, u32[]{:S(2)}) async-start(bf16[32,2,32,128]{3,2,1,0:T(8,128)(2,1)} %select_multiply_fusion.2), calls=%async_computation | async-start | bytes 1048576 | tf_op jit(solution)/shard_map/while/body/eval_jaxpr/all_to_all | solution.py:58
  474.3 0.7 copy-start
where the time goes:
time: 478 us; the launch traced here: 475 us
  blocking collectives  260 us (54%)
  matrix products  75.3 us (16%)
  starting transfers between devices  72.8 us (15%)
  local copies, waits for them, and re-layouts  42.8 us (9%)
  other arithmetic  21.9 us (5%)
    all_gather x10, blocking collectives, advance(): area_rates = lax.all_gather(rate_now, 'pop', axis=0, tiled=True)  260 us
    all_to_all x10, starting transfers between devices, turn_slots(): lax.all_to_all(chosen, 'area', split_axis=0, concat_axis=0, tiled=True)  72.8 us
    dot_general x10, matrix products, advance(): jnp.einsum('rkji,rktj->rti', w_inner, tile_rows, preferred_element_type=j...  43.2 us
    dot_general x10, matrix products, advance(): jnp.einsum('rkji,rktj->rti', w_outer, source_rows, preferred_element_type...  32.1 us
    gather x10, local copies, waits for them, and re-layouts, advance(): tile_rows = jnp.take(area_rates, tile_index, axis=0)  9.94 us
  transfers between devices with their start and end apart: 10, of which 0 were waited for; matrix products, arithmetic and copies ran while one was open for 13% of the time, Pallas kernels for 0%

commit v1 on v0

v1 whole, which is shorter than its diff:
```python
import functools
import jax
import jax.numpy as jnp
from jax import lax
from jax.experimental import pallas as pl
from jax.experimental.pallas import tpu as pltpu
from jax.sharding import PartitionSpec as P

SEND_DEV = 2
STEPS = 10
DMAX = 3

VMEM = pl.BlockSpec(memory_space=pltpu.VMEM)
SMEM = pl.BlockSpec(memory_space=pltpu.SMEM)


def tile_product(rows, weights):
    lhs = jnp.concatenate(rows, axis=1)
    rhs = weights.reshape(lhs.shape[1], weights.shape[-1])
    return lax.dot_general(
        lhs, rhs, (((1,), (0,)), ((), ())), preferred_element_type=jnp.float32
    )


def choose(delay_ref, recent_ref, chosen_ref):
    for area in range(chosen_ref.shape[0]):
        chosen_ref[area] = recent_ref[delay_ref[area]]


def first_kernel(count_ref, delay_ref, history_ref, activity_ref, spread_ref, now_ref, next_ref, recent_ref, older_ref):
    blocks = activity_ref.shape[0]
    count = count_ref[0]
    for block in range(blocks):
        alive = jnp.where(block < count, 1.0, 0.0)
        rates = (history_ref[0, block].astype(jnp.float32) * alive).astype(jnp.bfloat16)
        activity_ref[block] = rates.astype(jnp.float32)
        for pop in range(spread_ref.shape[0]):
            spread_ref[pop, block] = rates
    for block in range(SEND_DEV):
        alive = jnp.where(block < count, 1.0, 0.0)
        for age in range(DMAX + 1):
            rates = (history_ref[age, block].astype(jnp.float32) * alive).astype(jnp.bfloat16)
            older_ref[age, block] = rates
            if age < DMAX:
                recent_ref[age, block] = rates
    choose(delay_ref, older_ref.at[1:], now_ref)
    choose(delay_ref, older_ref, next_ref)


def inter_kernel(source_ref, pick_ref, received_ref, weight_ref, external_ref, out_ref):
    blocks, edges = weight_ref.shape[:2]

    def body(block, carry):
        rows = [received_ref[source_ref[e], pick_ref[block, e]] for e in range(edges)]
        total = tile_product(rows, weight_ref[block])
        out_ref[block] = total + external_ref[block].astype(jnp.float32)
        return carry

    lax.fori_loop(0, blocks, body, 0)


def intra_kernel(last, choosing, count_ref, delay_ref, index_ref, rates_ref, weight_ref, outer_ref, leak_ref, activity_ref, *refs):
    if choosing:
        recent_in_ref, activity_out_ref, spread_ref, recent_ref, chosen_ref = refs
    elif last:
        (activity_out_ref,) = refs
    else:
        activity_out_ref, spread_ref = refs
    blocks, tiles = weight_ref.shape[:2]
    count = count_ref[0]

    def body(block, carry):
        rows = [rates_ref[index_ref[block, k]] for k in range(tiles)]
        current = tile_product(rows, weight_ref[block]) + outer_ref[block]
        leak = leak_ref[block]
        alive = jnp.where(block < count, 1.0, 0.0)
        new = alive * ((1.0 - leak) * activity_ref[block] + leak * jnp.tanh(current))
        activity_out_ref[block] = new
        if not last:
            rates = new.astype(jnp.bfloat16)
            for pop in range(spread_ref.shape[0]):
                spread_ref[pop, block] = rates
        return carry

    lax.fori_loop(0, blocks, body, 0)
    if choosing:
        recent_ref[0] = spread_ref[0, :SEND_DEV]
        for age in range(1, DMAX):
            recent_ref[age] = recent_in_ref[age - 1]
        choose(delay_ref, recent_ref, chosen_ref)


def shards(
    history,
    external,
    leak_rate,
    intra_index,
    intra_weight,
    inter_pick,
    inter_weight,
    source_area,
    delays,
    live_blocks,
):
    area_pos = lax.axis_index("area")
    pop_pos = lax.axis_index("pop")
    areas = lax.axis_size("area")
    pops = lax.axis_size("pop")
    history = history[:, 0]
    blocks, conds, units = history.shape[1:]
    tiles = intra_index.shape[2]
    edges = inter_pick.shape[2]
    count = (live_blocks[area_pos] - pop_pos * blocks)[None]
    delay_to = jnp.sum(jnp.where(source_area == area_pos, delays, 0), axis=1)
    delay_to = jnp.maximum(delay_to, 1) - 1
    my_source = source_area[area_pos]
    index = intra_index[0]
    pick = inter_pick[0]
    w_intra = intra_weight[0]
    w_inter = inter_weight[0]
    ext = external[0]
    leak = leak_rate[0][:, None, :]

    f32, bf16 = jnp.float32, jnp.bfloat16
    activity_t = jax.ShapeDtypeStruct((blocks, conds, units), f32)
    spread_t = jax.ShapeDtypeStruct((pops, blocks, conds, units), bf16)
    recent_t = jax.ShapeDtypeStruct((DMAX, SEND_DEV, conds, units), bf16)
    chosen_t = jax.ShapeDtypeStruct((areas, SEND_DEV, conds, units), bf16)
    params = pltpu.CompilerParams(vmem_limit_bytes=24 * 2**20)

    activity, spread, now, nxt, recent = pl.pallas_call(
        first_kernel,
        out_shape=(activity_t, spread_t, chosen_t, chosen_t, recent_t),
        in_specs=[SMEM, SMEM, VMEM],
        out_specs=(VMEM,) * 5,
        scratch_shapes=[pltpu.VMEM((DMAX + 1, SEND_DEV, conds, units), bf16)],
        compiler_params=params,
    )(count, delay_to, history)

    inter = pl.pallas_call(
        inter_kernel,
        out_shape=activity_t,
        in_specs=[SMEM, SMEM, VMEM, VMEM, VMEM],
        out_specs=VMEM,
        compiler_params=params,
        cost_estimate=pl.CostEstimate(
            flops=2 * blocks * edges * conds * units * units,
            bytes_accessed=2 * blocks * edges * units * units,
            transcendentals=0,
        ),
    )

    def exchange(x, axis):
        return lax.all_to_all(x, axis, split_axis=0, concat_axis=0, tiled=True)

    received = [exchange(now, "area"), exchange(nxt, "area")]
    for step in range(STEPS):
        rates = exchange(spread, "pop").reshape(pops * blocks, conds, units)
        outer = inter(my_source, pick, received[step], w_inter, ext)
        last = step == STEPS - 1
        choosing = step + 2 < STEPS
        outs = (activity_t,) if last else (activity_t, spread_t)
        if choosing:
            outs += (recent_t, chosen_t)
        got = pl.pallas_call(
            functools.partial(intra_kernel, last, choosing),
            out_shape=outs,
            in_specs=[SMEM] * 3 + [VMEM] * (6 if choosing else 5),
            out_specs=(VMEM,) * len(outs),
            compiler_params=params,
            cost_estimate=pl.CostEstimate(
                flops=2 * blocks * tiles * conds * units * units,
                bytes_accessed=2 * blocks * tiles * units * units,
                transcendentals=blocks * conds * units,
            ),
        )(count, delay_to, index, rates, w_intra, outer, leak, activity, *((recent,) if choosing else ()))
        activity = got[0]
        if not last:
            spread = got[1]
        if choosing:
            recent = got[2]
            received.append(exchange(got[3], "area"))
    return activity[None]


def solution(mesh):
    placed = (
        P(None, "area", "pop", None, None),
        P("area", "pop", None, None),
        P("area", "pop", None),
        P("area", "pop", None),
        P("area", "pop", None, None, None),
        P("area", "pop", None),
        P("area", "pop", None, None, None),
        P(),
        P(),
        P(),
    )
    return jax.shard_map(
        shards, mesh=mesh, in_specs=placed, out_specs=P("area", "pop", None, None), check_vma=False
    )
```

time: 478 us -> 445 us (0.931)
  matrix products: 75.3 us -> 0 us
  Pallas kernels: 0 us -> 58.1 us
  blocking collectives: 260 us -> 221 us
  local copies, waits for them, and re-layouts: 42.8 us -> 73.7 us
  other arithmetic: 21.9 us -> 0.74 us
  waiting for transfers between devices: 0.03 us -> 15.6 us
    all_gather x10 -> x0, blocking collectives: 260 us -> none  [advance(): area_rates = lax.all_gather(rate_now, 'pop', axis=0, tiled=True)]
    all_to_all x0 -> x10, blocking collectives: none -> 221 us  [exchange(): return lax.all_to_all(x, axis, split_axis=0, concat_axis=0, tiled=True)]
    dot_general x20 -> x0, matrix products: 75.3 us -> none  [the longest x10 43.2 us: advance(): jnp.einsum('rkji,rktj->rti', w_inner, tile_rows, preferred_element_type=j...]
    unnamed x2 -> x118, local copies, waits for them, and re-layouts: 0.65 us -> 71.6 us
    pallas_call x0 -> x21, Pallas kernels: none -> 58.1 us  [the longest x10 32.3 us: shards(): pl.pallas_call(functools.partial(intra_kernel, last, choosing), out_shape...]
    gather x40 -> x0, local copies, waits for them, and re-layouts: 29.4 us -> none  [the longest x10 9.94 us: advance(): tile_rows = jnp.take(area_rates, tile_index, axis=0)]
    all_to_all x10, waiting for transfers between devices: 0.03 us -> 15.6 us  [exchange(): return lax.all_to_all(x, axis, split_axis=0, concat_axis=0, tiled=True)]
    mul x21 -> x0, other arithmetic: 15.4 us -> none  [the longest x10 9.32 us: turn_slots(): chosen = jnp.take(sent_hist, delay_to, axis=0) * edge_flag]
  transfers between devices with their start and end apart: 10 -> 10, of which waited for: 0 -> 1; matrix products, arithmetic and copies ran while one was open for 13% -> 0% of each run, Pallas kernels for 0% -> 12%
where the time goes in v1:
time: 445 us; the launch traced here: 441 us
  blocking collectives  221 us (50%)
  local copies, waits for them, and re-layouts  73.7 us (17%)
  starting transfers between devices  70.9 us (16%)
  Pallas kernels  58.1 us (13%)
  waiting for transfers between devices  15.6 us (4%)
    all_to_all x10, blocking collectives, exchange(): return lax.all_to_all(x, axis, split_axis=0, concat_axis=0, tiled=True)  221 us
    unnamed x118, local copies, waits for them, and re-layouts  71.6 us
    all_to_all x10, starting transfers between devices, exchange(): return lax.all_to_all(x, axis, split_axis=0, concat_axis=0, tiled=True)  70.9 us
    pallas_call x10, Pallas kernels, shards(): pl.pallas_call(functools.partial(intra_kernel, last, choosing), out_shape...  32.3 us
    pallas_call x10, Pallas kernels, shards(): outer = inter(my_source, pick, received[step], w_inter, ext)  25.2 us
    all_to_all x10, waiting for transfers between devices, exchange(): return lax.all_to_all(x, axis, split_axis=0, concat_axis=0, tiled=True)  15.6 us
  transfers between devices with their start and end apart: 10, of which 1 were waited for; matrix products, arithmetic and copies ran while one was open for 0% of the time, Pallas kernels for 12%

profile of v1, /device:TPU:4, one launch (start us, length us, event | category | flops | bytes accessed | tf_op | source)
XLA Modules:
  0.0 441.0 jit_solution(7505289021295738151)
XLA Ops:
  0.7 1.2 dynamic_slice.6
  2.6 0.9 copy-done.48
  5.7 17.4 %all_to_all.100.received_ref = bf16[32,2,32,128]{3,2,1,0:T(8,128)(2,1)} all-to-all(bf16[32,2,32,128]{3,2,1,0:T(8,128)(2,1)S(1)} %get-tuple-element.44), channel_id=1, replica_groups=mesh['area'=32,'pop'=8] {'area'}, dimensions={0} | all-to-all | bytes 1048576 | tf_op jit(solution)/shard_map/all_to_all | solution.py:154
  23.1 25.7 %all_to_all.101 = bf16[8,8,32,128]{3,2,1,0:T(8,128)(2,1)} all-to-all(bf16[8,8,32,128]{3,2,1,0:T(8,128)(2,1)S(1)} %get-tuple-element.43), channel_id=1, replica_groups=mesh['area'=32,'pop'=8] {'pop'}, dimensions={0} | all-to-all | bytes 1048576 | tf_op jit(solution)/shard_map/all_to_all | solution.py:154
  48.8 7.1 %all-to-all-start.3 = ((bf16[32,2,32,128]{3,2,1,0:T(8,128)(2,1)}), bf16[32,2,32,128]{3,2,1,0:T(8,128)(2,1)}, u32[]{:S(2)}, u32[]{:S(2)}) async-start(bf16[32,2,32,128]{3,2,1,0:T(8,128)(2,1)} %copy-done.32), calls=%async_computation.3 | async-start | bytes 1048576 | tf_op jit(solution)/shard_map/all_to_all | solution.py:154
  56.8 1.9 copy-done.10
  59.5 1.0 copy-done.23
  61.2 2.1 shard_map.101.outer_ref
  63.4 3.4 copy-done
  66.8 1.0 copy-done.14
  70.0 3.1 shard_map.102
  74.7 22.2 %all_to_all.102 = bf16[8,8,32,128]{3,2,1,0:T(8,128)(2,1)} all-to-all(bf16[8,8,32,128]{3,2,1,0:T(8,128)(2,1)} %copy-done.34), channel_id=1, replica_groups=mesh['area'=32,'pop'=8] {'pop'}, dimensions={0} | all-to-all | bytes 1048576 | tf_op jit(solution)/shard_map/all_to_all | solution.py:154
  96.9 7.5 %all-to-all-start.5 = ((bf16[32,2,32,128]{3,2,1,0:T(8,128)(2,1)}), bf16[32,2,32,128]{3,2,1,0:T(8,128)(2,1)}, u32[]{:S(2)}, u32[]{:S(2)}) async-start(bf16[32,2,32,128]{3,2,1,0:T(8,128)(2,1)} %copy-done.25), calls=%async_computation.5 | async-start | bytes 1048576 | tf_op jit(solution)/shard_map/all_to_all | solution.py:154
  104.4 2.6 shard_map.103.outer_ref
  107.1 3.4 copy-done.1
  110.4 1.0 copy-done.15
  111.5 3.1 shard_map.104
  116.8 22.2 %all_to_all.103 = bf16[8,8,32,128]{3,2,1,0:T(8,128)(2,1)} all-to-all(bf16[8,8,32,128]{3,2,1,0:T(8,128)(2,1)} %copy-done.35), channel_id=1, replica_groups=mesh['area'=32,'pop'=8] {'pop'}, dimensions={0} | all-to-all | bytes 1048576 | tf_op jit(solution)/shard_map/all_to_all | solution.py:154
  139.0 7.4 %all-to-all-start.7 = ((bf16[32,2,32,128]{3,2,1,0:T(8,128)(2,1)}), bf16[32,2,32,128]{3,2,1,0:T(8,128)(2,1)}, u32[]{:S(2)}, u32[]{:S(2)}) async-start(bf16[32,2,32,128]{3,2,1,0:T(8,128)(2,1)} %copy-done.26), calls=%async_computation.7 | async-start | bytes 1048576 | tf_op jit(solution)/shard_map/all_to_all | solution.py:154
  146.4 2.6 shard_map.105.outer_ref
  149.0 3.4 copy-done.2
  152.4 1.0 copy-done.16
  154.2 3.1 shard_map.106
  158.9 22.2 %all_to_all.104 = bf16[8,8,32,128]{3,2,1,0:T(8,128)(2,1)} all-to-all(bf16[8,8,32,128]{3,2,1,0:T(8,128)(2,1)} %copy-done.36), channel_id=1, replica_groups=mesh['area'=32,'pop'=8] {'pop'}, dimensions={0} | all-to-all | bytes 1048576 | tf_op jit(solution)/shard_map/all_to_all | solution.py:154
  181.1 7.5 %all-to-all-start.9 = ((bf16[32,2,32,128]{3,2,1,0:T(8,128)(2,1)}), bf16[32,2,32,128]{3,2,1,0:T(8,128)(2,1)}, u32[]{:S(2)}, u32[]{:S(2)}) async-start(bf16[32,2,32,128]{3,2,1,0:T(8,128)(2,1)} %copy-done.27), calls=%async_computation.9 | async-start | bytes 1048576 | tf_op jit(solution)/shard_map/all_to_all | solution.py:154
  188.6 2.6 shard_map.107.outer_ref
  191.2 3.4 copy-done.3
  194.6 1.0 copy-done.17
  195.6 3.1 shard_map.108
  200.9 22.2 %all_to_all.105 = bf16[8,8,32,128]{3,2,1,0:T(8,128)(2,1)} all-to-all(bf16[8,8,32,128]{3,2,1,0:T(8,128)(2,1)} %copy-done.37), channel_id=1, replica_groups=mesh['area'=32,'pop'=8] {'pop'}, dimensions={0} | all-to-all | bytes 1048576 | tf_op jit(solution)/shard_map/all_to_all | solution.py:154
  223.1 7.4 %all-to-all-start.11 = ((bf16[32,2,32,128]{3,2,1,0:T(8,128)(2,1)}), bf16[32,2,32,128]{3,2,1,0:T(8,128)(2,1)}, u32[]{:S(2)}, u32[]{:S(2)}) async-start(bf16[32,2,32,128]{3,2,1,0:T(8,128)(2,1)} %copy-done.28), calls=%async_computation.11 | async-start | bytes 1048576 | tf_op jit(solution)/shard_map/all_to_all | solution.py:154
  230.6 2.6 shard_map.109.outer_ref
  233.2 3.4 copy-done.4
  236.5 1.0 copy-done.18
  238.4 3.1 shard_map.110
  243.1 22.2 %all_to_all.106 = bf16[8,8,32,128]{3,2,1,0:T(8,128)(2,1)} all-to-all(bf16[8,8,32,128]{3,2,1,0:T(8,128)(2,1)} %copy-done.38), channel_id=1, replica_groups=mesh['area'=32,'pop'=8] {'pop'}, dimensions={0} | all-to-all | bytes 1048576 | tf_op jit(solution)/shard_map/all_to_all | solution.py:154
  265.3 7.4 %all-to-all-start.13 = ((bf16[32,2,32,128]{3,2,1,0:T(8,128)(2,1)}), bf16[32,2,32,128]{3,2,1,0:T(8,128)(2,1)}, u32[]{:S(2)}, u32[]{:S(2)}) async-start(bf16[32,2,32,128]{3,2,1,0:T(8,128)(2,1)} %copy-done.29), calls=%async_computation.13 | async-start | bytes 1048576 | tf_op jit(solution)/shard_map/all_to_all | solution.py:154
  272.7 2.6 shard_map.111.outer_ref
  275.3 3.4 copy-done.5
  278.7 1.0 copy-done.19
  279.7 3.1 shard_map.112
  285.0 22.2 %all_to_all.107 = bf16[8,8,32,128]{3,2,1,0:T(8,128)(2,1)} all-to-all(bf16[8,8,32,128]{3,2,1,0:T(8,128)(2,1)} %copy-done.39), channel_id=1, replica_groups=mesh['area'=32,'pop'=8] {'pop'}, dimensions={0} | all-to-all | bytes 1048576 | tf_op jit(solution)/shard_map/all_to_all | solution.py:154
  307.3 7.4 %all-to-all-start.15 = ((bf16[32,2,32,128]{3,2,1,0:T(8,128)(2,1)}), bf16[32,2,32,128]{3,2,1,0:T(8,128)(2,1)}, u32[]{:S(2)}, u32[]{:S(2)}) async-start(bf16[32,2,32,128]{3,2,1,0:T(8,128)(2,1)} %copy-done.30), calls=%async_computation.15 | async-start | bytes 1048576 | tf_op jit(solution)/shard_map/all_to_all | solution.py:154
  314.7 2.6 shard_map.113.outer_ref
  317.3 3.4 copy-done.6
  320.7 1.0 copy-done.20
  322.5 3.1 shard_map.114
  327.2 22.2 %all_to_all.108 = bf16[8,8,32,128]{3,2,1,0:T(8,128)(2,1)} all-to-all(bf16[8,8,32,128]{3,2,1,0:T(8,128)(2,1)} %copy-done.40), channel_id=1, replica_groups=mesh['area'=32,'pop'=8] {'pop'}, dimensions={0} | all-to-all | bytes 1048576 | tf_op jit(solution)/shard_map/all_to_all | solution.py:154
  349.4 7.4 %all-to-all-start.17 = ((bf16[32,2,32,128]{3,2,1,0:T(8,128)(2,1)}), bf16[32,2,32,128]{3,2,1,0:T(8,128)(2,1)}, u32[]{:S(2)}, u32[]{:S(2)}) async-start(bf16[32,2,32,128]{3,2,1,0:T(8,128)(2,1)} %copy-done.24), calls=%async_computation.17 | async-start | bytes 1048576 | tf_op jit(solution)/shard_map/all_to_all | solution.py:154
  356.9 2.6 shard_map.115.outer_ref
  359.4 3.4 copy-done.7
  362.8 1.0 copy-done.21
  363.9 3.7 shard_map.116
  369.8 22.2 %all_to_all.109 = bf16[8,8,32,128]{3,2,1,0:T(8,128)(2,1)} all-to-all(bf16[8,8,32,128]{3,2,1,0:T(8,128)(2,1)} %copy-done.41), channel_id=1, replica_groups=mesh['area'=32,'pop'=8] {'pop'}, dimensions={0} | all-to-all | bytes 1048576 | tf_op jit(solution)/shard_map/all_to_all | solution.py:154
  392.0 7.4 %all-to-all-start.19 = ((bf16[32,2,32,128]{3,2,1,0:T(8,128)(2,1)}), bf16[32,2,32,128]{3,2,1,0:T(8,128)(2,1)}, u32[]{:S(2)}, u32[]{:S(2)}) async-start(bf16[32,2,32,128]{3,2,1,0:T(8,128)(2,1)} %copy-done.31), calls=%async_computation.19 | async-start | bytes 1048576 | tf_op jit(solution)/shard_map/all_to_all | solution.py:154
  399.5 2.6 shard_map.117.outer_ref
  402.0 3.4 copy-done.8
  405.4 1.0 copy-done.22
  407.4 3.0 shard_map.118
  411.2 4.1 all-to-all-start.18
  415.3 2.6 shard_map.119.outer_ref
  417.9 15.6 %all-to-all-done.18 = bf16[8,8,32,128]{3,2,1,0:T(8,128)(2,1)} async-done(((bf16[8,8,32,128]{3,2,1,0:T(8,128)(2,1)}), bf16[8,8,32,128]{3,2,1,0:T(8,128)(2,1)}, u32[]{:S(2)}, u32[]{:S(2)}) %all-to-all-start.18) | async-done | bytes 524320 | tf_op jit(solution)/shard_map/all_to_all | solution.py:154
  433.5 3.4 copy-done.9
  436.8 4.1 shard_map.120
  (109 shorter events, 26.9 us)
Async XLA Ops:
  2.6 1.0 copy-start.48
  3.6 100.8 %copy-start.13 = (bf16[1,8,32,128]{3,2,1,0:T(8,128)(2,1)S(1)}, bf16[1,8,32,128]{3,2,1,0:T(8,128)(2,1)}, u32[]{:S(2)}) copy-start(bf16[1,8,32,128]{3,2,1,0:T(8,128)(2,1)} %param.11) | copy-start | bytes 196612
  4.3 0.8 copy-start.32
  5.7 98.7 %copy-start.11 = (bf16[1,8,12,128,128]{4,3,2,1,0:T(8,128)(2,1)S(1)}, bf16[1,8,12,128,128]{4,3,2,1,0:T(8,128)(2,1)}, u32[]{:S(2)}) copy-start(bf16[1,8,12,128,128]{4,3,2,1,0:T(8,128)(2,1)} %param.16) | copy-start | bytes 9437188
  48.8 55.6 %copy-start.43 = (s32[1,8,12]{2,1,0:T(8,128)S(1)}, s32[1,8,12]{2,1,0:T(8,128)}, u32[]{:S(2)}) copy-start(s32[1,8,12]{2,1,0:T(8,128)} %param.15) | copy-start | bytes 1156
  48.8 25.9 %all-to-all-start.3 = ((bf16[32,2,32,128]{3,2,1,0:T(8,128)(2,1)}), bf16[32,2,32,128]{3,2,1,0:T(8,128)(2,1)}, u32[]{:S(2)}, u32[]{:S(2)}) async-start(bf16[32,2,32,128]{3,2,1,0:T(8,128)(2,1)} %copy-done.32), calls=%async_computation.3 | async-start | bytes 1048576 | tf_op jit(solution)/shard_map/all_to_all | solution.py:154
  56.7 1.9 copy-start.10
  58.6 0.8 copy-start.12
  59.5 1.0 copy-start.23
  60.5 0.7 copy-start.42
  63.3 43.7 %copy-start.45 = (s32[1,8,32]{2,1,0:T(8,128)S(1)}, s32[1,8,32]{2,1,0:T(8,128)}, u32[]{:S(2)}) copy-start(s32[1,8,32]{2,1,0:T(8,128)} %param.13) | copy-start | bytes 3076
  63.4 43.7 %copy-start.47 = (f32[1,8,128]{2,1,0:T(8,128)S(1)}, f32[1,8,128]{2,1,0:T(8,128)}, u32[]{:S(2)}) copy-start(f32[1,8,128]{2,1,0:T(8,128)} %param.12) | copy-start | bytes 12292
  63.4 3.4 copy-start
  66.8 1.0 copy-start.14
  67.8 0.7 copy-start.44
  68.5 0.7 copy-start.46
  69.2 0.8 copy-start.58
  73.1 0.8 copy-start.25
  73.9 0.8 copy-start.34
  96.9 19.9 %all-to-all-start.5 = ((bf16[32,2,32,128]{3,2,1,0:T(8,128)(2,1)}), bf16[32,2,32,128]{3,2,1,0:T(8,128)(2,1)}, u32[]{:S(2)}, u32[]{:S(2)}) async-start(bf16[32,2,32,128]{3,2,1,0:T(8,128)(2,1)} %copy-done.25), calls=%async_computation.5 | async-start | bytes 1048576 | tf_op jit(solution)/shard_map/all_to_all | solution.py:154
  107.0 3.4 copy-start.1
  110.4 1.0 copy-start.15
  114.5 0.8 copy-start.26
  115.4 0.8 copy-start.35
  139.0 19.9 %all-to-all-start.7 = ((bf16[32,2,32,128]{3,2,1,0:T(8,128)(2,1)}), bf16[32,2,32,128]{3,2,1,0:T(8,128)(2,1)}, u32[]{:S(2)}, u32[]{:S(2)}) async-start(bf16[32,2,32,128]{3,2,1,0:T(8,128)(2,1)} %copy-done.26), calls=%async_computation.7 | async-start | bytes 1048576 | tf_op jit(solution)/shard_map/all_to_all | solution.py:154
  149.0 3.4 copy-start.2
  152.4 1.0 copy-start.16
  153.4 0.8 copy-start.52
  157.3 0.8 copy-start.27
  158.1 0.8 copy-start.36
  181.1 19.8 %all-to-all-start.9 = ((bf16[32,2,32,128]{3,2,1,0:T(8,128)(2,1)}), bf16[32,2,32,128]{3,2,1,0:T(8,128)(2,1)}, u32[]{:S(2)}, u32[]{:S(2)}) async-start(bf16[32,2,32,128]{3,2,1,0:T(8,128)(2,1)} %copy-done.27), calls=%async_computation.9 | async-start | bytes 1048576 | tf_op jit(solution)/shard_map/all_to_all | solution.py:154
  191.2 3.4 copy-start.3
  194.6 1.0 copy-start.17
  198.7 0.8 copy-start.28
  199.5 0.8 copy-start.37
  223.1 19.9 %all-to-all-start.11 = ((bf16[32,2,32,128]{3,2,1,0:T(8,128)(2,1)}), bf16[32,2,32,128]{3,2,1,0:T(8,128)(2,1)}, u32[]{:S(2)}, u32[]{:S(2)}) async-start(bf16[32,2,32,128]{3,2,1,0:T(8,128)(2,1)} %copy-done.28), calls=%async_computation.11 | async-start | bytes 1048576 | tf_op jit(solution)/shard_map/all_to_all | solution.py:154
  233.2 3.4 copy-start.4
  236.5 1.0 copy-start.18
  237.6 0.8 copy-start.54
  241.5 0.8 copy-start.29
  242.3 0.8 copy-start.38
  265.3 19.8 %all-to-all-start.13 = ((bf16[32,2,32,128]{3,2,1,0:T(8,128)(2,1)}), bf16[32,2,32,128]{3,2,1,0:T(8,128)(2,1)}, u32[]{:S(2)}, u32[]{:S(2)}) async-start(bf16[32,2,32,128]{3,2,1,0:T(8,128)(2,1)} %copy-done.29), calls=%async_computation.13 | async-start | bytes 1048576 | tf_op jit(solution)/shard_map/all_to_all | solution.py:154
  275.3 3.4 copy-start.5
  278.7 1.0 copy-start.19
  282.8 0.8 copy-start.30
  283.6 0.8 copy-start.39
  307.3 19.9 %all-to-all-start.15 = ((bf16[32,2,32,128]{3,2,1,0:T(8,128)(2,1)}), bf16[32,2,32,128]{3,2,1,0:T(8,128)(2,1)}, u32[]{:S(2)}, u32[]{:S(2)}) async-start(bf16[32,2,32,128]{3,2,1,0:T(8,128)(2,1)} %copy-done.30), calls=%async_computation.15 | async-start | bytes 1048576 | tf_op jit(solution)/shard_map/all_to_all | solution.py:154
  317.3 3.4 copy-start.6
  320.7 1.0 copy-start.20
  321.7 0.8 copy-start.56
  325.6 0.8 copy-start.24
  326.4 0.8 copy-start.40
  349.4 20.4 %all-to-all-start.17 = ((bf16[32,2,32,128]{3,2,1,0:T(8,128)(2,1)}), bf16[32,2,32,128]{3,2,1,0:T(8,128)(2,1)}, u32[]{:S(2)}, u32[]{:S(2)}) async-start(bf16[32,2,32,128]{3,2,1,0:T(8,128)(2,1)} %copy-done.24), calls=%async_computation.17 | async-start | bytes 1048576 | tf_op jit(solution)/shard_map/all_to_all | solution.py:154
  359.4 3.4 copy-start.7
  362.8 1.0 copy-start.21
  367.6 0.8 copy-start.31
  368.3 0.8 copy-start.41
  392.0 19.2 %all-to-all-start.19 = ((bf16[32,2,32,128]{3,2,1,0:T(8,128)(2,1)}), bf16[32,2,32,128]{3,2,1,0:T(8,128)(2,1)}, u32[]{:S(2)}, u32[]{:S(2)}) async-start(bf16[32,2,32,128]{3,2,1,0:T(8,128)(2,1)} %copy-done.31), calls=%async_computation.19 | async-start | bytes 1048576 | tf_op jit(solution)/shard_map/all_to_all | solution.py:154
  402.0 3.4 copy-start.8
  405.4 1.0 copy-start.22
  406.5 0.9 copy-start.50
  410.4 0.8 copy-start.33
  411.2 22.3 %all-to-all-start.18 = ((bf16[8,8,32,128]{3,2,1,0:T(8,128)(2,1)}), bf16[8,8,32,128]{3,2,1,0:T(8,128)(2,1)}, u32[]{:S(2)}, u32[]{:S(2)}) async-start(bf16[8,8,32,128]{3,2,1,0:T(8,128)(2,1)} %copy-done.33), calls=%async_computation.18 | async-start | bytes 1048576 | tf_op jit(solution)/shard_map/all_to_all | solution.py:154
  433.5 3.4 copy-start.9
  (5 other events, 3.1 us)

commit v2 on v1

v2 whole, which is shorter than its diff:
```python
import functools
import jax
import jax.numpy as jnp
from jax import lax
from jax.experimental import pallas as pl
from jax.experimental.pallas import tpu as pltpu
from jax.sharding import PartitionSpec as P

SEND_DEV = 2
STEPS = 10
DMAX = 3
SPAN = 2

VMEM = pl.BlockSpec(memory_space=pltpu.VMEM)
SMEM = pl.BlockSpec(memory_space=pltpu.SMEM)


def tile_product(rows, weights):
    lhs = jnp.concatenate(rows, axis=1)
    rhs = weights.reshape(lhs.shape[1], weights.shape[-1])
    return lax.dot_general(
        lhs, rhs, (((1,), (0,)), ((), ())), preferred_element_type=jnp.float32
    )


def choose(delay_ref, older_ref, chosen_ref):
    for area in range(chosen_ref.shape[0]):
        delay = delay_ref[area]
        chosen_ref[area, :SEND_DEV] = older_ref[delay]
        chosen_ref[area, SEND_DEV:] = older_ref[delay - 1]


def first_kernel(count_ref, delay_ref, history_ref, activity_ref, spread_ref, chosen_ref, recent_ref, older_ref):
    blocks = activity_ref.shape[0]
    count = count_ref[0]
    for block in range(blocks):
        alive = jnp.where(block < count, 1.0, 0.0)
        rates = (history_ref[0, block].astype(jnp.float32) * alive).astype(jnp.bfloat16)
        activity_ref[block] = rates.astype(jnp.float32)
        for pop in range(spread_ref.shape[0]):
            spread_ref[pop, block] = rates
    for block in range(SEND_DEV):
        alive = jnp.where(block < count, 1.0, 0.0)
        for age in range(DMAX + 1):
            rates = (history_ref[age, block].astype(jnp.float32) * alive).astype(jnp.bfloat16)
            older_ref[age, block] = rates
            if age < DMAX:
                recent_ref[age, block] = rates
    choose(delay_ref, older_ref, chosen_ref)


def step_kernel(
    phase, last, choosing,
    count_ref, delay_ref, source_ref, pick_ref, index_ref,
    rates_ref, received_ref, intra_ref, inter_ref, external_ref, leak_ref, activity_ref, recent_ref,
    *refs,
):
    if last:
        (activity_out_ref,) = refs
    elif choosing:
        activity_out_ref, spread_ref, recent_out_ref, chosen_ref, older_ref = refs
    else:
        activity_out_ref, spread_ref, recent_out_ref = refs
    blocks, tiles = intra_ref.shape[:2]
    edges = inter_ref.shape[1]
    count = count_ref[0]

    def body(block, carry):
        rows = [received_ref[source_ref[e], SEND_DEV * phase + pick_ref[block, e]] for e in range(edges)]
        current = tile_product(rows, inter_ref[block])
        rows = [rates_ref[index_ref[block, k]] for k in range(tiles)]
        current += tile_product(rows, intra_ref[block])
        leak = leak_ref[block]
        alive = jnp.where(block < count, 1.0, 0.0)
        driven = jnp.tanh(current + external_ref[block].astype(jnp.float32))
        new = alive * ((1.0 - leak) * activity_ref[block] + leak * driven)
        activity_out_ref[block] = new
        if not last:
            rates = new.astype(jnp.bfloat16)
            for pop in range(spread_ref.shape[0]):
                spread_ref[pop, block] = rates
        return carry

    lax.fori_loop(0, blocks, body, 0)
    if not last:
        recent_out_ref[0] = spread_ref[0, :SEND_DEV]
        for age in range(1, DMAX):
            recent_out_ref[age] = recent_ref[age - 1]
    if choosing:
        older_ref[0] = spread_ref[0, :SEND_DEV]
        for age in range(DMAX):
            older_ref[age + 1] = recent_ref[age]
        choose(delay_ref, older_ref, chosen_ref)


def shards(
    history,
    external,
    leak_rate,
    intra_index,
    intra_weight,
    inter_pick,
    inter_weight,
    source_area,
    delays,
    live_blocks,
):
    area_pos = lax.axis_index("area")
    pop_pos = lax.axis_index("pop")
    areas = lax.axis_size("area")
    pops = lax.axis_size("pop")
    history = history[:, 0]
    blocks, conds, units = history.shape[1:]
    tiles = intra_index.shape[2]
    edges = inter_pick.shape[2]
    count = (live_blocks[area_pos] - pop_pos * blocks)[None]
    delay_to = jnp.sum(jnp.where(source_area == area_pos, delays, 0), axis=1)
    delay_to = jnp.maximum(delay_to, 1)
    my_source = source_area[area_pos]
    leak = leak_rate[0][:, None, :]

    f32, bf16 = jnp.float32, jnp.bfloat16
    activity_t = jax.ShapeDtypeStruct((blocks, conds, units), f32)
    spread_t = jax.ShapeDtypeStruct((pops, blocks, conds, units), bf16)
    recent_t = jax.ShapeDtypeStruct((DMAX, SEND_DEV, conds, units), bf16)
    chosen_t = jax.ShapeDtypeStruct((areas, SPAN * SEND_DEV, conds, units), bf16)
    older = pltpu.VMEM((DMAX + 1, SEND_DEV, conds, units), bf16)
    params = pltpu.CompilerParams(vmem_limit_bytes=4 * 2**20)

    activity, spread, chosen, recent = pl.pallas_call(
        first_kernel,
        out_shape=(activity_t, spread_t, chosen_t, recent_t),
        in_specs=[SMEM, SMEM, VMEM],
        out_specs=(VMEM,) * 4,
        scratch_shapes=[older],
        compiler_params=params,
    )(count, delay_to, history)

    def exchange(x, axis):
        return lax.all_to_all(x, axis, split_axis=0, concat_axis=0, tiled=True)

    products = blocks * (tiles + edges) * units * units
    for step in range(STEPS):
        phase = step % SPAN
        if phase == 0:
            received = exchange(chosen, "area")
        rates = exchange(spread, "pop").reshape(pops * blocks, conds, units)
        last = step == STEPS - 1
        choosing = phase == SPAN - 1 and not last
        outs = (activity_t,) if last else (activity_t, spread_t, recent_t)
        if choosing:
            outs += (chosen_t,)
        got = pl.pallas_call(
            functools.partial(step_kernel, phase, last, choosing),
            out_shape=outs,
            in_specs=[SMEM] * 5 + [VMEM] * 8,
            out_specs=(VMEM,) * len(outs),
            scratch_shapes=[older] if choosing else [],
            compiler_params=params,
            cost_estimate=pl.CostEstimate(
                flops=2 * products * conds,
                bytes_accessed=2 * products,
                transcendentals=blocks * conds * units,
            ),
        )(
            count, delay_to, my_source, inter_pick[0], intra_index[0],
            rates, received, intra_weight[0], inter_weight[0], external[0], leak, activity, recent,
        )
        activity = got[0]
        if not last:
            spread, recent = got[1:3]
        if choosing:
            chosen = got[3]
    return activity[None]


def solution(mesh):
    placed = (
        P(None, "area", "pop", None, None),
        P("area", "pop", None, None),
        P("area", "pop", None),
        P("area", "pop", None),
        P("area", "pop", None, None, None),
        P("area", "pop", None),
        P("area", "pop", None, None, None),
        P(),
        P(),
        P(),
    )
    return jax.shard_map(
        shards, mesh=mesh, in_specs=placed, out_specs=P("area", "pop", None, None), check_vma=False
    )
```

time: 445 us -> 374 us (0.84)
  blocking collectives: 221 us -> 294 us
  starting transfers between devices: 70.9 us -> 7.79 us
  local copies, waits for them, and re-layouts: 73.7 us -> 12.3 us
  Pallas kernels: 58.1 us -> 40.7 us
    all_to_all x10 -> x14, blocking collectives: 221 us -> 294 us  [exchange(): return lax.all_to_all(x, axis, split_axis=0, concat_axis=0, tiled=True)]
    all_to_all x10 -> x1, starting transfers between devices: 70.9 us -> 7.79 us  [exchange(): return lax.all_to_all(x, axis, split_axis=0, concat_axis=0, tiled=True)]
    unnamed x118 -> x30, local copies, waits for them, and re-layouts: 71.6 us -> 10.2 us
    pallas_call x21 -> x11, Pallas kernels: 58.1 us -> 40.7 us  [the longest x10 40.1 us: shards(): pl.pallas_call(functools.partial(step_kernel, phase, last, choosing), out...]
    all_to_all x10 -> x1, waiting for transfers between devices: 15.6 us -> 14.5 us  [exchange(): return lax.all_to_all(x, axis, split_axis=0, concat_axis=0, tiled=True)]
  transfers between devices with their start and end apart: 10 -> 1, of which waited for: 1 -> 1; matrix products, arithmetic and copies ran while one was open for 0% -> 0% of each run, Pallas kernels for 12% -> 0%
where the time goes in v2:
time: 374 us; the launch traced here: 371 us
  blocking collectives  294 us (79%)
  Pallas kernels  40.7 us (11%)
  waiting for transfers between devices  14.5 us (4%)
  local copies, waits for them, and re-layouts  12.3 us (3%)
  starting transfers between devices  7.79 us (2%)
    all_to_all x14, blocking collectives, exchange(): return lax.all_to_all(x, axis, split_axis=0, concat_axis=0, tiled=True)  294 us
    pallas_call x10, Pallas kernels, shards(): pl.pallas_call(functools.partial(step_kernel, phase, last, choosing), out...  40.1 us
    all_to_all x1, waiting for transfers between devices, exchange(): return lax.all_to_all(x, axis, split_axis=0, concat_axis=0, tiled=True)  14.5 us
    unnamed x30, local copies, waits for them, and re-layouts  10.2 us
    all_to_all x1, starting transfers between devices, exchange(): return lax.all_to_all(x, axis, split_axis=0, concat_axis=0, tiled=True)  7.79 us
  transfers between devices with their start and end apart: 1, of which 1 were waited for; matrix products, arithmetic and copies ran while one was open for 0% of the time, Pallas kernels for 0%

profile of v2, /device:TPU:4, one launch (start us, length us, event | category | flops | bytes accessed | tf_op | source)
XLA Modules:
  0.0 370.5 jit_solution(17185197685911018048)
XLA Ops:
  0.0 0.7 select_reduce_fusion
  0.7 1.2 dynamic_slice.6
  2.6 0.0 copy-start.14
  2.6 0.9 copy-done.14
  3.6 0.0 copy-start.5
  3.6 0.7 shard_map.100
  4.3 0.0 copy-start.7
  4.3 0.0 copy-start.3
  4.3 26.1 %all_to_all.75 = bf16[8,8,32,128]{3,2,1,0:T(8,128)(2,1)} all-to-all(bf16[8,8,32,128]{3,2,1,0:T(8,128)(2,1)S(1)} %get-tuple-element.40), channel_id=1, replica_groups=mesh['area'=32,'pop'=8] {'pop'}, dimensions={0} | all-to-all | bytes 1048576 | tf_op jit(solution)/shard_map/all_to_all | solution.py:140
  30.4 0.0 copy-done.7
  30.4 0.0 copy-start.9
  30.4 0.0 copy-start.11
  30.4 0.0 copy-start.13
  30.4 7.8 %all-to-all-start.1 = ((bf16[32,4,32,128]{3,2,1,0:T(8,128)(2,1)}), bf16[32,4,32,128]{3,2,1,0:T(8,128)(2,1)}, u32[]{:S(2)}, u32[]{:S(2)}) async-start(bf16[32,4,32,128]{3,2,1,0:T(8,128)(2,1)} %copy-done.7), calls=%async_computation.1 | async-start | bytes 2097152 | tf_op jit(solution)/shard_map/all_to_all | solution.py:140
  38.2 0.9 dynamic-slice_reduce_fusion.source_ref
  39.1 14.5 %all-to-all-done.1.received_ref = bf16[32,4,32,128]{3,2,1,0:T(8,128)(2,1)} async-done(((bf16[32,4,32,128]{3,2,1,0:T(8,128)(2,1)}), bf16[32,4,32,128]{3,2,1,0:T(8,128)(2,1)}, u32[]{:S(2)}, u32[]{:S(2)}) %all-to-all-start.1) | async-done | bytes 1048608 | tf_op jit(solution)/shard_map/all_to_all | solution.py:140
  53.6 0.0 copy-start
  53.6 3.4 copy-done
  57.0 0.0 copy-start.2
  57.0 1.9 copy-done.2
  58.8 0.0 copy-start.4
  58.8 0.8 copy-done.4
  59.7 0.0 copy-start.6
  59.7 1.0 copy-done.6
  60.7 0.0 copy-start.8
  60.7 0.7 copy-done.8
  61.4 0.0 copy-start.10
  61.4 0.7 copy-done.10
  62.1 0.0 copy-start.12
  62.1 0.7 copy-done.12
  62.8 0.0 copy-start.1
  62.8 4.5 %shard_map.101 = (f32[8,32,128]{2,1,0:T(8,128)S(1)}, bf16[8,8,32,128]{3,2,1,0:T(8,128)(2,1)S(1)}, bf16[3,2,32,128]{3,2,1,0:T(8,128)(2,1)S(1)}) custom-call(s32[1]{0:T(128)} %bitcast.1.count_ref, s32[32]{0:T(128)S(1)} %broadcast_maximum_fusion.delay_ref, s32[12]{0:T(128)S(1)} %dynamic-slice_reduce_fusion.source_ref, s32[8,12]{1,0:T(8,128)S(1)} %bitcast.60, ...), custom_call_target="tpu_custom_call" | custom-call | flops 369098752 | bytes 11534336 | tf_op jit(solution)/shard_map/pallas_call | solution.py:153
  67.3 20.4 %all_to_all.76 = bf16[8,8,32,128]{3,2,1,0:T(8,128)(2,1)S(1)} all-to-all(bf16[8,8,32,128]{3,2,1,0:T(8,128)(2,1)S(1)} %get-tuple-element.44), channel_id=1, replica_groups=mesh['area'=32,'pop'=8] {'pop'}, dimensions={0} | all-to-all | bytes 1048576 | tf_op jit(solution)/shard_map/all_to_all | solution.py:140
  87.7 0.0 copy-done.5
  87.7 0.0 copy-done.3
  87.7 0.0 copy-done.9
  87.7 0.0 copy-done.11
  87.7 0.0 copy-done.13
  87.7 0.0 copy-done.1
  87.8 4.4 %shard_map.102 = (f32[8,32,128]{2,1,0:T(8,128)S(1)}, bf16[8,8,32,128]{3,2,1,0:T(8,128)(2,1)S(1)}, bf16[3,2,32,128]{3,2,1,0:T(8,128)(2,1)S(1)}, bf16[32,4,32,128]{3,2,1,0:T(8,128)(2,1)S(1)}) custom-call(s32[1]{0:T(128)} %bitcast.1.count_ref, s32[32]{0:T(128)S(1)} %broadcast_maximum_fusion.delay_ref, s32[12]{0:T(128)S(1)} %dynamic-slice_reduce_fusion.source_ref, ...), custom_call_target="tpu_custom_call" | custom-call | flops 369098752 | bytes 11534336 | tf_op jit(solution)/shard_map/pallas_call | solution.py:153
  92.2 20.3 %all_to_all.77 = bf16[8,8,32,128]{3,2,1,0:T(8,128)(2,1)S(1)} all-to-all(bf16[8,8,32,128]{3,2,1,0:T(8,128)(2,1)S(1)} %get-tuple-element.47), channel_id=1, replica_groups=mesh['area'=32,'pop'=8] {'pop'}, dimensions={0} | all-to-all | bytes 1048576 | tf_op jit(solution)/shard_map/all_to_all | solution.py:140
  112.5 21.1 %all_to_all.78.received_ref = bf16[32,4,32,128]{3,2,1,0:T(8,128)(2,1)S(1)} all-to-all(bf16[32,4,32,128]{3,2,1,0:T(8,128)(2,1)S(1)} %get-tuple-element.48), channel_id=1, replica_groups=mesh['area'=32,'pop'=8] {'area'}, dimensions={0} | all-to-all | bytes 2097152 | tf_op jit(solution)/shard_map/all_to_all | solution.py:140
  133.6 3.8 %shard_map.103 = (f32[8,32,128]{2,1,0:T(8,128)S(1)}, bf16[8,8,32,128]{3,2,1,0:T(8,128)(2,1)S(1)}, bf16[3,2,32,128]{3,2,1,0:T(8,128)(2,1)S(1)}) custom-call(s32[1]{0:T(128)} %bitcast.1.count_ref, s32[32]{0:T(128)S(1)} %broadcast_maximum_fusion.delay_ref, s32[12]{0:T(128)S(1)} %dynamic-slice_reduce_fusion.source_ref, s32[8,12]{1,0:T(8,128)S(1)} %bitcast.62, ...), custom_call_target="tpu_custom_call" | custom-call | flops 369098752 | bytes 11534336 | tf_op jit(solution)/shard_map/pallas_call | solution.py:153
  137.3 20.5 %all_to_all.79 = bf16[8,8,32,128]{3,2,1,0:T(8,128)(2,1)S(1)} all-to-all(bf16[8,8,32,128]{3,2,1,0:T(8,128)(2,1)S(1)} %get-tuple-element.51), channel_id=1, replica_groups=mesh['area'=32,'pop'=8] {'pop'}, dimensions={0} | all-to-all | bytes 1048576 | tf_op jit(solution)/shard_map/all_to_all | solution.py:140
  157.8 3.9 %shard_map.104 = (f32[8,32,128]{2,1,0:T(8,128)S(1)}, bf16[8,8,32,128]{3,2,1,0:T(8,128)(2,1)S(1)}, bf16[3,2,32,128]{3,2,1,0:T(8,128)(2,1)S(1)}, bf16[32,4,32,128]{3,2,1,0:T(8,128)(2,1)S(1)}) custom-call(s32[1]{0:T(128)} %bitcast.1.count_ref, s32[32]{0:T(128)S(1)} %broadcast_maximum_fusion.delay_ref, s32[12]{0:T(128)S(1)} %dynamic-slice_reduce_fusion.source_ref, ...), custom_call_target="tpu_custom_call" | custom-call | flops 369098752 | bytes 11534336 | tf_op jit(solution)/shard_map/pallas_call | solution.py:153
  161.7 20.4 %all_to_all.80 = bf16[8,8,32,128]{3,2,1,0:T(8,128)(2,1)S(1)} all-to-all(bf16[8,8,32,128]{3,2,1,0:T(8,128)(2,1)S(1)} %get-tuple-element.54), channel_id=1, replica_groups=mesh['area'=32,'pop'=8] {'pop'}, dimensions={0} | all-to-all | bytes 1048576 | tf_op jit(solution)/shard_map/all_to_all | solution.py:140
  182.0 21.0 %all_to_all.81.received_ref = bf16[32,4,32,128]{3,2,1,0:T(8,128)(2,1)S(1)} all-to-all(bf16[32,4,32,128]{3,2,1,0:T(8,128)(2,1)S(1)} %get-tuple-element.55), channel_id=1, replica_groups=mesh['area'=32,'pop'=8] {'area'}, dimensions={0} | all-to-all | bytes 2097152 | tf_op jit(solution)/shard_map/all_to_all | solution.py:140
  203.0 3.8 %shard_map.105 = (f32[8,32,128]{2,1,0:T(8,128)S(1)}, bf16[8,8,32,128]{3,2,1,0:T(8,128)(2,1)S(1)}, bf16[3,2,32,128]{3,2,1,0:T(8,128)(2,1)S(1)}) custom-call(s32[1]{0:T(128)} %bitcast.1.count_ref, s32[32]{0:T(128)S(1)} %broadcast_maximum_fusion.delay_ref, s32[12]{0:T(128)S(1)} %dynamic-slice_reduce_fusion.source_ref, s32[8,12]{1,0:T(8,128)S(1)} %bitcast.64, ...), custom_call_target="tpu_custom_call" | custom-call | flops 369098752 | bytes 11534336 | tf_op jit(solution)/shard_map/pallas_call | solution.py:153
  206.8 20.5 %all_to_all.82 = bf16[8,8,32,128]{3,2,1,0:T(8,128)(2,1)S(1)} all-to-all(bf16[8,8,32,128]{3,2,1,0:T(8,128)(2,1)S(1)} %get-tuple-element.58), channel_id=1, replica_groups=mesh['area'=32,'pop'=8] {'pop'}, dimensions={0} | all-to-all | bytes 1048576 | tf_op jit(solution)/shard_map/all_to_all | solution.py:140
  227.2 3.9 %shard_map.106 = (f32[8,32,128]{2,1,0:T(8,128)S(1)}, bf16[8,8,32,128]{3,2,1,0:T(8,128)(2,1)S(1)}, bf16[3,2,32,128]{3,2,1,0:T(8,128)(2,1)S(1)}, bf16[32,4,32,128]{3,2,1,0:T(8,128)(2,1)S(1)}) custom-call(s32[1]{0:T(128)} %bitcast.1.count_ref, s32[32]{0:T(128)S(1)} %broadcast_maximum_fusion.delay_ref, s32[12]{0:T(128)S(1)} %dynamic-slice_reduce_fusion.source_ref, ...), custom_call_target="tpu_custom_call" | custom-call | flops 369098752 | bytes 11534336 | tf_op jit(solution)/shard_map/pallas_call | solution.py:153
  231.1 20.4 %all_to_all.83 = bf16[8,8,32,128]{3,2,1,0:T(8,128)(2,1)S(1)} all-to-all(bf16[8,8,32,128]{3,2,1,0:T(8,128)(2,1)S(1)} %get-tuple-element.61), channel_id=1, replica_groups=mesh['area'=32,'pop'=8] {'pop'}, dimensions={0} | all-to-all | bytes 1048576 | tf_op jit(solution)/shard_map/all_to_all | solution.py:140
  251.5 21.0 %all_to_all.84.received_ref = bf16[32,4,32,128]{3,2,1,0:T(8,128)(2,1)S(1)} all-to-all(bf16[32,4,32,128]{3,2,1,0:T(8,128)(2,1)S(1)} %get-tuple-element.62), channel_id=1, replica_groups=mesh['area'=32,'pop'=8] {'area'}, dimensions={0} | all-to-all | bytes 2097152 | tf_op jit(solution)/shard_map/all_to_all | solution.py:140
  272.4 3.8 %shard_map.107 = (f32[8,32,128]{2,1,0:T(8,128)S(1)}, bf16[8,8,32,128]{3,2,1,0:T(8,128)(2,1)S(1)}, bf16[3,2,32,128]{3,2,1,0:T(8,128)(2,1)S(1)}) custom-call(s32[1]{0:T(128)} %bitcast.1.count_ref, s32[32]{0:T(128)S(1)} %broadcast_maximum_fusion.delay_ref, s32[12]{0:T(128)S(1)} %dynamic-slice_reduce_fusion.source_ref, s32[8,12]{1,0:T(8,128)S(1)} %bitcast.66, ...), custom_call_target="tpu_custom_call" | custom-call | flops 369098752 | bytes 11534336 | tf_op jit(solution)/shard_map/pallas_call | solution.py:153
  276.2 20.5 %all_to_all.85 = bf16[8,8,32,128]{3,2,1,0:T(8,128)(2,1)S(1)} all-to-all(bf16[8,8,32,128]{3,2,1,0:T(8,128)(2,1)S(1)} %get-tuple-element.65), channel_id=1, replica_groups=mesh['area'=32,'pop'=8] {'pop'}, dimensions={0} | all-to-all | bytes 1048576 | tf_op jit(solution)/shard_map/all_to_all | solution.py:140
  296.7 3.9 %shard_map.108 = (f32[8,32,128]{2,1,0:T(8,128)S(1)}, bf16[8,8,32,128]{3,2,1,0:T(8,128)(2,1)S(1)}, bf16[3,2,32,128]{3,2,1,0:T(8,128)(2,1)S(1)}, bf16[32,4,32,128]{3,2,1,0:T(8,128)(2,1)S(1)}) custom-call(s32[1]{0:T(128)} %bitcast.1.count_ref, s32[32]{0:T(128)S(1)} %broadcast_maximum_fusion.delay_ref, s32[12]{0:T(128)S(1)} %dynamic-slice_reduce_fusion.source_ref, ...), custom_call_target="tpu_custom_call" | custom-call | flops 369098752 | bytes 11534336 | tf_op jit(solution)/shard_map/pallas_call | solution.py:153
  300.5 20.4 %all_to_all.86 = bf16[8,8,32,128]{3,2,1,0:T(8,128)(2,1)S(1)} all-to-all(bf16[8,8,32,128]{3,2,1,0:T(8,128)(2,1)S(1)} %get-tuple-element.68), channel_id=1, replica_groups=mesh['area'=32,'pop'=8] {'pop'}, dimensions={0} | all-to-all | bytes 1048576 | tf_op jit(solution)/shard_map/all_to_all | solution.py:140
  320.9 21.0 %all_to_all.87.received_ref = bf16[32,4,32,128]{3,2,1,0:T(8,128)(2,1)S(1)} all-to-all(bf16[32,4,32,128]{3,2,1,0:T(8,128)(2,1)S(1)} %get-tuple-element.69), channel_id=1, replica_groups=mesh['area'=32,'pop'=8] {'area'}, dimensions={0} | all-to-all | bytes 2097152 | tf_op jit(solution)/shard_map/all_to_all | solution.py:140
  341.9 3.8 %shard_map.109 = (f32[8,32,128]{2,1,0:T(8,128)S(1)}, bf16[8,8,32,128]{3,2,1,0:T(8,128)(2,1)S(1)}, bf16[3,2,32,128]{3,2,1,0:T(8,128)(2,1)S(1)}) custom-call(s32[1]{0:T(128)} %bitcast.1.count_ref, s32[32]{0:T(128)S(1)} %broadcast_maximum_fusion.delay_ref, s32[12]{0:T(128)S(1)} %dynamic-slice_reduce_fusion.source_ref, s32[8,12]{1,0:T(8,128)S(1)} %bitcast.68, ...), custom_call_target="tpu_custom_call" | custom-call | flops 369098752 | bytes 11534336 | tf_op jit(solution)/shard_map/pallas_call | solution.py:153
  345.7 20.4 %all_to_all.88 = bf16[8,8,32,128]{3,2,1,0:T(8,128)(2,1)S(1)} all-to-all(bf16[8,8,32,128]{3,2,1,0:T(8,128)(2,1)S(1)} %get-tuple-element.72), channel_id=1, replica_groups=mesh['area'=32,'pop'=8] {'pop'}, dimensions={0} | all-to-all | bytes 1048576 | tf_op jit(solution)/shard_map/all_to_all | solution.py:140
  366.1 4.4 %shard_map.110 = f32[8,32,128]{2,1,0:T(8,128)} custom-call(s32[1]{0:T(128)} %bitcast.1.count_ref, s32[32]{0:T(128)S(1)} %broadcast_maximum_fusion.delay_ref, s32[12]{0:T(128)S(1)} %dynamic-slice_reduce_fusion.source_ref, s32[8,12]{1,0:T(8,128)S(1)} %bitcast.69, s32[8,32]{1,0:T(8,128)S(1)} %bitcast.79, bf16[64,32,128]{2,1,0:T(8,128)(2,1)S(1)} %bitcast.59, ...), custom_call_target="tpu_custom_call" | custom-call | flops 369098752 | bytes 11534336 | tf_op jit(solution)/shard_map/pallas_call | solution.py:153
  (1 shorter events, 0.0 us)
Async XLA Ops:
  2.6 1.0 copy-start.14
  3.6 84.1 %copy-start.5 = (bf16[1,8,32,128]{3,2,1,0:T(8,128)(2,1)S(1)}, bf16[1,8,32,128]{3,2,1,0:T(8,128)(2,1)}, u32[]{:S(2)}) copy-start(bf16[1,8,32,128]{3,2,1,0:T(8,128)(2,1)} %param.11) | copy-start | bytes 196612
  4.3 26.2 %copy-start.7 = (bf16[32,4,32,128]{3,2,1,0:T(8,128)(2,1)}, bf16[32,4,32,128]{3,2,1,0:T(8,128)(2,1)S(1)}, u32[]{:S(2)}) copy-start(bf16[32,4,32,128]{3,2,1,0:T(8,128)(2,1)S(1)} %get-tuple-element.41) | copy-start | bytes 3145732
  4.3 83.5 %copy-start.3 = (bf16[1,8,12,128,128]{4,3,2,1,0:T(8,128)(2,1)S(1)}, bf16[1,8,12,128,128]{4,3,2,1,0:T(8,128)(2,1)}, u32[]{:S(2)}) copy-start(bf16[1,8,12,128,128]{4,3,2,1,0:T(8,128)(2,1)} %param.16) | copy-start | bytes 9437188
  30.4 57.3 %copy-start.9 = (s32[1,8,12]{2,1,0:T(8,128)S(1)}, s32[1,8,12]{2,1,0:T(8,128)}, u32[]{:S(2)}) copy-start(s32[1,8,12]{2,1,0:T(8,128)} %param.15) | copy-start | bytes 1156
  30.4 57.3 %copy-start.11 = (s32[1,8,32]{2,1,0:T(8,128)S(1)}, s32[1,8,32]{2,1,0:T(8,128)}, u32[]{:S(2)}) copy-start(s32[1,8,32]{2,1,0:T(8,128)} %param.13) | copy-start | bytes 3076
  30.4 57.3 %copy-start.13 = (f32[1,8,128]{2,1,0:T(8,128)S(1)}, f32[1,8,128]{2,1,0:T(8,128)}, u32[]{:S(2)}) copy-start(f32[1,8,128]{2,1,0:T(8,128)} %param.12) | copy-start | bytes 12292
  30.4 23.1 %all-to-all-start.1 = ((bf16[32,4,32,128]{3,2,1,0:T(8,128)(2,1)}), bf16[32,4,32,128]{3,2,1,0:T(8,128)(2,1)}, u32[]{:S(2)}, u32[]{:S(2)}) async-start(bf16[32,4,32,128]{3,2,1,0:T(8,128)(2,1)} %copy-done.7), calls=%async_computation.1 | async-start | bytes 2097152 | tf_op jit(solution)/shard_map/all_to_all | solution.py:140
  53.6 3.4 copy-start
  57.0 1.9 copy-start.2
  58.8 0.8 copy-start.4
  59.7 1.0 copy-start.6
  60.7 0.7 copy-start.8
  61.4 0.7 copy-start.10
  62.1 0.7 copy-start.12
  62.8 25.0 %copy-start.1 = (bf16[1,8,32,128,128]{4,3,2,1,0:T(8,128)(2,1)S(1)}, bf16[1,8,32,128,128]{4,3,2,1,0:T(8,128)(2,1)}, u32[]{:S(2)}) copy-start(bf16[1,8,32,128,128]{4,3,2,1,0:T(8,128)(2,1)} %param.14) | copy-start | bytes 25165828

commit v3 on v2

--- a/solution.py
+++ b/solution.py
@@ -13,6 +13,8 @@
 
 VMEM = pl.BlockSpec(memory_space=pltpu.VMEM)
 SMEM = pl.BlockSpec(memory_space=pltpu.SMEM)
+ANY = pl.BlockSpec(memory_space=pl.ANY)
+HBM = pl.BlockSpec(memory_space=pltpu.HBM)
 
 
 def tile_product(rows, weights):
@@ -52,28 +54,60 @@
 def step_kernel(
     phase, last, choosing,
     count_ref, delay_ref, source_ref, pick_ref, index_ref,
-    rates_ref, received_ref, intra_ref, inter_ref, external_ref, leak_ref, activity_ref, recent_ref,
+    rates_hbm, received_hbm, intra_hbm, inter_hbm, external_ref, leak_ref, activity_ref, recent_ref,
     *refs,
 ):
+    outs, scratch = refs[:-9], refs[-9:]
+    rates_ref, received_ref, intra_ref, inter_ref, rates_sem, received_sem, intra_sem, inter_sem, outer_ref = scratch
+    chosen_ref = None
     if last:
-        (activity_out_ref,) = refs
+        (activity_out_ref,) = outs
     elif choosing:
-        activity_out_ref, spread_ref, recent_out_ref, chosen_ref, older_ref = refs
+        activity_out_ref, spread_ref, recent_out_ref, chosen_hbm, older_ref, chosen_ref, chosen_sem = outs
     else:
-        activity_out_ref, spread_ref, recent_out_ref = refs
+        activity_out_ref, spread_ref, recent_out_ref = outs
     blocks, tiles = intra_ref.shape[:2]
     edges = inter_ref.shape[1]
     count = count_ref[0]
 
+    def received_copy(e):
+        return pltpu.make_async_copy(
+            received_hbm.at[source_ref[e], pl.ds(SEND_DEV * phase, SEND_DEV)], received_ref.at[e], received_sem.at[e]
+        )
+
+    def intra_copy(block):
+        return pltpu.make_async_copy(intra_hbm.at[block], intra_ref.at[block], intra_sem.at[block])
+
+    def inter_copy(block):
+        return pltpu.make_async_copy(inter_hbm.at[block], inter_ref.at[block], inter_sem.at[block])
+
+    rates_copy = pltpu.make_async_copy(rates_hbm, rates_ref, rates_sem)
+    for e in range(edges):
+        received_copy(e).start()
+    for block in range(blocks):
+        inter_copy(block).start()
+    rates_copy.start()
+    for block in range(blocks):
+        intra_copy(block).start()
+    for e in range(edges):
+        received_copy(e).wait()
+
+    def outer_body(block, carry):
+        inter_copy(block).wait()
+        rows = [received_ref[e, pick_ref[block, e]] for e in range(edges)]
+        outer_ref[block] = tile_product(rows, inter_ref[block]) + external_ref[block].astype(jnp.float32)
+        return carry
+
+    lax.fori_loop(0, blocks, outer_body, 0)
+    rates_copy.wait()
+
     def body(block, carry):
-        rows = [received_ref[source_ref[e], SEND_DEV * phase + pick_ref[block, e]] for e in range(edges)]
-        current = tile_product(rows, inter_ref[block])
+        intra_copy(block).wait()
         rows = [rates_ref[index_ref[block, k]] for k in range(tiles)]
-        current += tile_product(rows, intra_ref[block])
+        current = tile_product(rows, intra_ref[block]) + outer_ref[block]
         leak = leak_ref[block]
         alive = jnp.where(block < count, 1.0, 0.0)
-        driven = jnp.tanh(current + external_ref[block].astype(jnp.float32))
-        new = alive * ((1.0 - leak) * activity_ref[block] + leak * driven)
+        new = alive * ((1.0 - leak) * activity_ref[block] + leak * jnp.tanh(current))
         activity_out_ref[block] = new
         if not last:
             rates = new.astype(jnp.bfloat16)
@@ -81,16 +115,21 @@
                 spread_ref[pop, block] = rates
         return carry
 
-    lax.fori_loop(0, blocks, body, 0)
+    lax.fori_loop(0, SEND_DEV, body, 0)
+    if choosing:
+        older_ref[0] = spread_ref[0, :SEND_DEV]
+        for age in range(DMAX):
+            older_ref[age + 1] = recent_ref[age]
+        choose(delay_ref, older_ref, chosen_ref)
+        chosen_copy = pltpu.make_async_copy(chosen_ref, chosen_hbm, chosen_sem)
+        chosen_copy.start()
+    lax.fori_loop(SEND_DEV, blocks, body, 0)
     if not last:
         recent_out_ref[0] = spread_ref[0, :SEND_DEV]
         for age in range(1, DMAX):
             recent_out_ref[age] = recent_ref[age - 1]
     if choosing:
-        older_ref[0] = spread_ref[0, :SEND_DEV]
-        for age in range(DMAX):
-            older_ref[age + 1] = recent_ref[age]
-        choose(delay_ref, older_ref, chosen_ref)
+        chosen_copy.wait()
 
 
 def shards(
@@ -121,15 +160,18 @@
 
     f32, bf16 = jnp.float32, jnp.bfloat16
     activity_t = jax.ShapeDtypeStruct((blocks, conds, units), f32)
-    spread_t = jax.ShapeDtypeStruct((pops, blocks, conds, units), bf16)
+    spread_t = [
+        jax.ShapeDtypeStruct((1, blocks, conds, units), bf16),
+        jax.ShapeDtypeStruct((pops, blocks, conds, units), bf16),
+    ]
     recent_t = jax.ShapeDtypeStruct((DMAX, SEND_DEV, conds, units), bf16)
     chosen_t = jax.ShapeDtypeStruct((areas, SPAN * SEND_DEV, conds, units), bf16)
     older = pltpu.VMEM((DMAX + 1, SEND_DEV, conds, units), bf16)
-    params = pltpu.CompilerParams(vmem_limit_bytes=4 * 2**20)
+    params = pltpu.CompilerParams(vmem_limit_bytes=50 * 2**20)
 
     activity, spread, chosen, recent = pl.pallas_call(
         first_kernel,
-        out_shape=(activity_t, spread_t, chosen_t, recent_t),
+        out_shape=(activity_t, spread_t[0], chosen_t, recent_t),
         in_specs=[SMEM, SMEM, VMEM],
         out_specs=(VMEM,) * 4,
         scratch_shapes=[older],
@@ -139,23 +181,50 @@
     def exchange(x, axis):
         return lax.all_to_all(x, axis, split_axis=0, concat_axis=0, tiled=True)
 
+    half = pops // 2
+    strided = [list(range(parity, pops, 2)) for parity in range(2)]
+    paired = [[2 * pair, 2 * pair + 1] for pair in range(half)]
+
+    def gather(x):
+        x = lax.all_gather(x, "pop", axis=0, axis_index_groups=strided, tiled=True)
+        return lax.all_gather(x, "pop", axis=0, axis_index_groups=paired, tiled=True)
+
+    index = intra_index[0]
+    owner, place = index // blocks, index % blocks
+    indices = [((owner % 2) * half + owner // 2) * blocks + place, index]
+
+    chosen_scratch = pltpu.VMEM(chosen_t.shape, bf16)
+    scratch = [
+        pltpu.VMEM((pops * blocks, conds, units), bf16),
+        pltpu.VMEM((edges, SEND_DEV, conds, units), bf16),
+        pltpu.VMEM((blocks, tiles, units, units), bf16),
+        pltpu.VMEM((blocks, edges, units, units), bf16),
+        pltpu.SemaphoreType.DMA,
+        pltpu.SemaphoreType.DMA((edges,)),
+        pltpu.SemaphoreType.DMA((blocks,)),
+        pltpu.SemaphoreType.DMA((blocks,)),
+        pltpu.VMEM((blocks, conds, units), f32),
+    ]
     products = blocks * (tiles + edges) * units * units
     for step in range(STEPS):
         phase = step % SPAN
         if phase == 0:
             received = exchange(chosen, "area")
-        rates = exchange(spread, "pop").reshape(pops * blocks, conds, units)
+            rates = gather(spread)
+        else:
+            rates = exchange(spread, "pop")
+        rates = rates.reshape(pops * blocks, conds, units)
         last = step == STEPS - 1
         choosing = phase == SPAN - 1 and not last
-        outs = (activity_t,) if last else (activity_t, spread_t, recent_t)
+        outs = (activity_t,) if last else (activity_t, spread_t[1 - phase], recent_t)
         if choosing:
             outs += (chosen_t,)
         got = pl.pallas_call(
             functools.partial(step_kernel, phase, last, choosing),
             out_shape=outs,
-            in_specs=[SMEM] * 5 + [VMEM] * 8,
-            out_specs=(VMEM,) * len(outs),
-            scratch_shapes=[older] if choosing else [],
+            in_specs=[SMEM] * 5 + [ANY, ANY, HBM, HBM] + [VMEM] * 4,
+            out_specs=(VMEM,) * min(len(outs), 3) + (ANY,) * choosing,
+            scratch_shapes=([older, chosen_scratch, pltpu.SemaphoreType.DMA] if choosing else []) + scratch,
             compiler_params=params,
             cost_estimate=pl.CostEstimate(
                 flops=2 * products * conds,
@@ -163,7 +232,7 @@
                 transcendentals=blocks * conds * units,
             ),
         )(
-            count, delay_to, my_source, inter_pick[0], intra_index[0],
+            count, delay_to, my_source, inter_pick[0], indices[phase],
             rates, received, intra_weight[0], inter_weight[0], external[0], leak, activity, recent,
         )
         activity = got[0]

time: 374 us -> 312 us (0.83)
  blocking collectives: 294 us -> 203 us
  starting transfers between devices: 7.79 us -> 35.7 us
  Pallas kernels: 40.7 us -> 64.6 us
  waiting for transfers between devices: 14.5 us -> 0.01 us
  local copies, waits for them, and re-layouts: 12.3 us -> 5.29 us
    all_to_all x14 -> x5, blocking collectives: 294 us -> 90.5 us  [exchange(): return lax.all_to_all(x, axis, split_axis=0, concat_axis=0, tiled=True)]
    all_gather x0 -> x10, blocking collectives: none -> 112 us  [the longest x5 77.1 us: gather(): x = lax.all_gather(x, 'pop', axis=0, axis_index_groups=strided, tiled=True)]
    all_to_all x1 -> x5, starting transfers between devices: 7.79 us -> 35.7 us  [exchange(): return lax.all_to_all(x, axis, split_axis=0, concat_axis=0, tiled=True)]
    pallas_call x10, Pallas kernels: 40.1 us -> 63 us  [shards(): pl.pallas_call(functools.partial(step_kernel, phase, last, choosing), out...]
    all_to_all x1 -> x5, waiting for transfers between devices: 14.5 us -> 0.01 us  [exchange(): return lax.all_to_all(x, axis, split_axis=0, concat_axis=0, tiled=True)]
    unnamed x30 -> x16, local copies, waits for them, and re-layouts: 10.2 us -> 3.17 us
  transfers between devices with their start and end apart: 1 -> 5, of which waited for: 1 -> 0; matrix products, arithmetic and copies ran while one was open for 0% -> 1% of each run, Pallas kernels for 0% -> 0%
where the time goes in v3:
time: 312 us; the launch traced here: 311 us
  blocking collectives  203 us (65%)
  Pallas kernels  64.6 us (21%)
  starting transfers between devices  35.7 us (11%)
  local copies, waits for them, and re-layouts  5.29 us (2%)
    all_to_all x5, blocking collectives, exchange(): return lax.all_to_all(x, axis, split_axis=0, concat_axis=0, tiled=True)  90.5 us
    all_gather x5, blocking collectives, gather(): x = lax.all_gather(x, 'pop', axis=0, axis_index_groups=strided, tiled=True)  77.1 us
    pallas_call x10, Pallas kernels, shards(): pl.pallas_call(functools.partial(step_kernel, phase, last, choosing), out...  63 us
    all_to_all x5, starting transfers between devices, exchange(): return lax.all_to_all(x, axis, split_axis=0, concat_axis=0, tiled=True)  35.7 us
    all_gather x5, blocking collectives, gather(): lax.all_gather(x, 'pop', axis=0, axis_index_groups=paired, tiled=True)  35.2 us
  transfers between devices with their start and end apart: 5, of which 0 were waited for; matrix products, arithmetic and copies ran while one was open for 1% of the time, Pallas kernels for 0%

profile of v3, /device:TPU:4, one launch (start us, length us, event | category | flops | bytes accessed | tf_op | source)
XLA Modules:
  0.0 310.7 jit_solution(18260181084739424922)
XLA Ops:
  0.0 0.7 select_reduce_fusion
  0.7 1.2 dynamic_slice.6
  2.6 0.0 copy-start.6
  2.6 0.9 copy-done.6
  3.6 1.6 shard_map.100
  5.2 0.0 copy-start.5
  5.2 0.0 copy-start.7
  5.2 7.7 %all-to-all-start = ((bf16[32,4,32,128]{3,2,1,0:T(8,128)(2,1)}), bf16[32,4,32,128]{3,2,1,0:T(8,128)(2,1)S(1)}, u32[]{:S(2)}, u32[]{:S(2)}) async-start(bf16[32,4,32,128]{3,2,1,0:T(8,128)(2,1)} %get-tuple-element.41), calls=%async_computation | async-start | bytes 2097152 | tf_op jit(solution)/shard_map/all_to_all | solution.py:182
  13.0 0.9 dynamic-slice_reduce_fusion.source_ref
  13.8 17.7 %all_gather.30 = bf16[4,8,32,128]{3,2,1,0:T(8,128)(2,1)S(1)} all-gather(bf16[1,8,32,128]{3,2,1,0:T(8,128)(2,1)S(1)} %get-tuple-element.40), channel_id=1, replica_groups={{0,2,4,6},{1,3,5,7},{8,10,12,14},{9,11,13,15},{16,18,20,22},{17,19,21,2..., dimensions={0}, use_global_device_ids=true | all-gather | bytes 327680 | tf_op jit(solution)/shard_map/all_gather | solution.py:189
  31.5 7.0 %all_gather.31 = bf16[8,8,32,128]{3,2,1,0:T(8,128)(2,1)S(1)} all-gather(bf16[4,8,32,128]{3,2,1,0:T(8,128)(2,1)S(1)} %all_gather.30), channel_id=1, replica_groups={{0,1},{2,3},{4,5},{6,7},{8,9},{10,11},{12,13},{14,15},{16,17},{18,19},{..., dimensions={0}, use_global_device_ids=true | all-gather | bytes 786432 | tf_op jit(solution)/shard_map/all_gather | solution.py:190
  38.6 0.7 fusion.3.index_ref
  39.3 0.0 all-to-all-done.received_hbm
  39.3 0.0 copy-start
  39.3 0.8 copy-done
  40.1 0.0 copy-start.2
  40.1 0.7 copy-done.2
  40.8 0.0 copy-start.4
  40.8 0.7 copy-done.4
  41.5 6.2 %shard_map.101 = (f32[8,32,128]{2,1,0:T(8,128)S(1)}, bf16[8,8,32,128]{3,2,1,0:T(8,128)(2,1)S(1)}, bf16[3,2,32,128]{3,2,1,0:T(8,128)(2,1)S(1)}) custom-call(s32[1]{0:T(128)} %bitcast.1.count_ref, s32[32]{0:T(128)S(1)} %broadcast_maximum_fusion.delay_ref, s32[12]{0:T(128)S(1)} %dynamic-slice_reduce_fusion.source_ref, s32[8,12]{1,0:T(8,128)S(1)} %bitcast.41, ...), custom_call_target="tpu_custom_call" | custom-call | flops 369098752 | bytes 11534336 | tf_op jit(solution)/shard_map/pallas_call | solution.py:222
  47.7 19.3 %all_to_all.50 = bf16[8,8,32,128]{3,2,1,0:T(8,128)(2,1)S(1)} all-to-all(bf16[8,8,32,128]{3,2,1,0:T(8,128)(2,1)S(1)} %get-tuple-element.44), channel_id=1, replica_groups=mesh['area'=32,'pop'=8] {'pop'}, dimensions={0} | all-to-all | bytes 1048576 | tf_op jit(solution)/shard_map/all_to_all | solution.py:182
  67.0 0.0 copy-start.1
  67.0 0.0 copy-start.3
  67.0 0.0 copy-done.5
  67.0 0.0 copy-done.7
  67.0 6.3 %shard_map.102 = (f32[8,32,128]{2,1,0:T(8,128)S(1)}, bf16[1,8,32,128]{3,2,1,0:T(8,128)(2,1)S(1)}, bf16[3,2,32,128]{3,2,1,0:T(8,128)(2,1)S(1)}, bf16[32,4,32,128]{3,2,1,0:T(8,128)(2,1)}) custom-call(s32[1]{0:T(128)} %bitcast.1.count_ref, s32[32]{0:T(128)S(1)} %broadcast_maximum_fusion.delay_ref, s32[12]{0:T(128)S(1)} %dynamic-slice_reduce_fusion.source_ref, ...), custom_call_target="tpu_custom_call" | custom-call | flops 369098752 | bytes 11534336 | tf_op jit(solution)/shard_map/pallas_call | solution.py:222
  73.3 7.2 %all-to-all-start.2 = ((bf16[32,4,32,128]{3,2,1,0:T(8,128)(2,1)}), bf16[32,4,32,128]{3,2,1,0:T(8,128)(2,1)S(1)}, u32[]{:S(2)}, u32[]{:S(2)}) async-start(bf16[32,4,32,128]{3,2,1,0:T(8,128)(2,1)} %get-tuple-element.48), calls=%async_computation.2 | async-start | bytes 2097152 | tf_op jit(solution)/shard_map/all_to_all | solution.py:182
  80.5 14.9 %all_gather.32 = bf16[4,8,32,128]{3,2,1,0:T(8,128)(2,1)S(1)} all-gather(bf16[1,8,32,128]{3,2,1,0:T(8,128)(2,1)S(1)} %get-tuple-element.47), channel_id=1, replica_groups={{0,2,4,6},{1,3,5,7},{8,10,12,14},{9,11,13,15},{16,18,20,22},{17,19,21,2..., dimensions={0}, use_global_device_ids=true | all-gather | bytes 327680 | tf_op jit(solution)/shard_map/all_gather | solution.py:189
  95.4 7.0 %all_gather.33 = bf16[8,8,32,128]{3,2,1,0:T(8,128)(2,1)S(1)} all-gather(bf16[4,8,32,128]{3,2,1,0:T(8,128)(2,1)S(1)} %all_gather.32), channel_id=1, replica_groups={{0,1},{2,3},{4,5},{6,7},{8,9},{10,11},{12,13},{14,15},{16,17},{18,19},{..., dimensions={0}, use_global_device_ids=true | all-gather | bytes 786432 | tf_op jit(solution)/shard_map/all_gather | solution.py:190
  102.5 0.0 all-to-all-done.2.received_hbm
  102.5 0.0 copy-done.1
  102.5 0.0 copy-done.3
  102.5 6.2 %shard_map.103 = (f32[8,32,128]{2,1,0:T(8,128)S(1)}, bf16[8,8,32,128]{3,2,1,0:T(8,128)(2,1)S(1)}, bf16[3,2,32,128]{3,2,1,0:T(8,128)(2,1)S(1)}) custom-call(s32[1]{0:T(128)} %bitcast.1.count_ref, s32[32]{0:T(128)S(1)} %broadcast_maximum_fusion.delay_ref, s32[12]{0:T(128)S(1)} %dynamic-slice_reduce_fusion.source_ref, s32[8,12]{1,0:T(8,128)S(1)} %bitcast.43, ...), custom_call_target="tpu_custom_call" | custom-call | flops 369098752 | bytes 11534336 | tf_op jit(solution)/shard_map/pallas_call | solution.py:222
  108.7 17.7 %all_to_all.51 = bf16[8,8,32,128]{3,2,1,0:T(8,128)(2,1)S(1)} all-to-all(bf16[8,8,32,128]{3,2,1,0:T(8,128)(2,1)S(1)} %get-tuple-element.51), channel_id=1, replica_groups=mesh['area'=32,'pop'=8] {'pop'}, dimensions={0} | all-to-all | bytes 1048576 | tf_op jit(solution)/shard_map/all_to_all | solution.py:182
  126.4 6.3 %shard_map.104 = (f32[8,32,128]{2,1,0:T(8,128)S(1)}, bf16[1,8,32,128]{3,2,1,0:T(8,128)(2,1)S(1)}, bf16[3,2,32,128]{3,2,1,0:T(8,128)(2,1)S(1)}, bf16[32,4,32,128]{3,2,1,0:T(8,128)(2,1)}) custom-call(s32[1]{0:T(128)} %bitcast.1.count_ref, s32[32]{0:T(128)S(1)} %broadcast_maximum_fusion.delay_ref, s32[12]{0:T(128)S(1)} %dynamic-slice_reduce_fusion.source_ref, ...), custom_call_target="tpu_custom_call" | custom-call | flops 369098752 | bytes 11534336 | tf_op jit(solution)/shard_map/pallas_call | solution.py:222
  132.7 6.9 %all-to-all-start.4 = ((bf16[32,4,32,128]{3,2,1,0:T(8,128)(2,1)}), bf16[32,4,32,128]{3,2,1,0:T(8,128)(2,1)S(1)}, u32[]{:S(2)}, u32[]{:S(2)}) async-start(bf16[32,4,32,128]{3,2,1,0:T(8,128)(2,1)} %get-tuple-element.55), calls=%async_computation.4 | async-start | bytes 2097152 | tf_op jit(solution)/shard_map/all_to_all | solution.py:182
  139.5 14.8 %all_gather.34 = bf16[4,8,32,128]{3,2,1,0:T(8,128)(2,1)S(1)} all-gather(bf16[1,8,32,128]{3,2,1,0:T(8,128)(2,1)S(1)} %get-tuple-element.54), channel_id=1, replica_groups={{0,2,4,6},{1,3,5,7},{8,10,12,14},{9,11,13,15},{16,18,20,22},{17,19,21,2..., dimensions={0}, use_global_device_ids=true | all-gather | bytes 327680 | tf_op jit(solution)/shard_map/all_gather | solution.py:189
  154.4 7.0 %all_gather.35 = bf16[8,8,32,128]{3,2,1,0:T(8,128)(2,1)S(1)} all-gather(bf16[4,8,32,128]{3,2,1,0:T(8,128)(2,1)S(1)} %all_gather.34), channel_id=1, replica_groups={{0,1},{2,3},{4,5},{6,7},{8,9},{10,11},{12,13},{14,15},{16,17},{18,19},{..., dimensions={0}, use_global_device_ids=true | all-gather | bytes 786432 | tf_op jit(solution)/shard_map/all_gather | solution.py:190
  161.4 0.0 all-to-all-done.4.received_hbm
  161.4 6.2 %shard_map.105 = (f32[8,32,128]{2,1,0:T(8,128)S(1)}, bf16[8,8,32,128]{3,2,1,0:T(8,128)(2,1)S(1)}, bf16[3,2,32,128]{3,2,1,0:T(8,128)(2,1)S(1)}) custom-call(s32[1]{0:T(128)} %bitcast.1.count_ref, s32[32]{0:T(128)S(1)} %broadcast_maximum_fusion.delay_ref, s32[12]{0:T(128)S(1)} %dynamic-slice_reduce_fusion.source_ref, s32[8,12]{1,0:T(8,128)S(1)} %bitcast.45, ...), custom_call_target="tpu_custom_call" | custom-call | flops 369098752 | bytes 11534336 | tf_op jit(solution)/shard_map/pallas_call | solution.py:222
  167.6 17.9 %all_to_all.52 = bf16[8,8,32,128]{3,2,1,0:T(8,128)(2,1)S(1)} all-to-all(bf16[8,8,32,128]{3,2,1,0:T(8,128)(2,1)S(1)} %get-tuple-element.58), channel_id=1, replica_groups=mesh['area'=32,'pop'=8] {'pop'}, dimensions={0} | all-to-all | bytes 1048576 | tf_op jit(solution)/shard_map/all_to_all | solution.py:182
  185.5 6.3 %shard_map.106 = (f32[8,32,128]{2,1,0:T(8,128)S(1)}, bf16[1,8,32,128]{3,2,1,0:T(8,128)(2,1)S(1)}, bf16[3,2,32,128]{3,2,1,0:T(8,128)(2,1)S(1)}, bf16[32,4,32,128]{3,2,1,0:T(8,128)(2,1)}) custom-call(s32[1]{0:T(128)} %bitcast.1.count_ref, s32[32]{0:T(128)S(1)} %broadcast_maximum_fusion.delay_ref, s32[12]{0:T(128)S(1)} %dynamic-slice_reduce_fusion.source_ref, ...), custom_call_target="tpu_custom_call" | custom-call | flops 369098752 | bytes 11534336 | tf_op jit(solution)/shard_map/pallas_call | solution.py:222
  191.8 6.9 %all-to-all-start.6 = ((bf16[32,4,32,128]{3,2,1,0:T(8,128)(2,1)}), bf16[32,4,32,128]{3,2,1,0:T(8,128)(2,1)S(1)}, u32[]{:S(2)}, u32[]{:S(2)}) async-start(bf16[32,4,32,128]{3,2,1,0:T(8,128)(2,1)} %get-tuple-element.62), calls=%async_computation.6 | async-start | bytes 2097152 | tf_op jit(solution)/shard_map/all_to_all | solution.py:182
  198.7 14.9 %all_gather.36 = bf16[4,8,32,128]{3,2,1,0:T(8,128)(2,1)S(1)} all-gather(bf16[1,8,32,128]{3,2,1,0:T(8,128)(2,1)S(1)} %get-tuple-element.61), channel_id=1, replica_groups={{0,2,4,6},{1,3,5,7},{8,10,12,14},{9,11,13,15},{16,18,20,22},{17,19,21,2..., dimensions={0}, use_global_device_ids=true | all-gather | bytes 327680 | tf_op jit(solution)/shard_map/all_gather | solution.py:189
  213.6 7.0 %all_gather.37 = bf16[8,8,32,128]{3,2,1,0:T(8,128)(2,1)S(1)} all-gather(bf16[4,8,32,128]{3,2,1,0:T(8,128)(2,1)S(1)} %all_gather.36), channel_id=1, replica_groups={{0,1},{2,3},{4,5},{6,7},{8,9},{10,11},{12,13},{14,15},{16,17},{18,19},{..., dimensions={0}, use_global_device_ids=true | all-gather | bytes 786432 | tf_op jit(solution)/shard_map/all_gather | solution.py:190
  220.6 0.0 all-to-all-done.6.received_hbm
  220.6 6.2 %shard_map.107 = (f32[8,32,128]{2,1,0:T(8,128)S(1)}, bf16[8,8,32,128]{3,2,1,0:T(8,128)(2,1)S(1)}, bf16[3,2,32,128]{3,2,1,0:T(8,128)(2,1)S(1)}) custom-call(s32[1]{0:T(128)} %bitcast.1.count_ref, s32[32]{0:T(128)S(1)} %broadcast_maximum_fusion.delay_ref, s32[12]{0:T(128)S(1)} %dynamic-slice_reduce_fusion.source_ref, s32[8,12]{1,0:T(8,128)S(1)} %bitcast.47, ...), custom_call_target="tpu_custom_call" | custom-call | flops 369098752 | bytes 11534336 | tf_op jit(solution)/shard_map/pallas_call | solution.py:222
  226.8 17.8 %all_to_all.53 = bf16[8,8,32,128]{3,2,1,0:T(8,128)(2,1)S(1)} all-to-all(bf16[8,8,32,128]{3,2,1,0:T(8,128)(2,1)S(1)} %get-tuple-element.65), channel_id=1, replica_groups=mesh['area'=32,'pop'=8] {'pop'}, dimensions={0} | all-to-all | bytes 1048576 | tf_op jit(solution)/shard_map/all_to_all | solution.py:182
  244.6 6.3 %shard_map.108 = (f32[8,32,128]{2,1,0:T(8,128)S(1)}, bf16[1,8,32,128]{3,2,1,0:T(8,128)(2,1)S(1)}, bf16[3,2,32,128]{3,2,1,0:T(8,128)(2,1)S(1)}, bf16[32,4,32,128]{3,2,1,0:T(8,128)(2,1)}) custom-call(s32[1]{0:T(128)} %bitcast.1.count_ref, s32[32]{0:T(128)S(1)} %broadcast_maximum_fusion.delay_ref, s32[12]{0:T(128)S(1)} %dynamic-slice_reduce_fusion.source_ref, ...), custom_call_target="tpu_custom_call" | custom-call | flops 369098752 | bytes 11534336 | tf_op jit(solution)/shard_map/pallas_call | solution.py:222
  250.9 7.0 %all-to-all-start.8 = ((bf16[32,4,32,128]{3,2,1,0:T(8,128)(2,1)}), bf16[32,4,32,128]{3,2,1,0:T(8,128)(2,1)S(1)}, u32[]{:S(2)}, u32[]{:S(2)}) async-start(bf16[32,4,32,128]{3,2,1,0:T(8,128)(2,1)} %get-tuple-element.69), calls=%async_computation.8 | async-start | bytes 2097152 | tf_op jit(solution)/shard_map/all_to_all | solution.py:182
  257.9 14.8 %all_gather.38 = bf16[4,8,32,128]{3,2,1,0:T(8,128)(2,1)S(1)} all-gather(bf16[1,8,32,128]{3,2,1,0:T(8,128)(2,1)S(1)} %get-tuple-element.68), channel_id=1, replica_groups={{0,2,4,6},{1,3,5,7},{8,10,12,14},{9,11,13,15},{16,18,20,22},{17,19,21,2..., dimensions={0}, use_global_device_ids=true | all-gather | bytes 327680 | tf_op jit(solution)/shard_map/all_gather | solution.py:189
  272.7 7.0 %all_gather.39 = bf16[8,8,32,128]{3,2,1,0:T(8,128)(2,1)S(1)} all-gather(bf16[4,8,32,128]{3,2,1,0:T(8,128)(2,1)S(1)} %all_gather.38), channel_id=1, replica_groups={{0,1},{2,3},{4,5},{6,7},{8,9},{10,11},{12,13},{14,15},{16,17},{18,19},{..., dimensions={0}, use_global_device_ids=true | all-gather | bytes 786432 | tf_op jit(solution)/shard_map/all_gather | solution.py:190
  279.8 0.0 all-to-all-done.8.received_hbm
  279.8 6.2 %shard_map.109 = (f32[8,32,128]{2,1,0:T(8,128)S(1)}, bf16[8,8,32,128]{3,2,1,0:T(8,128)(2,1)S(1)}, bf16[3,2,32,128]{3,2,1,0:T(8,128)(2,1)S(1)}) custom-call(s32[1]{0:T(128)} %bitcast.1.count_ref, s32[32]{0:T(128)S(1)} %broadcast_maximum_fusion.delay_ref, s32[12]{0:T(128)S(1)} %dynamic-slice_reduce_fusion.source_ref, s32[8,12]{1,0:T(8,128)S(1)} %bitcast.49, ...), custom_call_target="tpu_custom_call" | custom-call | flops 369098752 | bytes 11534336 | tf_op jit(solution)/shard_map/pallas_call | solution.py:222
  286.0 17.9 %all_to_all.54 = bf16[8,8,32,128]{3,2,1,0:T(8,128)(2,1)S(1)} all-to-all(bf16[8,8,32,128]{3,2,1,0:T(8,128)(2,1)S(1)} %get-tuple-element.72), channel_id=1, replica_groups=mesh['area'=32,'pop'=8] {'pop'}, dimensions={0} | all-to-all | bytes 1048576 | tf_op jit(solution)/shard_map/all_to_all | solution.py:182
  303.9 6.8 %shard_map.110 = f32[8,32,128]{2,1,0:T(8,128)} custom-call(s32[1]{0:T(128)} %bitcast.1.count_ref, s32[32]{0:T(128)S(1)} %broadcast_maximum_fusion.delay_ref, s32[12]{0:T(128)S(1)} %dynamic-slice_reduce_fusion.source_ref, s32[8,12]{1,0:T(8,128)S(1)} %bitcast.50, s32[8,32]{1,0:T(8,128)S(1)} %bitcast.66, bf16[64,32,128]{2,1,0:T(8,128)(2,1)S(1)} %bitcast.40, ...), custom_call_target="tpu_custom_call" | custom-call | flops 369098752 | bytes 11534336 | tf_op jit(solution)/shard_map/pallas_call | solution.py:222
  (1 shorter events, 0.0 us)
Async XLA Ops:
  2.6 1.0 copy-start.6
  5.2 61.8 %copy-start.5 = (f32[1,8,128]{2,1,0:T(8,128)S(1)}, f32[1,8,128]{2,1,0:T(8,128)}, u32[]{:S(2)}) copy-start(f32[1,8,128]{2,1,0:T(8,128)} %param.12) | copy-start | bytes 12292
  5.2 61.8 %copy-start.7 = (s32[1,8,32]{2,1,0:T(8,128)S(1)}, s32[1,8,32]{2,1,0:T(8,128)}, u32[]{:S(2)}) copy-start(s32[1,8,32]{2,1,0:T(8,128)} %param.13) | copy-start | bytes 3076
  5.2 34.0 %all-to-all-start = ((bf16[32,4,32,128]{3,2,1,0:T(8,128)(2,1)}), bf16[32,4,32,128]{3,2,1,0:T(8,128)(2,1)S(1)}, u32[]{:S(2)}, u32[]{:S(2)}) async-start(bf16[32,4,32,128]{3,2,1,0:T(8,128)(2,1)} %get-tuple-element.41), calls=%async_computation | async-start | bytes 2097152 | tf_op jit(solution)/shard_map/all_to_all | solution.py:182
  39.3 0.8 copy-start
  40.1 0.7 copy-start.2
  40.8 0.7 copy-start.4
  67.0 35.5 %copy-start.1 = (bf16[1,8,32,128]{3,2,1,0:T(8,128)(2,1)S(1)}, bf16[1,8,32,128]{3,2,1,0:T(8,128)(2,1)}, u32[]{:S(2)}) copy-start(bf16[1,8,32,128]{3,2,1,0:T(8,128)(2,1)} %param.11) | copy-start | bytes 196612
  67.0 35.5 %copy-start.3 = (s32[1,8,12]{2,1,0:T(8,128)S(1)}, s32[1,8,12]{2,1,0:T(8,128)}, u32[]{:S(2)}) copy-start(s32[1,8,12]{2,1,0:T(8,128)} %param.15) | copy-start | bytes 1156
  73.3 29.2 %all-to-all-start.2 = ((bf16[32,4,32,128]{3,2,1,0:T(8,128)(2,1)}), bf16[32,4,32,128]{3,2,1,0:T(8,128)(2,1)S(1)}, u32[]{:S(2)}, u32[]{:S(2)}) async-start(bf16[32,4,32,128]{3,2,1,0:T(8,128)(2,1)} %get-tuple-element.48), calls=%async_computation.2 | async-start | bytes 2097152 | tf_op jit(solution)/shard_map/all_to_all | solution.py:182
  132.7 28.8 %all-to-all-start.4 = ((bf16[32,4,32,128]{3,2,1,0:T(8,128)(2,1)}), bf16[32,4,32,128]{3,2,1,0:T(8,128)(2,1)S(1)}, u32[]{:S(2)}, u32[]{:S(2)}) async-start(bf16[32,4,32,128]{3,2,1,0:T(8,128)(2,1)} %get-tuple-element.55), calls=%async_computation.4 | async-start | bytes 2097152 | tf_op jit(solution)/shard_map/all_to_all | solution.py:182
  191.8 28.8 %all-to-all-start.6 = ((bf16[32,4,32,128]{3,2,1,0:T(8,128)(2,1)}), bf16[32,4,32,128]{3,2,1,0:T(8,128)(2,1)S(1)}, u32[]{:S(2)}, u32[]{:S(2)}) async-start(bf16[32,4,32,128]{3,2,1,0:T(8,128)(2,1)} %get-tuple-element.62), calls=%async_computation.6 | async-start | bytes 2097152 | tf_op jit(solution)/shard_map/all_to_all | solution.py:182
  250.9 28.8 %all-to-all-start.8 = ((bf16[32,4,32,128]{3,2,1,0:T(8,128)(2,1)}), bf16[32,4,32,128]{3,2,1,0:T(8,128)(2,1)S(1)}, u32[]{:S(2)}, u32[]{:S(2)}) async-start(bf16[32,4,32,128]{3,2,1,0:T(8,128)(2,1)} %get-tuple-element.69), calls=%async_computation.8 | async-start | bytes 2097152 | tf_op jit(solution)/shard_map/all_to_all | solution.py:182

commit v4 on v3

v4 whole, which is shorter than its diff:
```python
import functools
import jax
import jax.numpy as jnp
from jax import lax
from jax.experimental import pallas as pl
from jax.experimental.pallas import tpu as pltpu
from jax.sharding import PartitionSpec as P

SEND_DEV = 2
STEPS = 10
DMAX = 3
SPAN = 2

VMEM = pl.BlockSpec(memory_space=pltpu.VMEM)
SMEM = pl.BlockSpec(memory_space=pltpu.SMEM)
ANY = pl.BlockSpec(memory_space=pl.ANY)
HBM = pl.BlockSpec(memory_space=pltpu.HBM)


def tile_product(rows, weights):
    lhs = jnp.concatenate(rows, axis=1)
    rhs = weights.reshape(lhs.shape[1], weights.shape[-1])
    return lax.dot_general(
        lhs, rhs, (((1,), (0,)), ((), ())), preferred_element_type=jnp.float32
    )


def choose(delay_ref, older_ref, chosen_ref):
    for area in range(chosen_ref.shape[0]):
        delay = delay_ref[area]
        chosen_ref[area, :SEND_DEV] = older_ref[delay]
        chosen_ref[area, SEND_DEV:] = older_ref[delay - 1]


def first_kernel(
    delay_ref, source_ref, live_ref, index_ref, history_hbm, *refs
):
    moved = (len(refs) - 14) // 2
    sources, outs, places = refs[:moved], refs[moved : moved + 6], refs[moved + 6 : 2 * moved + 6]
    activity_ref, rates_ref, chosen_hbm, recent_ref, table_ref, gathered_index_ref = outs
    scratch = refs[2 * moved + 6 :]
    history_ref, tail_ref, older_ref, chosen_ref, history_sem, tail_sem, chosen_sem, moved_sem = scratch
    blocks = activity_ref.shape[0]
    edges = source_ref.shape[0]
    area = lax.axis_index("area")
    pops = lax.axis_size("pop")
    tail_copy = pltpu.make_async_copy(history_hbm.at[:, pl.ds(0, SEND_DEV)], tail_ref, tail_sem)
    history_copy = pltpu.make_async_copy(history_hbm.at[0], history_ref, history_sem)
    tail_copy.start()
    history_copy.start()
    copies = [pltpu.make_async_copy(sources[i], places[i], moved_sem.at[i]) for i in range(moved)]
    for copy in copies:
        copy.start()
    count = live_ref[area] - lax.axis_index("pop") * blocks
    table_ref[0] = count
    for e in range(edges):
        table_ref[1 + e] = source_ref[e, area]
    owner, place = index_ref[...] // blocks, index_ref[...] % blocks
    gathered_index_ref[...] = ((owner % 2) * (pops // 2) + owner // 2) * blocks + place
    tail_copy.wait()
    for block in range(SEND_DEV):
        alive = jnp.where(block < count, 1.0, 0.0)
        for age in range(DMAX + 1):
            rates = (tail_ref[age, block].astype(jnp.float32) * alive).astype(jnp.bfloat16)
            older_ref[age, block] = rates
            if age < DMAX:
                recent_ref[age, block] = rates
    choose(delay_ref, older_ref, chosen_ref)
    chosen_copy = pltpu.make_async_copy(chosen_ref, chosen_hbm, chosen_sem)
    chosen_copy.start()
    history_copy.wait()
    for block in range(blocks):
        alive = jnp.where(block < count, 1.0, 0.0)
        rates = (history_ref[block].astype(jnp.float32) * alive).astype(jnp.bfloat16)
        activity_ref[block] = rates.astype(jnp.float32)
        rates_ref[0, block] = rates
    for copy in copies:
        copy.wait()
    chosen_copy.wait()


def step_kernel(
    phase, last, choosing,
    table_any, delay_any, pick_any, index_any,
    rates_any, received_any, intra_hbm, inter_hbm, external_ref, leak_ref, activity_ref, recent_ref,
    *refs,
):
    table_ref, delay_ref, pick_ref, index_ref, table_sem, rates_ref, received_ref, intra_ref, inter_ref = refs[:9]
    outer_ref, rates_sem, received_sem, intra_sem, inter_sem = refs[9:14]
    outs = list(refs[14:])
    activity_out_ref = outs.pop(0)
    if not last:
        spread_ref, recent_out_ref = outs.pop(0), outs.pop(0)
    if choosing:
        chosen_hbm, older_ref, chosen_ref, chosen_sem = outs
    blocks, tiles = intra_ref.shape[:2]
    edges = inter_ref.shape[1]

    def received_copy(e):
        return pltpu.make_async_copy(
            received_any.at[table_ref[1 + e], pl.ds(SEND_DEV * phase, SEND_DEV)], received_ref.at[e], received_sem.at[e]
        )

    def intra_copy(block):
        return pltpu.make_async_copy(intra_hbm.at[block], intra_ref.at[block], intra_sem.at[block])

    def inter_copy(block):
        return pltpu.make_async_copy(inter_hbm.at[block], inter_ref.at[block], inter_sem.at[block])

    tables = [(table_any, table_ref), (pick_any, pick_ref), (index_any, index_ref)]
    if choosing:
        tables.append((delay_any, delay_ref))
    table_copies = [pltpu.make_async_copy(src, dst, table_sem.at[i]) for i, (src, dst) in enumerate(tables)]
    rates_copy = pltpu.make_async_copy(rates_any, rates_ref, rates_sem)
    for copy in table_copies:
        copy.start()
    for block in range(blocks):
        inter_copy(block).start()
    rates_copy.start()
    for block in range(blocks):
        intra_copy(block).start()
    table_copies[0].wait()
    for e in range(edges):
        received_copy(e).start()
    for copy in table_copies[1:]:
        copy.wait()
    count = table_ref[0]
    for e in range(edges):
        received_copy(e).wait()

    def outer_body(block, carry):
        inter_copy(block).wait()
        rows = [received_ref[e, pick_ref[block, e]] for e in range(edges)]
        outer_ref[block] = tile_product(rows, inter_ref[block]) + external_ref[block].astype(jnp.float32)
        return carry

    lax.fori_loop(0, blocks, outer_body, 0)
    rates_copy.wait()

    def body(block, carry):
        intra_copy(block).wait()
        rows = [rates_ref[index_ref[block, k]] for k in range(tiles)]
        current = tile_product(rows, intra_ref[block]) + outer_ref[block]
        leak = leak_ref[pl.ds(block, 1), :]
        alive = jnp.where(block < count, 1.0, 0.0)
        new = alive * ((1.0 - leak) * activity_ref[block] + leak * jnp.tanh(current))
        activity_out_ref[block] = new
        if not last:
            rates = new.astype(jnp.bfloat16)
            for pop in range(spread_ref.shape[0]):
                spread_ref[pop, block] = rates
        return carry

    lax.fori_loop(0, SEND_DEV, body, 0)
    if choosing:
        older_ref[0] = spread_ref[0, :SEND_DEV]
        for age in range(DMAX):
            older_ref[age + 1] = recent_ref[age]
        choose(delay_ref, older_ref, chosen_ref)
        chosen_copy = pltpu.make_async_copy(chosen_ref, chosen_hbm, chosen_sem)
        chosen_copy.start()
    lax.fori_loop(SEND_DEV, blocks, body, 0)
    if not last:
        recent_out_ref[0] = spread_ref[0, :SEND_DEV]
        for age in range(1, DMAX):
            recent_out_ref[age] = recent_ref[age - 1]
    if choosing:
        chosen_copy.wait()


def ordered_kernel(n_in, n_out, n_common, kernel):
    def run(*refs):
        ins, outs, scratch = refs[:n_in], refs[n_in : n_in + n_out], refs[n_in + n_out :]
        kernel(*ins, *scratch[:n_common], *outs, *scratch[n_common:])

    return run


def shards(
    history,
    external,
    leak_rate,
    intra_index,
    intra_weight,
    inter_pick,
    inter_weight,
    source_area,
    delays,
    live_blocks,
):
    areas = lax.axis_size("area")
    pops = lax.axis_size("pop")
    history = history[:, 0]
    blocks, conds, units = history.shape[1:]
    tiles = intra_index.shape[2]
    edges = inter_pick.shape[2]

    f32, bf16, i32 = jnp.float32, jnp.bfloat16, jnp.int32
    shape = jax.ShapeDtypeStruct
    activity_t = shape((blocks, conds, units), f32)
    spread_t = [shape((pops, blocks, conds, units), bf16), shape((1, blocks, conds, units), bf16)]
    recent_t = shape((DMAX, SEND_DEV, conds, units), bf16)
    chosen_t = shape((areas, SPAN * SEND_DEV, conds, units), bf16)
    older = pltpu.VMEM((DMAX + 1, SEND_DEV, conds, units), bf16)
    chosen_scratch = pltpu.VMEM(chosen_t.shape, bf16)
    one = pltpu.SemaphoreType.DMA
    params = pltpu.CompilerParams(vmem_limit_bytes=50 * 2**20)

    area_pos = lax.axis_index("area")
    delay_to = jnp.sum(jnp.where(source_area == area_pos, delays, 0), axis=1)
    delay_to = jnp.maximum(delay_to, 1)
    moved = [external[0], leak_rate[0], inter_pick[0], intra_index[0]]
    activity, spread, chosen, recent, table, gathered_index, *moved = pl.pallas_call(
        first_kernel,
        out_shape=(
            activity_t, spread_t[1], chosen_t, recent_t,
            shape((1 + edges,), i32), shape((blocks, tiles), i32),
            *(shape(x.shape, x.dtype) for x in moved),
        ),
        in_specs=[SMEM] * 3 + [VMEM, ANY] + [ANY] * len(moved),
        out_specs=(VMEM, VMEM, ANY, VMEM, SMEM, VMEM) + (VMEM,) * len(moved),
        scratch_shapes=[
            pltpu.VMEM((blocks, conds, units), bf16),
            pltpu.VMEM((DMAX + 1, SEND_DEV, conds, units), bf16),
            older, chosen_scratch, one, one, one, pltpu.SemaphoreType.DMA((len(moved),)),
        ],
        compiler_params=pltpu.CompilerParams(vmem_limit_bytes=50 * 2**20),
    )(delay_to, source_area.T, live_blocks, intra_index[0], history, *moved)
    external, leak, pick, index = moved
    inter = inter_weight[0]

    def exchange(x, axis):
        return lax.all_to_all(x, axis, split_axis=0, concat_axis=0, tiled=True)

    strided = [list(range(parity, pops, 2)) for parity in range(2)]
    paired = [[2 * pair, 2 * pair + 1] for pair in range(pops // 2)]

    def gather(x):
        x = lax.all_gather(x, "pop", axis=0, axis_index_groups=strided, tiled=True)
        return lax.all_gather(x, "pop", axis=0, axis_index_groups=paired, tiled=True)

    common = [
        pltpu.SMEM((1 + edges,), i32),
        pltpu.SMEM((areas,), i32),
        pltpu.SMEM((blocks, edges), i32),
        pltpu.SMEM((blocks, tiles), i32),
        pltpu.SemaphoreType.DMA((4,)),
        pltpu.VMEM((pops * blocks, conds, units), bf16),
        pltpu.VMEM((edges, SEND_DEV, conds, units), bf16),
        pltpu.VMEM((blocks, tiles, units, units), bf16),
        pltpu.VMEM((blocks, edges, units, units), bf16),
        pltpu.VMEM((blocks, conds, units), f32),
        one,
        pltpu.SemaphoreType.DMA((edges,)),
        pltpu.SemaphoreType.DMA((blocks,)),
        pltpu.SemaphoreType.DMA((blocks,)),
    ]
    products = blocks * (tiles + edges) * units * units
    for step in range(STEPS):
        phase = step % SPAN
        last = step == STEPS - 1
        choosing = phase == SPAN - 1 and not last
        if phase == 0:
            received = exchange(chosen, "area")
            rates = gather(spread)
        else:
            rates = exchange(spread, "pop")
        outs, places, scratch = [activity_t], [VMEM], []
        if not last:
            outs += [spread_t[phase], recent_t]
            places += [VMEM, VMEM]
        if choosing:
            outs.append(chosen_t)
            places.append(ANY)
            scratch += [older, chosen_scratch, one]
        ins = (
            table, delay_to, pick, index if phase else gathered_index,
            rates.reshape(pops * blocks, conds, units), received, intra_weight[0], inter,
            external, leak, activity, recent,
        )
        got = pl.pallas_call(
            ordered_kernel(len(ins), len(outs), len(common), functools.partial(step_kernel, phase, last, choosing)),
            out_shape=tuple(outs),
            in_specs=[ANY] * 6 + [HBM] * 2 + [VMEM] * 4,
            out_specs=tuple(places),
            scratch_shapes=common + scratch,
            compiler_params=params,
            cost_estimate=pl.CostEstimate(
                flops=2 * products * conds,
                bytes_accessed=2 * products,
                transcendentals=blocks * conds * units,
            ),
        )(*ins)
        activity = got[0]
        if not last:
            spread, recent = got[1:3]
        if choosing:
            chosen = got[3]
    return activity[None]


def solution(mesh):
    placed = (
        P(None, "area", "pop", None, None),
        P("area", "pop", None, None),
        P("area", "pop", None),
        P("area", "pop", None),
        P("area", "pop", None, None, None),
        P("area", "pop", None),
        P("area", "pop", None, None, None),
        P(),
        P(),
        P(),
    )
    return jax.shard_map(
        shards, mesh=mesh, in_specs=placed, out_specs=P("area", "pop", None, None), check_vma=False
    )
```

time: 312 us -> 302 us (0.968)
  Pallas kernels: 64.6 us -> 56.2 us
    pallas_call x11, Pallas kernels: 64.6 us -> 56.2 us  [the longest x10 53.5 us: shards(): pl.pallas_call(ordered_kernel(len(ins), len(outs), len(common), functools...]
  transfers between devices with their start and end apart: 5 -> 5, of which waited for: 0 -> 0; matrix products, arithmetic and copies ran while one was open for 1% -> 0% of each run, Pallas kernels for 0% -> 0%
where the time goes in v4:
time: 302 us; the launch traced here: 301 us
  blocking collectives  203 us (67%)
  Pallas kernels  56.2 us (19%)
  starting transfers between devices  35.4 us (12%)
  local copies, waits for them, and re-layouts  5.19 us (2%)
    all_to_all x5, blocking collectives, exchange(): return lax.all_to_all(x, axis, split_axis=0, concat_axis=0, tiled=True)  90.9 us
    all_gather x5, blocking collectives, gather(): x = lax.all_gather(x, 'pop', axis=0, axis_index_groups=strided, tiled=True)  77.2 us
    pallas_call x10, Pallas kernels, shards(): pl.pallas_call(ordered_kernel(len(ins), len(outs), len(common), functools...  53.5 us
    all_to_all x5, starting transfers between devices, exchange(): return lax.all_to_all(x, axis, split_axis=0, concat_axis=0, tiled=True)  35.4 us
    all_gather x5, blocking collectives, gather(): lax.all_gather(x, 'pop', axis=0, axis_index_groups=paired, tiled=True)  35.2 us
  transfers between devices with their start and end apart: 5, of which 0 were waited for; matrix products, arithmetic and copies ran while one was open for 0% of the time, Pallas kernels for 0%

profile of v4, /device:TPU:4, one launch (start us, length us, event | category | flops | bytes accessed | tf_op | source)
XLA Modules:
  0.0 300.9 jit_solution(427497214003859787)
XLA Ops:
  0.0 0.7 select_reduce_fusion
  0.7 0.0 copy-start
  0.8 0.9 copy-done
  1.7 0.0 copy-start.1
  1.7 0.8 copy-done.1
  2.5 0.0 copy-start.2
  2.5 0.7 copy-done.2
  3.2 0.0 copy-start.3
  3.2 0.7 copy-done.3
  3.9 0.0 copy-start.4
  3.9 0.7 copy-done.4
  4.6 0.0 copy-start.5
  4.6 0.7 copy-done.5
  5.3 0.0 copy-start.6
  5.3 0.7 copy-done.6
  5.9 2.6 shard_map.100
  8.6 7.6 %all-to-all-start = ((bf16[32,4,32,128]{3,2,1,0:T(8,128)(2,1)}), bf16[32,4,32,128]{3,2,1,0:T(8,128)(2,1)S(1)}, u32[]{:S(2)}, u32[]{:S(2)}) async-start(bf16[32,4,32,128]{3,2,1,0:T(8,128)(2,1)} %get-tuple-element.51), calls=%async_computation | async-start | bytes 2097152 | tf_op jit(solution)/shard_map/all_to_all | solution.py:233
  16.2 17.7 %all_gather.30 = bf16[4,8,32,128]{3,2,1,0:T(8,128)(2,1)S(1)} all-gather(bf16[1,8,32,128]{3,2,1,0:T(8,128)(2,1)S(1)} %get-tuple-element.50), channel_id=1, replica_groups={{0,2,4,6},{1,3,5,7},{8,10,12,14},{9,11,13,15},{16,18,20,22},{17,19,21,2..., dimensions={0}, use_global_device_ids=true | all-gather | bytes 327680 | tf_op jit(solution)/shard_map/all_gather | solution.py:239
  33.9 7.0 %all_gather.31 = bf16[8,8,32,128]{3,2,1,0:T(8,128)(2,1)S(1)} all-gather(bf16[4,8,32,128]{3,2,1,0:T(8,128)(2,1)S(1)} %all_gather.30), channel_id=1, replica_groups={{0,1},{2,3},{4,5},{6,7},{8,9},{10,11},{12,13},{14,15},{16,17},{18,19},{..., dimensions={0}, use_global_device_ids=true | all-gather | bytes 786432 | tf_op jit(solution)/shard_map/all_gather | solution.py:240
  40.9 0.0 all-to-all-done.refs_5_
  40.9 5.3 %shard_map.101 = (f32[8,32,128]{2,1,0:T(8,128)S(1)}, bf16[8,8,32,128]{3,2,1,0:T(8,128)(2,1)S(1)}, bf16[3,2,32,128]{3,2,1,0:T(8,128)(2,1)S(1)}) custom-call(s32[13]{0:T(128)S(1)} %get-tuple-element.46.refs_0_, s32[32]{0:T(128)S(1)} %broadcast_maximum_fusion.delay_ref.refs_1_, s32[8,12]{1,0:T(8,128)S(1)} %get-tuple-element.47.refs_2_, ...), custom_call_target="tpu_custom_call" | custom-call | flops 369098752 | bytes 11534336 | tf_op jit(solution)/shard_map/pallas_call | solution.py:281
  46.2 19.7 %all_to_all.50 = bf16[8,8,32,128]{3,2,1,0:T(8,128)(2,1)S(1)} all-to-all(bf16[8,8,32,128]{3,2,1,0:T(8,128)(2,1)S(1)} %get-tuple-element.56), channel_id=1, replica_groups=mesh['area'=32,'pop'=8] {'pop'}, dimensions={0} | all-to-all | bytes 1048576 | tf_op jit(solution)/shard_map/all_to_all | solution.py:233
  65.9 5.3 %shard_map.102 = (f32[8,32,128]{2,1,0:T(8,128)S(1)}, bf16[1,8,32,128]{3,2,1,0:T(8,128)(2,1)S(1)}, bf16[3,2,32,128]{3,2,1,0:T(8,128)(2,1)S(1)}, bf16[32,4,32,128]{3,2,1,0:T(8,128)(2,1)}) custom-call(s32[13]{0:T(128)S(1)} %get-tuple-element.46.refs_0_, s32[32]{0:T(128)S(1)} %broadcast_maximum_fusion.delay_ref.refs_1_, s32[8,12]{1,0:T(8,128)S(1)} %get-tuple-element.47.refs_2_, ...), custom_call_target="tpu_custom_call" | custom-call | flops 369098752 | bytes 11534336 | tf_op jit(solution)/shard_map/pallas_call | solution.py:281
  71.2 6.7 %all-to-all-start.2 = ((bf16[32,4,32,128]{3,2,1,0:T(8,128)(2,1)}), bf16[32,4,32,128]{3,2,1,0:T(8,128)(2,1)S(1)}, u32[]{:S(2)}, u32[]{:S(2)}) async-start(bf16[32,4,32,128]{3,2,1,0:T(8,128)(2,1)} %get-tuple-element.60), calls=%async_computation.2 | async-start | bytes 2097152 | tf_op jit(solution)/shard_map/all_to_all | solution.py:233
  78.0 14.9 %all_gather.32 = bf16[4,8,32,128]{3,2,1,0:T(8,128)(2,1)S(1)} all-gather(bf16[1,8,32,128]{3,2,1,0:T(8,128)(2,1)S(1)} %get-tuple-element.59), channel_id=1, replica_groups={{0,2,4,6},{1,3,5,7},{8,10,12,14},{9,11,13,15},{16,18,20,22},{17,19,21,2..., dimensions={0}, use_global_device_ids=true | all-gather | bytes 327680 | tf_op jit(solution)/shard_map/all_gather | solution.py:239
  92.9 7.0 %all_gather.33 = bf16[8,8,32,128]{3,2,1,0:T(8,128)(2,1)S(1)} all-gather(bf16[4,8,32,128]{3,2,1,0:T(8,128)(2,1)S(1)} %all_gather.32), channel_id=1, replica_groups={{0,1},{2,3},{4,5},{6,7},{8,9},{10,11},{12,13},{14,15},{16,17},{18,19},{..., dimensions={0}, use_global_device_ids=true | all-gather | bytes 786432 | tf_op jit(solution)/shard_map/all_gather | solution.py:240
  99.9 0.0 all-to-all-done.2.refs_5_
  99.9 5.3 %shard_map.103 = (f32[8,32,128]{2,1,0:T(8,128)S(1)}, bf16[8,8,32,128]{3,2,1,0:T(8,128)(2,1)S(1)}, bf16[3,2,32,128]{3,2,1,0:T(8,128)(2,1)S(1)}) custom-call(s32[13]{0:T(128)S(1)} %get-tuple-element.46.refs_0_, s32[32]{0:T(128)S(1)} %broadcast_maximum_fusion.delay_ref.refs_1_, s32[8,12]{1,0:T(8,128)S(1)} %get-tuple-element.47.refs_2_, ...), custom_call_target="tpu_custom_call" | custom-call | flops 369098752 | bytes 11534336 | tf_op jit(solution)/shard_map/pallas_call | solution.py:281
  105.2 17.7 %all_to_all.51 = bf16[8,8,32,128]{3,2,1,0:T(8,128)(2,1)S(1)} all-to-all(bf16[8,8,32,128]{3,2,1,0:T(8,128)(2,1)S(1)} %get-tuple-element.63), channel_id=1, replica_groups=mesh['area'=32,'pop'=8] {'pop'}, dimensions={0} | all-to-all | bytes 1048576 | tf_op jit(solution)/shard_map/all_to_all | solution.py:233
  123.0 5.3 %shard_map.104 = (f32[8,32,128]{2,1,0:T(8,128)S(1)}, bf16[1,8,32,128]{3,2,1,0:T(8,128)(2,1)S(1)}, bf16[3,2,32,128]{3,2,1,0:T(8,128)(2,1)S(1)}, bf16[32,4,32,128]{3,2,1,0:T(8,128)(2,1)}) custom-call(s32[13]{0:T(128)S(1)} %get-tuple-element.46.refs_0_, s32[32]{0:T(128)S(1)} %broadcast_maximum_fusion.delay_ref.refs_1_, s32[8,12]{1,0:T(8,128)S(1)} %get-tuple-element.47.refs_2_, ...), custom_call_target="tpu_custom_call" | custom-call | flops 369098752 | bytes 11534336 | tf_op jit(solution)/shard_map/pallas_call | solution.py:281
  128.3 7.0 %all-to-all-start.4 = ((bf16[32,4,32,128]{3,2,1,0:T(8,128)(2,1)}), bf16[32,4,32,128]{3,2,1,0:T(8,128)(2,1)S(1)}, u32[]{:S(2)}, u32[]{:S(2)}) async-start(bf16[32,4,32,128]{3,2,1,0:T(8,128)(2,1)} %get-tuple-element.67), calls=%async_computation.4 | async-start | bytes 2097152 | tf_op jit(solution)/shard_map/all_to_all | solution.py:233
  135.3 14.9 %all_gather.34 = bf16[4,8,32,128]{3,2,1,0:T(8,128)(2,1)S(1)} all-gather(bf16[1,8,32,128]{3,2,1,0:T(8,128)(2,1)S(1)} %get-tuple-element.66), channel_id=1, replica_groups={{0,2,4,6},{1,3,5,7},{8,10,12,14},{9,11,13,15},{16,18,20,22},{17,19,21,2..., dimensions={0}, use_global_device_ids=true | all-gather | bytes 327680 | tf_op jit(solution)/shard_map/all_gather | solution.py:239
  150.2 7.0 %all_gather.35 = bf16[8,8,32,128]{3,2,1,0:T(8,128)(2,1)S(1)} all-gather(bf16[4,8,32,128]{3,2,1,0:T(8,128)(2,1)S(1)} %all_gather.34), channel_id=1, replica_groups={{0,1},{2,3},{4,5},{6,7},{8,9},{10,11},{12,13},{14,15},{16,17},{18,19},{..., dimensions={0}, use_global_device_ids=true | all-gather | bytes 786432 | tf_op jit(solution)/shard_map/all_gather | solution.py:240
  157.2 0.0 all-to-all-done.4.refs_5_
  157.2 5.3 %shard_map.105 = (f32[8,32,128]{2,1,0:T(8,128)S(1)}, bf16[8,8,32,128]{3,2,1,0:T(8,128)(2,1)S(1)}, bf16[3,2,32,128]{3,2,1,0:T(8,128)(2,1)S(1)}) custom-call(s32[13]{0:T(128)S(1)} %get-tuple-element.46.refs_0_, s32[32]{0:T(128)S(1)} %broadcast_maximum_fusion.delay_ref.refs_1_, s32[8,12]{1,0:T(8,128)S(1)} %get-tuple-element.47.refs_2_, ...), custom_call_target="tpu_custom_call" | custom-call | flops 369098752 | bytes 11534336 | tf_op jit(solution)/shard_map/pallas_call | solution.py:281
  162.5 17.8 %all_to_all.52 = bf16[8,8,32,128]{3,2,1,0:T(8,128)(2,1)S(1)} all-to-all(bf16[8,8,32,128]{3,2,1,0:T(8,128)(2,1)S(1)} %get-tuple-element.70), channel_id=1, replica_groups=mesh['area'=32,'pop'=8] {'pop'}, dimensions={0} | all-to-all | bytes 1048576 | tf_op jit(solution)/shard_map/all_to_all | solution.py:233
  180.3 5.3 %shard_map.106 = (f32[8,32,128]{2,1,0:T(8,128)S(1)}, bf16[1,8,32,128]{3,2,1,0:T(8,128)(2,1)S(1)}, bf16[3,2,32,128]{3,2,1,0:T(8,128)(2,1)S(1)}, bf16[32,4,32,128]{3,2,1,0:T(8,128)(2,1)}) custom-call(s32[13]{0:T(128)S(1)} %get-tuple-element.46.refs_0_, s32[32]{0:T(128)S(1)} %broadcast_maximum_fusion.delay_ref.refs_1_, s32[8,12]{1,0:T(8,128)S(1)} %get-tuple-element.47.refs_2_, ...), custom_call_target="tpu_custom_call" | custom-call | flops 369098752 | bytes 11534336 | tf_op jit(solution)/shard_map/pallas_call | solution.py:281
  185.6 7.0 %all-to-all-start.6 = ((bf16[32,4,32,128]{3,2,1,0:T(8,128)(2,1)}), bf16[32,4,32,128]{3,2,1,0:T(8,128)(2,1)S(1)}, u32[]{:S(2)}, u32[]{:S(2)}) async-start(bf16[32,4,32,128]{3,2,1,0:T(8,128)(2,1)} %get-tuple-element.74), calls=%async_computation.6 | async-start | bytes 2097152 | tf_op jit(solution)/shard_map/all_to_all | solution.py:233
  192.7 14.9 %all_gather.36 = bf16[4,8,32,128]{3,2,1,0:T(8,128)(2,1)S(1)} all-gather(bf16[1,8,32,128]{3,2,1,0:T(8,128)(2,1)S(1)} %get-tuple-element.73), channel_id=1, replica_groups={{0,2,4,6},{1,3,5,7},{8,10,12,14},{9,11,13,15},{16,18,20,22},{17,19,21,2..., dimensions={0}, use_global_device_ids=true | all-gather | bytes 327680 | tf_op jit(solution)/shard_map/all_gather | solution.py:239
  207.5 7.0 %all_gather.37 = bf16[8,8,32,128]{3,2,1,0:T(8,128)(2,1)S(1)} all-gather(bf16[4,8,32,128]{3,2,1,0:T(8,128)(2,1)S(1)} %all_gather.36), channel_id=1, replica_groups={{0,1},{2,3},{4,5},{6,7},{8,9},{10,11},{12,13},{14,15},{16,17},{18,19},{..., dimensions={0}, use_global_device_ids=true | all-gather | bytes 786432 | tf_op jit(solution)/shard_map/all_gather | solution.py:240
  214.6 0.0 all-to-all-done.6.refs_5_
  214.6 5.3 %shard_map.107 = (f32[8,32,128]{2,1,0:T(8,128)S(1)}, bf16[8,8,32,128]{3,2,1,0:T(8,128)(2,1)S(1)}, bf16[3,2,32,128]{3,2,1,0:T(8,128)(2,1)S(1)}) custom-call(s32[13]{0:T(128)S(1)} %get-tuple-element.46.refs_0_, s32[32]{0:T(128)S(1)} %broadcast_maximum_fusion.delay_ref.refs_1_, s32[8,12]{1,0:T(8,128)S(1)} %get-tuple-element.47.refs_2_, ...), custom_call_target="tpu_custom_call" | custom-call | flops 369098752 | bytes 11534336 | tf_op jit(solution)/shard_map/pallas_call | solution.py:281
  219.8 17.8 %all_to_all.53 = bf16[8,8,32,128]{3,2,1,0:T(8,128)(2,1)S(1)} all-to-all(bf16[8,8,32,128]{3,2,1,0:T(8,128)(2,1)S(1)} %get-tuple-element.77), channel_id=1, replica_groups=mesh['area'=32,'pop'=8] {'pop'}, dimensions={0} | all-to-all | bytes 1048576 | tf_op jit(solution)/shard_map/all_to_all | solution.py:233
  237.7 5.3 %shard_map.108 = (f32[8,32,128]{2,1,0:T(8,128)S(1)}, bf16[1,8,32,128]{3,2,1,0:T(8,128)(2,1)S(1)}, bf16[3,2,32,128]{3,2,1,0:T(8,128)(2,1)S(1)}, bf16[32,4,32,128]{3,2,1,0:T(8,128)(2,1)}) custom-call(s32[13]{0:T(128)S(1)} %get-tuple-element.46.refs_0_, s32[32]{0:T(128)S(1)} %broadcast_maximum_fusion.delay_ref.refs_1_, s32[8,12]{1,0:T(8,128)S(1)} %get-tuple-element.47.refs_2_, ...), custom_call_target="tpu_custom_call" | custom-call | flops 369098752 | bytes 11534336 | tf_op jit(solution)/shard_map/pallas_call | solution.py:281
  243.0 7.0 %all-to-all-start.8 = ((bf16[32,4,32,128]{3,2,1,0:T(8,128)(2,1)}), bf16[32,4,32,128]{3,2,1,0:T(8,128)(2,1)S(1)}, u32[]{:S(2)}, u32[]{:S(2)}) async-start(bf16[32,4,32,128]{3,2,1,0:T(8,128)(2,1)} %get-tuple-element.81), calls=%async_computation.8 | async-start | bytes 2097152 | tf_op jit(solution)/shard_map/all_to_all | solution.py:233
  250.0 14.9 %all_gather.38 = bf16[4,8,32,128]{3,2,1,0:T(8,128)(2,1)S(1)} all-gather(bf16[1,8,32,128]{3,2,1,0:T(8,128)(2,1)S(1)} %get-tuple-element.80), channel_id=1, replica_groups={{0,2,4,6},{1,3,5,7},{8,10,12,14},{9,11,13,15},{16,18,20,22},{17,19,21,2..., dimensions={0}, use_global_device_ids=true | all-gather | bytes 327680 | tf_op jit(solution)/shard_map/all_gather | solution.py:239
  264.9 7.0 %all_gather.39 = bf16[8,8,32,128]{3,2,1,0:T(8,128)(2,1)S(1)} all-gather(bf16[4,8,32,128]{3,2,1,0:T(8,128)(2,1)S(1)} %all_gather.38), channel_id=1, replica_groups={{0,1},{2,3},{4,5},{6,7},{8,9},{10,11},{12,13},{14,15},{16,17},{18,19},{..., dimensions={0}, use_global_device_ids=true | all-gather | bytes 786432 | tf_op jit(solution)/shard_map/all_gather | solution.py:240
  272.0 0.0 all-to-all-done.8.refs_5_
  272.0 5.3 %shard_map.109 = (f32[8,32,128]{2,1,0:T(8,128)S(1)}, bf16[8,8,32,128]{3,2,1,0:T(8,128)(2,1)S(1)}, bf16[3,2,32,128]{3,2,1,0:T(8,128)(2,1)S(1)}) custom-call(s32[13]{0:T(128)S(1)} %get-tuple-element.46.refs_0_, s32[32]{0:T(128)S(1)} %broadcast_maximum_fusion.delay_ref.refs_1_, s32[8,12]{1,0:T(8,128)S(1)} %get-tuple-element.47.refs_2_, ...), custom_call_target="tpu_custom_call" | custom-call | flops 369098752 | bytes 11534336 | tf_op jit(solution)/shard_map/pallas_call | solution.py:281
  277.2 17.8 %all_to_all.54 = bf16[8,8,32,128]{3,2,1,0:T(8,128)(2,1)S(1)} all-to-all(bf16[8,8,32,128]{3,2,1,0:T(8,128)(2,1)S(1)} %get-tuple-element.84), channel_id=1, replica_groups=mesh['area'=32,'pop'=8] {'pop'}, dimensions={0} | all-to-all | bytes 1048576 | tf_op jit(solution)/shard_map/all_to_all | solution.py:233
  295.0 5.9 %shard_map.110 = f32[8,32,128]{2,1,0:T(8,128)} custom-call(s32[13]{0:T(128)S(1)} %get-tuple-element.46.refs_0_, s32[32]{0:T(128)S(1)} %broadcast_maximum_fusion.delay_ref.refs_1_, s32[8,12]{1,0:T(8,128)S(1)} %get-tuple-element.47.refs_2_, s32[8,32]{1,0:T(8,128)S(1)} %get-tuple-element.48.refs_3_, bf16[64,32,128]{2,1,0:T(8,128)(2,1)S(1)} %bitcast.24, ...), custom_call_target="tpu_custom_call" | custom-call | flops 369098752 | bytes 11534336 | tf_op jit(solution)/shard_map/pallas_call | solution.py:281
  (1 shorter events, 0.0 us)
Async XLA Ops:
  0.7 1.0 copy-start
  1.7 0.8 copy-start.1
  2.5 0.7 copy-start.2
  3.2 0.7 copy-start.3
  3.9 0.7 copy-start.4
  4.6 0.7 copy-start.5
  5.3 0.7 copy-start.6
  8.6 32.3 %all-to-all-start = ((bf16[32,4,32,128]{3,2,1,0:T(8,128)(2,1)}), bf16[32,4,32,128]{3,2,1,0:T(8,128)(2,1)S(1)}, u32[]{:S(2)}, u32[]{:S(2)}) async-start(bf16[32,4,32,128]{3,2,1,0:T(8,128)(2,1)} %get-tuple-element.51), calls=%async_computation | async-start | bytes 2097152 | tf_op jit(solution)/shard_map/all_to_all | solution.py:233
  71.2 28.7 %all-to-all-start.2 = ((bf16[32,4,32,128]{3,2,1,0:T(8,128)(2,1)}), bf16[32,4,32,128]{3,2,1,0:T(8,128)(2,1)S(1)}, u32[]{:S(2)}, u32[]{:S(2)}) async-start(bf16[32,4,32,128]{3,2,1,0:T(8,128)(2,1)} %get-tuple-element.60), calls=%async_computation.2 | async-start | bytes 2097152 | tf_op jit(solution)/shard_map/all_to_all | solution.py:233
  128.3 28.9 %all-to-all-start.4 = ((bf16[32,4,32,128]{3,2,1,0:T(8,128)(2,1)}), bf16[32,4,32,128]{3,2,1,0:T(8,128)(2,1)S(1)}, u32[]{:S(2)}, u32[]{:S(2)}) async-start(bf16[32,4,32,128]{3,2,1,0:T(8,128)(2,1)} %get-tuple-element.67), calls=%async_computation.4 | async-start | bytes 2097152 | tf_op jit(solution)/shard_map/all_to_all | solution.py:233
  185.6 29.0 %all-to-all-start.6 = ((bf16[32,4,32,128]{3,2,1,0:T(8,128)(2,1)}), bf16[32,4,32,128]{3,2,1,0:T(8,128)(2,1)S(1)}, u32[]{:S(2)}, u32[]{:S(2)}) async-start(bf16[32,4,32,128]{3,2,1,0:T(8,128)(2,1)} %get-tuple-element.74), calls=%async_computation.6 | async-start | bytes 2097152 | tf_op jit(solution)/shard_map/all_to_all | solution.py:233
  243.0 29.0 %all-to-all-start.8 = ((bf16[32,4,32,128]{3,2,1,0:T(8,128)(2,1)}), bf16[32,4,32,128]{3,2,1,0:T(8,128)(2,1)S(1)}, u32[]{:S(2)}, u32[]{:S(2)}) async-start(bf16[32,4,32,128]{3,2,1,0:T(8,128)(2,1)} %get-tuple-element.81), calls=%async_computation.8 | async-start | bytes 2097152 | tf_op jit(solution)/shard_map/all_to_all | solution.py:233

commit v5 on v4

--- a/solution.py
+++ b/solution.py
@@ -9,6 +9,7 @@
 SEND_DEV = 2
 STEPS = 10
 DMAX = 3
+KEPT = 3
 SPAN = 2
 
 VMEM = pl.BlockSpec(memory_space=pltpu.VMEM)
@@ -82,7 +83,7 @@
 def step_kernel(
     phase, last, choosing,
     table_any, delay_any, pick_any, index_any,
-    rates_any, received_any, intra_hbm, inter_hbm, external_ref, leak_ref, activity_ref, recent_ref,
+    rates_any, received_any, intra_hbm, inter_hbm, kept_ref, external_ref, leak_ref, activity_ref, recent_ref,
     *refs,
 ):
     table_ref, delay_ref, pick_ref, index_ref, table_sem, rates_ref, received_ref, intra_ref, inter_ref = refs[:9]
@@ -95,6 +96,7 @@
         chosen_hbm, older_ref, chosen_ref, chosen_sem = outs
     blocks, tiles = intra_ref.shape[:2]
     edges = inter_ref.shape[1]
+    kept = kept_ref.shape[0]
 
     def received_copy(e):
         return pltpu.make_async_copy(
@@ -105,7 +107,7 @@
         return pltpu.make_async_copy(intra_hbm.at[block], intra_ref.at[block], intra_sem.at[block])
 
     def inter_copy(block):
-        return pltpu.make_async_copy(inter_hbm.at[block], inter_ref.at[block], inter_sem.at[block])
+        return pltpu.make_async_copy(inter_hbm.at[block], inter_ref.at[block - kept], inter_sem.at[block - kept])
 
     tables = [(table_any, table_ref), (pick_any, pick_ref), (index_any, index_ref)]
     if choosing:
@@ -114,7 +116,7 @@
     rates_copy = pltpu.make_async_copy(rates_any, rates_ref, rates_sem)
     for copy in table_copies:
         copy.start()
-    for block in range(blocks):
+    for block in range(kept, blocks):
         inter_copy(block).start()
     rates_copy.start()
     for block in range(blocks):
@@ -128,16 +130,18 @@
     for e in range(edges):
         received_copy(e).wait()
 
-    def outer_body(block, carry):
+    def outer(block, weights):
+        rows = [received_ref[e, pick_ref[block, e]] for e in range(edges)]
+        outer_ref[block] = tile_product(rows, weights) + external_ref[block].astype(jnp.float32)
+
+    for block in range(kept):
+        outer(block, kept_ref[block])
+    for block in range(kept, blocks):
         inter_copy(block).wait()
-        rows = [received_ref[e, pick_ref[block, e]] for e in range(edges)]
-        outer_ref[block] = tile_product(rows, inter_ref[block]) + external_ref[block].astype(jnp.float32)
-        return carry
-
-    lax.fori_loop(0, blocks, outer_body, 0)
+        outer(block, inter_ref[block - kept])
     rates_copy.wait()
 
-    def body(block, carry):
+    def advance(block):
         intra_copy(block).wait()
         rows = [rates_ref[index_ref[block, k]] for k in range(tiles)]
         current = tile_product(rows, intra_ref[block]) + outer_ref[block]
@@ -149,9 +153,9 @@
             rates = new.astype(jnp.bfloat16)
             for pop in range(spread_ref.shape[0]):
                 spread_ref[pop, block] = rates
-        return carry
-
-    lax.fori_loop(0, SEND_DEV, body, 0)
+
+    for block in range(SEND_DEV):
+        advance(block)
     if choosing:
         older_ref[0] = spread_ref[0, :SEND_DEV]
         for age in range(DMAX):
@@ -159,7 +163,8 @@
         choose(delay_ref, older_ref, chosen_ref)
         chosen_copy = pltpu.make_async_copy(chosen_ref, chosen_hbm, chosen_sem)
         chosen_copy.start()
-    lax.fori_loop(SEND_DEV, blocks, body, 0)
+    for block in range(SEND_DEV, blocks):
+        advance(block)
     if not last:
         recent_out_ref[0] = spread_ref[0, :SEND_DEV]
         for age in range(1, DMAX):
@@ -204,7 +209,7 @@
     older = pltpu.VMEM((DMAX + 1, SEND_DEV, conds, units), bf16)
     chosen_scratch = pltpu.VMEM(chosen_t.shape, bf16)
     one = pltpu.SemaphoreType.DMA
-    params = pltpu.CompilerParams(vmem_limit_bytes=50 * 2**20)
+    params = pltpu.CompilerParams(vmem_limit_bytes=49 * 2**20)
 
     area_pos = lax.axis_index("area")
     delay_to = jnp.sum(jnp.where(source_area == area_pos, delays, 0), axis=1)
@@ -248,12 +253,12 @@
         pltpu.VMEM((pops * blocks, conds, units), bf16),
         pltpu.VMEM((edges, SEND_DEV, conds, units), bf16),
         pltpu.VMEM((blocks, tiles, units, units), bf16),
-        pltpu.VMEM((blocks, edges, units, units), bf16),
+        pltpu.VMEM((blocks - KEPT, edges, units, units), bf16),
         pltpu.VMEM((blocks, conds, units), f32),
         one,
         pltpu.SemaphoreType.DMA((edges,)),
         pltpu.SemaphoreType.DMA((blocks,)),
-        pltpu.SemaphoreType.DMA((blocks,)),
+        pltpu.SemaphoreType.DMA((blocks - KEPT,)),
     ]
     products = blocks * (tiles + edges) * units * units
     for step in range(STEPS):
@@ -275,13 +280,13 @@
             scratch += [older, chosen_scratch, one]
         ins = (
             table, delay_to, pick, index if phase else gathered_index,
-            rates.reshape(pops * blocks, conds, units), received, intra_weight[0], inter,
+            rates.reshape(pops * blocks, conds, units), received, intra_weight[0], inter, inter[:KEPT],
             external, leak, activity, recent,
         )
         got = pl.pallas_call(
             ordered_kernel(len(ins), len(outs), len(common), functools.partial(step_kernel, phase, last, choosing)),
             out_shape=tuple(outs),
-            in_specs=[ANY] * 6 + [HBM] * 2 + [VMEM] * 4,
+            in_specs=[ANY] * 6 + [HBM] * 2 + [VMEM] * 5,
             out_specs=tuple(places),
             scratch_shapes=common + scratch,
             compiler_params=params,

time: 302 us -> 300 us (level)
  Pallas kernels: 56.2 us -> 52.8 us
    pallas_call x10, Pallas kernels: 53.5 us -> 50.2 us  [shards(): pl.pallas_call(ordered_kernel(len(ins), len(outs), len(common), functools...]
where the time goes in v5:
time: 300 us; the launch traced here: 299 us
  blocking collectives  203 us (68%)
  Pallas kernels  52.8 us (18%)
  starting transfers between devices  35.4 us (12%)
  local copies, waits for them, and re-layouts  6.54 us (2%)
    all_to_all x5, blocking collectives, exchange(): return lax.all_to_all(x, axis, split_axis=0, concat_axis=0, tiled=True)  90.7 us
    all_gather x5, blocking collectives, gather(): x = lax.all_gather(x, 'pop', axis=0, axis_index_groups=strided, tiled=True)  77.2 us
    pallas_call x10, Pallas kernels, shards(): pl.pallas_call(ordered_kernel(len(ins), len(outs), len(common), functools...  50.2 us
    all_to_all x5, starting transfers between devices, exchange(): return lax.all_to_all(x, axis, split_axis=0, concat_axis=0, tiled=True)  35.4 us
    all_gather x5, blocking collectives, gather(): lax.all_gather(x, 'pop', axis=0, axis_index_groups=paired, tiled=True)  35.2 us
  transfers between devices with their start and end apart: 5, of which 0 were waited for; matrix products, arithmetic and copies ran while one was open for 0% of the time, Pallas kernels for 0%

profile of v5, /device:TPU:4, one launch (start us, length us, event | category | flops | bytes accessed | tf_op | source)
XLA Modules:
  0.0 299.0 jit_solution(7772119247973993845)
XLA Ops:
  0.0 0.7 select_reduce_fusion
  0.7 0.0 copy-start
  0.8 0.9 copy-done
  1.7 0.0 copy-start.1
  1.7 0.8 copy-done.1
  2.5 0.0 copy-start.2
  2.5 0.7 copy-done.2
  3.2 0.0 copy-start.3
  3.2 0.7 copy-done.3
  3.9 0.0 copy-start.4
  3.9 0.7 copy-done.4
  4.6 0.0 copy-start.5
  4.6 0.7 copy-done.5
  5.3 0.0 copy-start.6
  5.3 0.7 copy-done.6
  5.9 2.6 shard_map.100
  8.6 7.6 %all-to-all-start = ((bf16[32,4,32,128]{3,2,1,0:T(8,128)(2,1)}), bf16[32,4,32,128]{3,2,1,0:T(8,128)(2,1)S(1)}, u32[]{:S(2)}, u32[]{:S(2)}) async-start(bf16[32,4,32,128]{3,2,1,0:T(8,128)(2,1)} %get-tuple-element.51), calls=%async_computation | async-start | bytes 2097152 | tf_op jit(solution)/shard_map/all_to_all | solution.py:238
  16.2 17.7 %all_gather.30 = bf16[4,8,32,128]{3,2,1,0:T(8,128)(2,1)S(1)} all-gather(bf16[1,8,32,128]{3,2,1,0:T(8,128)(2,1)S(1)} %get-tuple-element.50), channel_id=1, replica_groups={{0,2,4,6},{1,3,5,7},{8,10,12,14},{9,11,13,15},{16,18,20,22},{17,19,21,2..., dimensions={0}, use_global_device_ids=true | all-gather | bytes 327680 | tf_op jit(solution)/shard_map/all_gather | solution.py:244
  33.9 7.0 %all_gather.31 = bf16[8,8,32,128]{3,2,1,0:T(8,128)(2,1)S(1)} all-gather(bf16[4,8,32,128]{3,2,1,0:T(8,128)(2,1)S(1)} %all_gather.30), channel_id=1, replica_groups={{0,1},{2,3},{4,5},{6,7},{8,9},{10,11},{12,13},{14,15},{16,17},{18,19},{..., dimensions={0}, use_global_device_ids=true | all-gather | bytes 786432 | tf_op jit(solution)/shard_map/all_gather | solution.py:245
  40.9 1.3 slice_bitcast_fusion.refs_8_
  42.3 0.0 all-to-all-done.refs_5_
  42.3 4.9 %shard_map.101 = (f32[8,32,128]{2,1,0:T(8,128)S(1)}, bf16[8,8,32,128]{3,2,1,0:T(8,128)(2,1)S(1)}, bf16[3,2,32,128]{3,2,1,0:T(8,128)(2,1)S(1)}) custom-call(s32[13]{0:T(128)S(1)} %get-tuple-element.46.refs_0_, s32[32]{0:T(128)S(1)} %broadcast_maximum_fusion.delay_ref.refs_1_, s32[8,12]{1,0:T(8,128)S(1)} %get-tuple-element.47.refs_2_, ...), custom_call_target="tpu_custom_call" | custom-call | flops 369098752 | bytes 11534336 | tf_op jit(solution)/shard_map/pallas_call | solution.py:286
  47.2 19.7 %all_to_all.50 = bf16[8,8,32,128]{3,2,1,0:T(8,128)(2,1)S(1)} all-to-all(bf16[8,8,32,128]{3,2,1,0:T(8,128)(2,1)S(1)} %get-tuple-element.56), channel_id=1, replica_groups=mesh['area'=32,'pop'=8] {'pop'}, dimensions={0} | all-to-all | bytes 1048576 | tf_op jit(solution)/shard_map/all_to_all | solution.py:238
  66.9 5.0 %shard_map.102 = (f32[8,32,128]{2,1,0:T(8,128)S(1)}, bf16[1,8,32,128]{3,2,1,0:T(8,128)(2,1)S(1)}, bf16[3,2,32,128]{3,2,1,0:T(8,128)(2,1)S(1)}, bf16[32,4,32,128]{3,2,1,0:T(8,128)(2,1)}) custom-call(s32[13]{0:T(128)S(1)} %get-tuple-element.46.refs_0_, s32[32]{0:T(128)S(1)} %broadcast_maximum_fusion.delay_ref.refs_1_, s32[8,12]{1,0:T(8,128)S(1)} %get-tuple-element.47.refs_2_, ...), custom_call_target="tpu_custom_call" | custom-call | flops 369098752 | bytes 11534336 | tf_op jit(solution)/shard_map/pallas_call | solution.py:286
  71.9 6.7 %all-to-all-start.2 = ((bf16[32,4,32,128]{3,2,1,0:T(8,128)(2,1)}), bf16[32,4,32,128]{3,2,1,0:T(8,128)(2,1)S(1)}, u32[]{:S(2)}, u32[]{:S(2)}) async-start(bf16[32,4,32,128]{3,2,1,0:T(8,128)(2,1)} %get-tuple-element.60), calls=%async_computation.2 | async-start | bytes 2097152 | tf_op jit(solution)/shard_map/all_to_all | solution.py:238
  78.7 14.8 %all_gather.32 = bf16[4,8,32,128]{3,2,1,0:T(8,128)(2,1)S(1)} all-gather(bf16[1,8,32,128]{3,2,1,0:T(8,128)(2,1)S(1)} %get-tuple-element.59), channel_id=1, replica_groups={{0,2,4,6},{1,3,5,7},{8,10,12,14},{9,11,13,15},{16,18,20,22},{17,19,21,2..., dimensions={0}, use_global_device_ids=true | all-gather | bytes 327680 | tf_op jit(solution)/shard_map/all_gather | solution.py:244
  93.5 7.0 %all_gather.33 = bf16[8,8,32,128]{3,2,1,0:T(8,128)(2,1)S(1)} all-gather(bf16[4,8,32,128]{3,2,1,0:T(8,128)(2,1)S(1)} %all_gather.32), channel_id=1, replica_groups={{0,1},{2,3},{4,5},{6,7},{8,9},{10,11},{12,13},{14,15},{16,17},{18,19},{..., dimensions={0}, use_global_device_ids=true | all-gather | bytes 786432 | tf_op jit(solution)/shard_map/all_gather | solution.py:245
  100.5 0.0 all-to-all-done.2.refs_5_
  100.6 4.9 %shard_map.103 = (f32[8,32,128]{2,1,0:T(8,128)S(1)}, bf16[8,8,32,128]{3,2,1,0:T(8,128)(2,1)S(1)}, bf16[3,2,32,128]{3,2,1,0:T(8,128)(2,1)S(1)}) custom-call(s32[13]{0:T(128)S(1)} %get-tuple-element.46.refs_0_, s32[32]{0:T(128)S(1)} %broadcast_maximum_fusion.delay_ref.refs_1_, s32[8,12]{1,0:T(8,128)S(1)} %get-tuple-element.47.refs_2_, ...), custom_call_target="tpu_custom_call" | custom-call | flops 369098752 | bytes 11534336 | tf_op jit(solution)/shard_map/pallas_call | solution.py:286
  105.5 17.7 %all_to_all.51 = bf16[8,8,32,128]{3,2,1,0:T(8,128)(2,1)S(1)} all-to-all(bf16[8,8,32,128]{3,2,1,0:T(8,128)(2,1)S(1)} %get-tuple-element.63), channel_id=1, replica_groups=mesh['area'=32,'pop'=8] {'pop'}, dimensions={0} | all-to-all | bytes 1048576 | tf_op jit(solution)/shard_map/all_to_all | solution.py:238
  123.2 5.0 %shard_map.104 = (f32[8,32,128]{2,1,0:T(8,128)S(1)}, bf16[1,8,32,128]{3,2,1,0:T(8,128)(2,1)S(1)}, bf16[3,2,32,128]{3,2,1,0:T(8,128)(2,1)S(1)}, bf16[32,4,32,128]{3,2,1,0:T(8,128)(2,1)}) custom-call(s32[13]{0:T(128)S(1)} %get-tuple-element.46.refs_0_, s32[32]{0:T(128)S(1)} %broadcast_maximum_fusion.delay_ref.refs_1_, s32[8,12]{1,0:T(8,128)S(1)} %get-tuple-element.47.refs_2_, ...), custom_call_target="tpu_custom_call" | custom-call | flops 369098752 | bytes 11534336 | tf_op jit(solution)/shard_map/pallas_call | solution.py:286
  128.2 7.0 %all-to-all-start.4 = ((bf16[32,4,32,128]{3,2,1,0:T(8,128)(2,1)}), bf16[32,4,32,128]{3,2,1,0:T(8,128)(2,1)S(1)}, u32[]{:S(2)}, u32[]{:S(2)}) async-start(bf16[32,4,32,128]{3,2,1,0:T(8,128)(2,1)} %get-tuple-element.67), calls=%async_computation.4 | async-start | bytes 2097152 | tf_op jit(solution)/shard_map/all_to_all | solution.py:238
  135.2 14.8 %all_gather.34 = bf16[4,8,32,128]{3,2,1,0:T(8,128)(2,1)S(1)} all-gather(bf16[1,8,32,128]{3,2,1,0:T(8,128)(2,1)S(1)} %get-tuple-element.66), channel_id=1, replica_groups={{0,2,4,6},{1,3,5,7},{8,10,12,14},{9,11,13,15},{16,18,20,22},{17,19,21,2..., dimensions={0}, use_global_device_ids=true | all-gather | bytes 327680 | tf_op jit(solution)/shard_map/all_gather | solution.py:244
  150.1 7.0 %all_gather.35 = bf16[8,8,32,128]{3,2,1,0:T(8,128)(2,1)S(1)} all-gather(bf16[4,8,32,128]{3,2,1,0:T(8,128)(2,1)S(1)} %all_gather.34), channel_id=1, replica_groups={{0,1},{2,3},{4,5},{6,7},{8,9},{10,11},{12,13},{14,15},{16,17},{18,19},{..., dimensions={0}, use_global_device_ids=true | all-gather | bytes 786432 | tf_op jit(solution)/shard_map/all_gather | solution.py:245
  157.1 0.0 all-to-all-done.4.refs_5_
  157.1 4.9 %shard_map.105 = (f32[8,32,128]{2,1,0:T(8,128)S(1)}, bf16[8,8,32,128]{3,2,1,0:T(8,128)(2,1)S(1)}, bf16[3,2,32,128]{3,2,1,0:T(8,128)(2,1)S(1)}) custom-call(s32[13]{0:T(128)S(1)} %get-tuple-element.46.refs_0_, s32[32]{0:T(128)S(1)} %broadcast_maximum_fusion.delay_ref.refs_1_, s32[8,12]{1,0:T(8,128)S(1)} %get-tuple-element.47.refs_2_, ...), custom_call_target="tpu_custom_call" | custom-call | flops 369098752 | bytes 11534336 | tf_op jit(solution)/shard_map/pallas_call | solution.py:286
  162.0 17.9 %all_to_all.52 = bf16[8,8,32,128]{3,2,1,0:T(8,128)(2,1)S(1)} all-to-all(bf16[8,8,32,128]{3,2,1,0:T(8,128)(2,1)S(1)} %get-tuple-element.70), channel_id=1, replica_groups=mesh['area'=32,'pop'=8] {'pop'}, dimensions={0} | all-to-all | bytes 1048576 | tf_op jit(solution)/shard_map/all_to_all | solution.py:238
  179.9 5.0 %shard_map.106 = (f32[8,32,128]{2,1,0:T(8,128)S(1)}, bf16[1,8,32,128]{3,2,1,0:T(8,128)(2,1)S(1)}, bf16[3,2,32,128]{3,2,1,0:T(8,128)(2,1)S(1)}, bf16[32,4,32,128]{3,2,1,0:T(8,128)(2,1)}) custom-call(s32[13]{0:T(128)S(1)} %get-tuple-element.46.refs_0_, s32[32]{0:T(128)S(1)} %broadcast_maximum_fusion.delay_ref.refs_1_, s32[8,12]{1,0:T(8,128)S(1)} %get-tuple-element.47.refs_2_, ...), custom_call_target="tpu_custom_call" | custom-call | flops 369098752 | bytes 11534336 | tf_op jit(solution)/shard_map/pallas_call | solution.py:286
  184.9 7.1 %all-to-all-start.6 = ((bf16[32,4,32,128]{3,2,1,0:T(8,128)(2,1)}), bf16[32,4,32,128]{3,2,1,0:T(8,128)(2,1)S(1)}, u32[]{:S(2)}, u32[]{:S(2)}) async-start(bf16[32,4,32,128]{3,2,1,0:T(8,128)(2,1)} %get-tuple-element.74), calls=%async_computation.6 | async-start | bytes 2097152 | tf_op jit(solution)/shard_map/all_to_all | solution.py:238
  192.0 15.0 %all_gather.36 = bf16[4,8,32,128]{3,2,1,0:T(8,128)(2,1)S(1)} all-gather(bf16[1,8,32,128]{3,2,1,0:T(8,128)(2,1)S(1)} %get-tuple-element.73), channel_id=1, replica_groups={{0,2,4,6},{1,3,5,7},{8,10,12,14},{9,11,13,15},{16,18,20,22},{17,19,21,2..., dimensions={0}, use_global_device_ids=true | all-gather | bytes 327680 | tf_op jit(solution)/shard_map/all_gather | solution.py:244
  207.0 7.0 %all_gather.37 = bf16[8,8,32,128]{3,2,1,0:T(8,128)(2,1)S(1)} all-gather(bf16[4,8,32,128]{3,2,1,0:T(8,128)(2,1)S(1)} %all_gather.36), channel_id=1, replica_groups={{0,1},{2,3},{4,5},{6,7},{8,9},{10,11},{12,13},{14,15},{16,17},{18,19},{..., dimensions={0}, use_global_device_ids=true | all-gather | bytes 786432 | tf_op jit(solution)/shard_map/all_gather | solution.py:245
  214.0 0.0 all-to-all-done.6.refs_5_
  214.0 4.9 %shard_map.107 = (f32[8,32,128]{2,1,0:T(8,128)S(1)}, bf16[8,8,32,128]{3,2,1,0:T(8,128)(2,1)S(1)}, bf16[3,2,32,128]{3,2,1,0:T(8,128)(2,1)S(1)}) custom-call(s32[13]{0:T(128)S(1)} %get-tuple-element.46.refs_0_, s32[32]{0:T(128)S(1)} %broadcast_maximum_fusion.delay_ref.refs_1_, s32[8,12]{1,0:T(8,128)S(1)} %get-tuple-element.47.refs_2_, ...), custom_call_target="tpu_custom_call" | custom-call | flops 369098752 | bytes 11534336 | tf_op jit(solution)/shard_map/pallas_call | solution.py:286
  219.0 17.6 %all_to_all.53 = bf16[8,8,32,128]{3,2,1,0:T(8,128)(2,1)S(1)} all-to-all(bf16[8,8,32,128]{3,2,1,0:T(8,128)(2,1)S(1)} %get-tuple-element.77), channel_id=1, replica_groups=mesh['area'=32,'pop'=8] {'pop'}, dimensions={0} | all-to-all | bytes 1048576 | tf_op jit(solution)/shard_map/all_to_all | solution.py:238
  236.6 5.0 %shard_map.108 = (f32[8,32,128]{2,1,0:T(8,128)S(1)}, bf16[1,8,32,128]{3,2,1,0:T(8,128)(2,1)S(1)}, bf16[3,2,32,128]{3,2,1,0:T(8,128)(2,1)S(1)}, bf16[32,4,32,128]{3,2,1,0:T(8,128)(2,1)}) custom-call(s32[13]{0:T(128)S(1)} %get-tuple-element.46.refs_0_, s32[32]{0:T(128)S(1)} %broadcast_maximum_fusion.delay_ref.refs_1_, s32[8,12]{1,0:T(8,128)S(1)} %get-tuple-element.47.refs_2_, ...), custom_call_target="tpu_custom_call" | custom-call | flops 369098752 | bytes 11534336 | tf_op jit(solution)/shard_map/pallas_call | solution.py:286
  241.6 7.1 %all-to-all-start.8 = ((bf16[32,4,32,128]{3,2,1,0:T(8,128)(2,1)}), bf16[32,4,32,128]{3,2,1,0:T(8,128)(2,1)S(1)}, u32[]{:S(2)}, u32[]{:S(2)}) async-start(bf16[32,4,32,128]{3,2,1,0:T(8,128)(2,1)} %get-tuple-element.81), calls=%async_computation.8 | async-start | bytes 2097152 | tf_op jit(solution)/shard_map/all_to_all | solution.py:238
  248.7 14.8 %all_gather.38 = bf16[4,8,32,128]{3,2,1,0:T(8,128)(2,1)S(1)} all-gather(bf16[1,8,32,128]{3,2,1,0:T(8,128)(2,1)S(1)} %get-tuple-element.80), channel_id=1, replica_groups={{0,2,4,6},{1,3,5,7},{8,10,12,14},{9,11,13,15},{16,18,20,22},{17,19,21,2..., dimensions={0}, use_global_device_ids=true | all-gather | bytes 327680 | tf_op jit(solution)/shard_map/all_gather | solution.py:244
  263.5 7.0 %all_gather.39 = bf16[8,8,32,128]{3,2,1,0:T(8,128)(2,1)S(1)} all-gather(bf16[4,8,32,128]{3,2,1,0:T(8,128)(2,1)S(1)} %all_gather.38), channel_id=1, replica_groups={{0,1},{2,3},{4,5},{6,7},{8,9},{10,11},{12,13},{14,15},{16,17},{18,19},{..., dimensions={0}, use_global_device_ids=true | all-gather | bytes 786432 | tf_op jit(solution)/shard_map/all_gather | solution.py:245
  270.5 0.0 all-to-all-done.8.refs_5_
  270.5 4.9 %shard_map.109 = (f32[8,32,128]{2,1,0:T(8,128)S(1)}, bf16[8,8,32,128]{3,2,1,0:T(8,128)(2,1)S(1)}, bf16[3,2,32,128]{3,2,1,0:T(8,128)(2,1)S(1)}) custom-call(s32[13]{0:T(128)S(1)} %get-tuple-element.46.refs_0_, s32[32]{0:T(128)S(1)} %broadcast_maximum_fusion.delay_ref.refs_1_, s32[8,12]{1,0:T(8,128)S(1)} %get-tuple-element.47.refs_2_, ...), custom_call_target="tpu_custom_call" | custom-call | flops 369098752 | bytes 11534336 | tf_op jit(solution)/shard_map/pallas_call | solution.py:286
  275.5 17.8 %all_to_all.54 = bf16[8,8,32,128]{3,2,1,0:T(8,128)(2,1)S(1)} all-to-all(bf16[8,8,32,128]{3,2,1,0:T(8,128)(2,1)S(1)} %get-tuple-element.84), channel_id=1, replica_groups=mesh['area'=32,'pop'=8] {'pop'}, dimensions={0} | all-to-all | bytes 1048576 | tf_op jit(solution)/shard_map/all_to_all | solution.py:238
  293.2 5.5 %shard_map.110 = f32[8,32,128]{2,1,0:T(8,128)} custom-call(s32[13]{0:T(128)S(1)} %get-tuple-element.46.refs_0_, s32[32]{0:T(128)S(1)} %broadcast_maximum_fusion.delay_ref.refs_1_, s32[8,12]{1,0:T(8,128)S(1)} %get-tuple-element.47.refs_2_, s32[8,32]{1,0:T(8,128)S(1)} %get-tuple-element.48.refs_3_, bf16[64,32,128]{2,1,0:T(8,128)(2,1)S(1)} %bitcast.26, ...), custom_call_target="tpu_custom_call" | custom-call | flops 369098752 | bytes 11534336 | tf_op jit(solution)/shard_map/pallas_call | solution.py:286
  (1 shorter events, 0.0 us)
Async XLA Ops:
  0.7 1.0 copy-start
  1.7 0.8 copy-start.1
  2.5 0.7 copy-start.2
  3.2 0.7 copy-start.3
  3.9 0.7 copy-start.4
  4.6 0.7 copy-start.5
  5.3 0.7 copy-start.6
  8.6 33.7 %all-to-all-start = ((bf16[32,4,32,128]{3,2,1,0:T(8,128)(2,1)}), bf16[32,4,32,128]{3,2,1,0:T(8,128)(2,1)S(1)}, u32[]{:S(2)}, u32[]{:S(2)}) async-start(bf16[32,4,32,128]{3,2,1,0:T(8,128)(2,1)} %get-tuple-element.51), calls=%async_computation | async-start | bytes 2097152 | tf_op jit(solution)/shard_map/all_to_all | solution.py:238
  71.9 28.6 %all-to-all-start.2 = ((bf16[32,4,32,128]{3,2,1,0:T(8,128)(2,1)}), bf16[32,4,32,128]{3,2,1,0:T(8,128)(2,1)S(1)}, u32[]{:S(2)}, u32[]{:S(2)}) async-start(bf16[32,4,32,128]{3,2,1,0:T(8,128)(2,1)} %get-tuple-element.60), calls=%async_computation.2 | async-start | bytes 2097152 | tf_op jit(solution)/shard_map/all_to_all | solution.py:238
  128.2 28.9 %all-to-all-start.4 = ((bf16[32,4,32,128]{3,2,1,0:T(8,128)(2,1)}), bf16[32,4,32,128]{3,2,1,0:T(8,128)(2,1)S(1)}, u32[]{:S(2)}, u32[]{:S(2)}) async-start(bf16[32,4,32,128]{3,2,1,0:T(8,128)(2,1)} %get-tuple-element.67), calls=%async_computation.4 | async-start | bytes 2097152 | tf_op jit(solution)/shard_map/all_to_all | solution.py:238
  184.9 29.1 %all-to-all-start.6 = ((bf16[32,4,32,128]{3,2,1,0:T(8,128)(2,1)}), bf16[32,4,32,128]{3,2,1,0:T(8,128)(2,1)S(1)}, u32[]{:S(2)}, u32[]{:S(2)}) async-start(bf16[32,4,32,128]{3,2,1,0:T(8,128)(2,1)} %get-tuple-element.74), calls=%async_computation.6 | async-start | bytes 2097152 | tf_op jit(solution)/shard_map/all_to_all | solution.py:238
  241.6 29.0 %all-to-all-start.8 = ((bf16[32,4,32,128]{3,2,1,0:T(8,128)(2,1)}), bf16[32,4,32,128]{3,2,1,0:T(8,128)(2,1)S(1)}, u32[]{:S(2)}, u32[]{:S(2)}) async-start(bf16[32,4,32,128]{3,2,1,0:T(8,128)(2,1)} %get-tuple-element.81), calls=%async_computation.8 | async-start | bytes 2097152 | tf_op jit(solution)/shard_map/all_to_all | solution.py:238

commit v6 on v5

--- a/solution.py
+++ b/solution.py
@@ -229,7 +229,7 @@
             pltpu.VMEM((DMAX + 1, SEND_DEV, conds, units), bf16),
             older, chosen_scratch, one, one, one, pltpu.SemaphoreType.DMA((len(moved),)),
         ],
-        compiler_params=pltpu.CompilerParams(vmem_limit_bytes=50 * 2**20),
+        compiler_params=pltpu.CompilerParams(vmem_limit_bytes=56 * 2**20),
     )(delay_to, source_area.T, live_blocks, intra_index[0], history, *moved)
     external, leak, pick, index = moved
     inter = inter_weight[0]

time: 300 us -> 297 us (0.990)
  local copies, waits for them, and re-layouts: 6.54 us -> 1.39 us
    unnamed x14 -> x18, local copies, waits for them, and re-layouts: 5.19 us -> 0.04 us
where the time goes in v6:
time: 297 us; the launch traced here: 296 us
  blocking collectives  203 us (68%)
  Pallas kernels  54.1 us (18%)
  starting transfers between devices  36 us (12%)
    all_to_all x5, blocking collectives, exchange(): return lax.all_to_all(x, axis, split_axis=0, concat_axis=0, tiled=True)  90.5 us
    all_gather x5, blocking collectives, gather(): x = lax.all_gather(x, 'pop', axis=0, axis_index_groups=strided, tiled=True)  77.3 us
    pallas_call x10, Pallas kernels, shards(): pl.pallas_call(ordered_kernel(len(ins), len(outs), len(common), functools...  50.3 us
    all_to_all x5, starting transfers between devices, exchange(): return lax.all_to_all(x, axis, split_axis=0, concat_axis=0, tiled=True)  36 us
    all_gather x5, blocking collectives, gather(): lax.all_gather(x, 'pop', axis=0, axis_index_groups=paired, tiled=True)  35.2 us
  transfers between devices with their start and end apart: 5, of which 0 were waited for; matrix products, arithmetic and copies ran while one was open for 0% of the time, Pallas kernels for 0%

profile of v6, /device:TPU:4, one launch (start us, length us, event | category | flops | bytes accessed | tf_op | source)
XLA Modules:
  0.0 296.3 jit_solution(334677024223372513)
XLA Ops:
  0.0 0.7 select_reduce_fusion
  0.7 0.6 broadcast_maximum_fusion.delay_ref.refs_1_
  1.3 0.0 copy-start.6
  1.3 3.7 %shard_map.100 = (f32[8,32,128]{2,1,0:T(8,128)}, bf16[1,8,32,128]{3,2,1,0:T(8,128)(2,1)}, bf16[32,4,32,128]{3,2,1,0:T(8,128)(2,1)}, bf16[3,2,32,128]{3,2,1,0:T(8...) custom-call(s32[32]{0:T(128)} %broadcast_maximum_fusion.delay_ref.re, ...), custom_call_target="tpu_custom_call" | custom-call | tf_op jit(solution)/shard_map/pallas_call | solution.py:218
  5.1 0.0 copy-start
  5.1 0.0 copy-start.1
  5.1 0.0 copy-start.2
  5.1 0.0 copy-start.3
  5.1 0.0 copy-start.5
  5.1 0.0 copy-start.7
  5.1 0.0 copy-start.8
  5.1 7.7 %all-to-all-start = ((bf16[32,4,32,128]{3,2,1,0:T(8,128)(2,1)}), bf16[32,4,32,128]{3,2,1,0:T(8,128)(2,1)S(1)}, u32[]{:S(2)}, u32[]{:S(2)}) async-start(bf16[32,4,32,128]{3,2,1,0:T(8,128)(2,1)} %get-tuple-element.51), calls=%async_computation | async-start | bytes 2097152 | tf_op jit(solution)/shard_map/all_to_all | solution.py:238
  12.9 17.9 %all_gather.30 = bf16[4,8,32,128]{3,2,1,0:T(8,128)(2,1)S(1)} all-gather(bf16[1,8,32,128]{3,2,1,0:T(8,128)(2,1)} %get-tuple-element.50), channel_id=1, replica_groups={{0,2,4,6},{1,3,5,7},{8,10,12,14},{9,11,13,15},{16,18,20,22},{17,19,21,2..., dimensions={0}, use_global_device_ids=true | all-gather | bytes 327680 | tf_op jit(solution)/shard_map/all_gather | solution.py:244
  30.8 7.0 %all_gather.31 = bf16[8,8,32,128]{3,2,1,0:T(8,128)(2,1)S(1)} all-gather(bf16[4,8,32,128]{3,2,1,0:T(8,128)(2,1)S(1)} %all_gather.30), channel_id=1, replica_groups={{0,1},{2,3},{4,5},{6,7},{8,9},{10,11},{12,13},{14,15},{16,17},{18,19},{..., dimensions={0}, use_global_device_ids=true | all-gather | bytes 786432 | tf_op jit(solution)/shard_map/all_gather | solution.py:245
  37.8 1.3 slice_bitcast_fusion.refs_8_
  39.2 0.0 all-to-all-done.refs_5_
  39.2 0.0 copy-done.6
  39.2 0.0 copy-done
  39.2 0.0 copy-done.1
  39.2 0.0 copy-done.2
  39.2 0.0 copy-done.3
  39.2 0.0 copy-done.5
  39.2 0.0 copy-done.7
  39.2 0.0 copy-done.8
  39.2 0.0 copy-start.4
  39.3 4.9 %shard_map.101 = (f32[8,32,128]{2,1,0:T(8,128)S(1)}, bf16[8,8,32,128]{3,2,1,0:T(8,128)(2,1)S(1)}, bf16[3,2,32,128]{3,2,1,0:T(8,128)(2,1)S(1)}) custom-call(s32[13]{0:T(128)S(1)} %copy-done.7, s32[32]{0:T(128)S(1)} %copy-done.6, s32[8,12]{1,0:T(8,128)S(1)} %copy-done.2, s32[8,32]{1,0:T(8,128)S(1)} %copy-done.5, bf16[64,32,128]{2,1,0:T(8,128)(2,1)S(1)} %bitcast.22, ...), custom_call_target="tpu_custom_call" | custom-call | flops 369098752 | bytes 11534336 | tf_op jit(solution)/shard_map/pallas_call | solution.py:286
  44.2 19.3 %all_to_all.50 = bf16[8,8,32,128]{3,2,1,0:T(8,128)(2,1)S(1)} all-to-all(bf16[8,8,32,128]{3,2,1,0:T(8,128)(2,1)S(1)} %get-tuple-element.56), channel_id=1, replica_groups=mesh['area'=32,'pop'=8] {'pop'}, dimensions={0} | all-to-all | bytes 1048576 | tf_op jit(solution)/shard_map/all_to_all | solution.py:238
  63.5 0.0 copy-done.4
  63.5 5.0 %shard_map.102 = (f32[8,32,128]{2,1,0:T(8,128)S(1)}, bf16[1,8,32,128]{3,2,1,0:T(8,128)(2,1)S(1)}, bf16[3,2,32,128]{3,2,1,0:T(8,128)(2,1)S(1)}, bf16[32,4,32,128]{3,2,1,0:T(8,128)(2,1)}) custom-call(s32[13]{0:T(128)S(1)} %copy-done.7, s32[32]{0:T(128)S(1)} %copy-done.6, s32[8,12]{1,0:T(8,128)S(1)} %copy-done.2, s32[8,32]{1,0:T(8,128)S(1)} %copy-done.4, ...), custom_call_target="tpu_custom_call" | custom-call | flops 369098752 | bytes 11534336 | tf_op jit(solution)/shard_map/pallas_call | solution.py:286
  68.5 7.3 %all-to-all-start.2 = ((bf16[32,4,32,128]{3,2,1,0:T(8,128)(2,1)}), bf16[32,4,32,128]{3,2,1,0:T(8,128)(2,1)S(1)}, u32[]{:S(2)}, u32[]{:S(2)}) async-start(bf16[32,4,32,128]{3,2,1,0:T(8,128)(2,1)} %get-tuple-element.60), calls=%async_computation.2 | async-start | bytes 2097152 | tf_op jit(solution)/shard_map/all_to_all | solution.py:238
  75.9 14.9 %all_gather.32 = bf16[4,8,32,128]{3,2,1,0:T(8,128)(2,1)S(1)} all-gather(bf16[1,8,32,128]{3,2,1,0:T(8,128)(2,1)S(1)} %get-tuple-element.59), channel_id=1, replica_groups={{0,2,4,6},{1,3,5,7},{8,10,12,14},{9,11,13,15},{16,18,20,22},{17,19,21,2..., dimensions={0}, use_global_device_ids=true | all-gather | bytes 327680 | tf_op jit(solution)/shard_map/all_gather | solution.py:244
  90.7 7.0 %all_gather.33 = bf16[8,8,32,128]{3,2,1,0:T(8,128)(2,1)S(1)} all-gather(bf16[4,8,32,128]{3,2,1,0:T(8,128)(2,1)S(1)} %all_gather.32), channel_id=1, replica_groups={{0,1},{2,3},{4,5},{6,7},{8,9},{10,11},{12,13},{14,15},{16,17},{18,19},{..., dimensions={0}, use_global_device_ids=true | all-gather | bytes 786432 | tf_op jit(solution)/shard_map/all_gather | solution.py:245
  97.8 0.0 all-to-all-done.2.refs_5_
  97.8 4.9 %shard_map.103 = (f32[8,32,128]{2,1,0:T(8,128)S(1)}, bf16[8,8,32,128]{3,2,1,0:T(8,128)(2,1)S(1)}, bf16[3,2,32,128]{3,2,1,0:T(8,128)(2,1)S(1)}) custom-call(s32[13]{0:T(128)S(1)} %copy-done.7, s32[32]{0:T(128)S(1)} %copy-done.6, s32[8,12]{1,0:T(8,128)S(1)} %copy-done.2, s32[8,32]{1,0:T(8,128)S(1)} %copy-done.5, bf16[64,32,128]{2,1,0:T(8,128)(2,1)S(1)} %bitcast.23, ...), custom_call_target="tpu_custom_call" | custom-call | flops 369098752 | bytes 11534336 | tf_op jit(solution)/shard_map/pallas_call | solution.py:286
  102.7 17.7 %all_to_all.51 = bf16[8,8,32,128]{3,2,1,0:T(8,128)(2,1)S(1)} all-to-all(bf16[8,8,32,128]{3,2,1,0:T(8,128)(2,1)S(1)} %get-tuple-element.63), channel_id=1, replica_groups=mesh['area'=32,'pop'=8] {'pop'}, dimensions={0} | all-to-all | bytes 1048576 | tf_op jit(solution)/shard_map/all_to_all | solution.py:238
  120.4 5.0 %shard_map.104 = (f32[8,32,128]{2,1,0:T(8,128)S(1)}, bf16[1,8,32,128]{3,2,1,0:T(8,128)(2,1)S(1)}, bf16[3,2,32,128]{3,2,1,0:T(8,128)(2,1)S(1)}, bf16[32,4,32,128]{3,2,1,0:T(8,128)(2,1)}) custom-call(s32[13]{0:T(128)S(1)} %copy-done.7, s32[32]{0:T(128)S(1)} %copy-done.6, s32[8,12]{1,0:T(8,128)S(1)} %copy-done.2, s32[8,32]{1,0:T(8,128)S(1)} %copy-done.4, ...), custom_call_target="tpu_custom_call" | custom-call | flops 369098752 | bytes 11534336 | tf_op jit(solution)/shard_map/pallas_call | solution.py:286
  125.5 7.0 %all-to-all-start.4 = ((bf16[32,4,32,128]{3,2,1,0:T(8,128)(2,1)}), bf16[32,4,32,128]{3,2,1,0:T(8,128)(2,1)S(1)}, u32[]{:S(2)}, u32[]{:S(2)}) async-start(bf16[32,4,32,128]{3,2,1,0:T(8,128)(2,1)} %get-tuple-element.67), calls=%async_computation.4 | async-start | bytes 2097152 | tf_op jit(solution)/shard_map/all_to_all | solution.py:238
  132.4 14.8 %all_gather.34 = bf16[4,8,32,128]{3,2,1,0:T(8,128)(2,1)S(1)} all-gather(bf16[1,8,32,128]{3,2,1,0:T(8,128)(2,1)S(1)} %get-tuple-element.66), channel_id=1, replica_groups={{0,2,4,6},{1,3,5,7},{8,10,12,14},{9,11,13,15},{16,18,20,22},{17,19,21,2..., dimensions={0}, use_global_device_ids=true | all-gather | bytes 327680 | tf_op jit(solution)/shard_map/all_gather | solution.py:244
  147.3 7.0 %all_gather.35 = bf16[8,8,32,128]{3,2,1,0:T(8,128)(2,1)S(1)} all-gather(bf16[4,8,32,128]{3,2,1,0:T(8,128)(2,1)S(1)} %all_gather.34), channel_id=1, replica_groups={{0,1},{2,3},{4,5},{6,7},{8,9},{10,11},{12,13},{14,15},{16,17},{18,19},{..., dimensions={0}, use_global_device_ids=true | all-gather | bytes 786432 | tf_op jit(solution)/shard_map/all_gather | solution.py:245
  154.3 0.0 all-to-all-done.4.refs_5_
  154.3 4.9 %shard_map.105 = (f32[8,32,128]{2,1,0:T(8,128)S(1)}, bf16[8,8,32,128]{3,2,1,0:T(8,128)(2,1)S(1)}, bf16[3,2,32,128]{3,2,1,0:T(8,128)(2,1)S(1)}) custom-call(s32[13]{0:T(128)S(1)} %copy-done.7, s32[32]{0:T(128)S(1)} %copy-done.6, s32[8,12]{1,0:T(8,128)S(1)} %copy-done.2, s32[8,32]{1,0:T(8,128)S(1)} %copy-done.5, bf16[64,32,128]{2,1,0:T(8,128)(2,1)S(1)} %bitcast.24, ...), custom_call_target="tpu_custom_call" | custom-call | flops 369098752 | bytes 11534336 | tf_op jit(solution)/shard_map/pallas_call | solution.py:286
  159.3 17.8 %all_to_all.52 = bf16[8,8,32,128]{3,2,1,0:T(8,128)(2,1)S(1)} all-to-all(bf16[8,8,32,128]{3,2,1,0:T(8,128)(2,1)S(1)} %get-tuple-element.70), channel_id=1, replica_groups=mesh['area'=32,'pop'=8] {'pop'}, dimensions={0} | all-to-all | bytes 1048576 | tf_op jit(solution)/shard_map/all_to_all | solution.py:238
  177.1 5.0 %shard_map.106 = (f32[8,32,128]{2,1,0:T(8,128)S(1)}, bf16[1,8,32,128]{3,2,1,0:T(8,128)(2,1)S(1)}, bf16[3,2,32,128]{3,2,1,0:T(8,128)(2,1)S(1)}, bf16[32,4,32,128]{3,2,1,0:T(8,128)(2,1)}) custom-call(s32[13]{0:T(128)S(1)} %copy-done.7, s32[32]{0:T(128)S(1)} %copy-done.6, s32[8,12]{1,0:T(8,128)S(1)} %copy-done.2, s32[8,32]{1,0:T(8,128)S(1)} %copy-done.4, ...), custom_call_target="tpu_custom_call" | custom-call | flops 369098752 | bytes 11534336 | tf_op jit(solution)/shard_map/pallas_call | solution.py:286
  182.1 7.0 %all-to-all-start.6 = ((bf16[32,4,32,128]{3,2,1,0:T(8,128)(2,1)}), bf16[32,4,32,128]{3,2,1,0:T(8,128)(2,1)S(1)}, u32[]{:S(2)}, u32[]{:S(2)}) async-start(bf16[32,4,32,128]{3,2,1,0:T(8,128)(2,1)} %get-tuple-element.74), calls=%async_computation.6 | async-start | bytes 2097152 | tf_op jit(solution)/shard_map/all_to_all | solution.py:238
  189.1 14.9 %all_gather.36 = bf16[4,8,32,128]{3,2,1,0:T(8,128)(2,1)S(1)} all-gather(bf16[1,8,32,128]{3,2,1,0:T(8,128)(2,1)S(1)} %get-tuple-element.73), channel_id=1, replica_groups={{0,2,4,6},{1,3,5,7},{8,10,12,14},{9,11,13,15},{16,18,20,22},{17,19,21,2..., dimensions={0}, use_global_device_ids=true | all-gather | bytes 327680 | tf_op jit(solution)/shard_map/all_gather | solution.py:244
  204.0 7.0 %all_gather.37 = bf16[8,8,32,128]{3,2,1,0:T(8,128)(2,1)S(1)} all-gather(bf16[4,8,32,128]{3,2,1,0:T(8,128)(2,1)S(1)} %all_gather.36), channel_id=1, replica_groups={{0,1},{2,3},{4,5},{6,7},{8,9},{10,11},{12,13},{14,15},{16,17},{18,19},{..., dimensions={0}, use_global_device_ids=true | all-gather | bytes 786432 | tf_op jit(solution)/shard_map/all_gather | solution.py:245
  211.0 0.0 all-to-all-done.6.refs_5_
  211.0 4.9 %shard_map.107 = (f32[8,32,128]{2,1,0:T(8,128)S(1)}, bf16[8,8,32,128]{3,2,1,0:T(8,128)(2,1)S(1)}, bf16[3,2,32,128]{3,2,1,0:T(8,128)(2,1)S(1)}) custom-call(s32[13]{0:T(128)S(1)} %copy-done.7, s32[32]{0:T(128)S(1)} %copy-done.6, s32[8,12]{1,0:T(8,128)S(1)} %copy-done.2, s32[8,32]{1,0:T(8,128)S(1)} %copy-done.5, bf16[64,32,128]{2,1,0:T(8,128)(2,1)S(1)} %bitcast.25, ...), custom_call_target="tpu_custom_call" | custom-call | flops 369098752 | bytes 11534336 | tf_op jit(solution)/shard_map/pallas_call | solution.py:286
  216.0 17.8 %all_to_all.53 = bf16[8,8,32,128]{3,2,1,0:T(8,128)(2,1)S(1)} all-to-all(bf16[8,8,32,128]{3,2,1,0:T(8,128)(2,1)S(1)} %get-tuple-element.77), channel_id=1, replica_groups=mesh['area'=32,'pop'=8] {'pop'}, dimensions={0} | all-to-all | bytes 1048576 | tf_op jit(solution)/shard_map/all_to_all | solution.py:238
  233.8 5.0 %shard_map.108 = (f32[8,32,128]{2,1,0:T(8,128)S(1)}, bf16[1,8,32,128]{3,2,1,0:T(8,128)(2,1)S(1)}, bf16[3,2,32,128]{3,2,1,0:T(8,128)(2,1)S(1)}, bf16[32,4,32,128]{3,2,1,0:T(8,128)(2,1)}) custom-call(s32[13]{0:T(128)S(1)} %copy-done.7, s32[32]{0:T(128)S(1)} %copy-done.6, s32[8,12]{1,0:T(8,128)S(1)} %copy-done.2, s32[8,32]{1,0:T(8,128)S(1)} %copy-done.4, ...), custom_call_target="tpu_custom_call" | custom-call | flops 369098752 | bytes 11534336 | tf_op jit(solution)/shard_map/pallas_call | solution.py:286
  238.8 7.0 %all-to-all-start.8 = ((bf16[32,4,32,128]{3,2,1,0:T(8,128)(2,1)}), bf16[32,4,32,128]{3,2,1,0:T(8,128)(2,1)S(1)}, u32[]{:S(2)}, u32[]{:S(2)}) async-start(bf16[32,4,32,128]{3,2,1,0:T(8,128)(2,1)} %get-tuple-element.81), calls=%async_computation.8 | async-start | bytes 2097152 | tf_op jit(solution)/shard_map/all_to_all | solution.py:238
  245.8 14.8 %all_gather.38 = bf16[4,8,32,128]{3,2,1,0:T(8,128)(2,1)S(1)} all-gather(bf16[1,8,32,128]{3,2,1,0:T(8,128)(2,1)S(1)} %get-tuple-element.80), channel_id=1, replica_groups={{0,2,4,6},{1,3,5,7},{8,10,12,14},{9,11,13,15},{16,18,20,22},{17,19,21,2..., dimensions={0}, use_global_device_ids=true | all-gather | bytes 327680 | tf_op jit(solution)/shard_map/all_gather | solution.py:244
  260.7 7.0 %all_gather.39 = bf16[8,8,32,128]{3,2,1,0:T(8,128)(2,1)S(1)} all-gather(bf16[4,8,32,128]{3,2,1,0:T(8,128)(2,1)S(1)} %all_gather.38), channel_id=1, replica_groups={{0,1},{2,3},{4,5},{6,7},{8,9},{10,11},{12,13},{14,15},{16,17},{18,19},{..., dimensions={0}, use_global_device_ids=true | all-gather | bytes 786432 | tf_op jit(solution)/shard_map/all_gather | solution.py:245
  267.7 0.0 all-to-all-done.8.refs_5_
  267.7 4.9 %shard_map.109 = (f32[8,32,128]{2,1,0:T(8,128)S(1)}, bf16[8,8,32,128]{3,2,1,0:T(8,128)(2,1)S(1)}, bf16[3,2,32,128]{3,2,1,0:T(8,128)(2,1)S(1)}) custom-call(s32[13]{0:T(128)S(1)} %copy-done.7, s32[32]{0:T(128)S(1)} %copy-done.6, s32[8,12]{1,0:T(8,128)S(1)} %copy-done.2, s32[8,32]{1,0:T(8,128)S(1)} %copy-done.5, bf16[64,32,128]{2,1,0:T(8,128)(2,1)S(1)} %bitcast.21, ...), custom_call_target="tpu_custom_call" | custom-call | flops 369098752 | bytes 11534336 | tf_op jit(solution)/shard_map/pallas_call | solution.py:286
  272.7 17.8 %all_to_all.54 = bf16[8,8,32,128]{3,2,1,0:T(8,128)(2,1)S(1)} all-to-all(bf16[8,8,32,128]{3,2,1,0:T(8,128)(2,1)S(1)} %get-tuple-element.84), channel_id=1, replica_groups=mesh['area'=32,'pop'=8] {'pop'}, dimensions={0} | all-to-all | bytes 1048576 | tf_op jit(solution)/shard_map/all_to_all | solution.py:238
  290.5 5.6 %shard_map.110 = f32[8,32,128]{2,1,0:T(8,128)} custom-call(s32[13]{0:T(128)S(1)} %copy-done.7, s32[32]{0:T(128)S(1)} %copy-done.6, s32[8,12]{1,0:T(8,128)S(1)} %copy-done.2, s32[8,32]{1,0:T(8,128)S(1)} %copy-done.4, bf16[64,32,128]{2,1,0:T(8,128)(2,1)S(1)} %bitcast.26, bf16[32,4,32,128]{3,2,1,0:T(8,128)(2,1)S(1)} %all-to-all-done.8.refs_5_, ...), custom_call_target="tpu_custom_call" | custom-call | flops 369098752 | bytes 11534336 | tf_op jit(solution)/shard_map/pallas_call | solution.py:286
Async XLA Ops:
  1.3 37.9 %copy-start.6 = (s32[32]{0:T(128)S(1)}, s32[32]{0:T(128)}, u32[]{:S(2)}) copy-start(s32[32]{0:T(128)} %broadcast_maximum_fusion.delay_ref.refs_1_) | copy-start | bytes 388
  5.1 34.1 %copy-start = (bf16[8,32,128]{2,1,0:T(8,128)(2,1)S(1)}, bf16[8,32,128]{2,1,0:T(8,128)(2,1)}, u32[]{:S(2)}) copy-start(bf16[8,32,128]{2,1,0:T(8,128)(2,1)} %get-tuple-element.52.refs_9_) | copy-start | bytes 196612
  5.1 34.1 %copy-start.1 = (f32[8,128]{1,0:T(8,128)S(1)}, f32[8,128]{1,0:T(8,128)}, u32[]{:S(2)}) copy-start(f32[8,128]{1,0:T(8,128)} %get-tuple-element.53.refs_10_) | copy-start | bytes 12292
  5.1 34.1 %copy-start.2 = (s32[8,12]{1,0:T(8,128)S(1)}, s32[8,12]{1,0:T(8,128)}, u32[]{:S(2)}) copy-start(s32[8,12]{1,0:T(8,128)} %get-tuple-element.47.refs_2_) | copy-start | bytes 1156
  5.1 34.1 %copy-start.3 = (f32[8,32,128]{2,1,0:T(8,128)S(1)}, f32[8,32,128]{2,1,0:T(8,128)}, u32[]{:S(2)}) copy-start(f32[8,32,128]{2,1,0:T(8,128)} %get-tuple-element.54.refs_11_) | copy-start | bytes 393220
  5.1 34.1 %copy-start.5 = (s32[8,32]{1,0:T(8,128)S(1)}, s32[8,32]{1,0:T(8,128)}, u32[]{:S(2)}) copy-start(s32[8,32]{1,0:T(8,128)} %get-tuple-element.49.refs_3_) | copy-start | bytes 3076
  5.1 34.1 %copy-start.7 = (s32[13]{0:T(128)S(1)}, s32[13]{0:T(128)}, u32[]{:S(2)}) copy-start(s32[13]{0:T(128)} %get-tuple-element.46.refs_0_) | copy-start | bytes 160
  5.1 34.1 %copy-start.8 = (bf16[3,2,32,128]{3,2,1,0:T(8,128)(2,1)S(1)}, bf16[3,2,32,128]{3,2,1,0:T(8,128)(2,1)}, u32[]{:S(2)}) copy-start(bf16[3,2,32,128]{3,2,1,0:T(8,128)(2,1)} %get-tuple-element.55.refs_12_) | copy-start | bytes 147460
  5.1 34.0 %all-to-all-start = ((bf16[32,4,32,128]{3,2,1,0:T(8,128)(2,1)}), bf16[32,4,32,128]{3,2,1,0:T(8,128)(2,1)S(1)}, u32[]{:S(2)}, u32[]{:S(2)}) async-start(bf16[32,4,32,128]{3,2,1,0:T(8,128)(2,1)} %get-tuple-element.51), calls=%async_computation | async-start | bytes 2097152 | tf_op jit(solution)/shard_map/all_to_all | solution.py:238
  39.2 24.3 %copy-start.4 = (s32[8,32]{1,0:T(8,128)S(1)}, s32[8,32]{1,0:T(8,128)}, u32[]{:S(2)}) copy-start(s32[8,32]{1,0:T(8,128)} %get-tuple-element.48.refs_3_) | copy-start | bytes 3076
  68.5 29.2 %all-to-all-start.2 = ((bf16[32,4,32,128]{3,2,1,0:T(8,128)(2,1)}), bf16[32,4,32,128]{3,2,1,0:T(8,128)(2,1)S(1)}, u32[]{:S(2)}, u32[]{:S(2)}) async-start(bf16[32,4,32,128]{3,2,1,0:T(8,128)(2,1)} %get-tuple-element.60), calls=%async_computation.2 | async-start | bytes 2097152 | tf_op jit(solution)/shard_map/all_to_all | solution.py:238
  125.5 28.9 %all-to-all-start.4 = ((bf16[32,4,32,128]{3,2,1,0:T(8,128)(2,1)}), bf16[32,4,32,128]{3,2,1,0:T(8,128)(2,1)S(1)}, u32[]{:S(2)}, u32[]{:S(2)}) async-start(bf16[32,4,32,128]{3,2,1,0:T(8,128)(2,1)} %get-tuple-element.67), calls=%async_computation.4 | async-start | bytes 2097152 | tf_op jit(solution)/shard_map/all_to_all | solution.py:238
  182.1 28.9 %all-to-all-start.6 = ((bf16[32,4,32,128]{3,2,1,0:T(8,128)(2,1)}), bf16[32,4,32,128]{3,2,1,0:T(8,128)(2,1)S(1)}, u32[]{:S(2)}, u32[]{:S(2)}) async-start(bf16[32,4,32,128]{3,2,1,0:T(8,128)(2,1)} %get-tuple-element.74), calls=%async_computation.6 | async-start | bytes 2097152 | tf_op jit(solution)/shard_map/all_to_all | solution.py:238
  238.8 28.9 %all-to-all-start.8 = ((bf16[32,4,32,128]{3,2,1,0:T(8,128)(2,1)}), bf16[32,4,32,128]{3,2,1,0:T(8,128)(2,1)S(1)}, u32[]{:S(2)}, u32[]{:S(2)}) async-start(bf16[32,4,32,128]{3,2,1,0:T(8,128)(2,1)} %get-tuple-element.81), calls=%async_computation.8 | async-start | bytes 2097152 | tf_op jit(solution)/shard_map/all_to_all | solution.py:238

commit v7 on v6

--- a/solution.py
+++ b/solution.py
@@ -28,7 +28,7 @@
 
 def choose(delay_ref, older_ref, chosen_ref):
     for area in range(chosen_ref.shape[0]):
-        delay = delay_ref[area]
+        delay = jnp.maximum(delay_ref[area], 1)
         chosen_ref[area, :SEND_DEV] = older_ref[delay]
         chosen_ref[area, SEND_DEV:] = older_ref[delay - 1]
 
@@ -213,7 +213,6 @@
 
     area_pos = lax.axis_index("area")
     delay_to = jnp.sum(jnp.where(source_area == area_pos, delays, 0), axis=1)
-    delay_to = jnp.maximum(delay_to, 1)
     moved = [external[0], leak_rate[0], inter_pick[0], intra_index[0]]
     activity, spread, chosen, recent, table, gathered_index, *moved = pl.pallas_call(
         first_kernel,

time: 297 us -> 297 us (level)
  no operation moved by 1% of the time
where the time goes in v7:
time: 297 us; the launch traced here: 296 us
  blocking collectives  203 us (68%)
  Pallas kernels  54 us (18%)
  starting transfers between devices  36.3 us (12%)
    all_to_all x5, blocking collectives, exchange(): return lax.all_to_all(x, axis, split_axis=0, concat_axis=0, tiled=True)  90.1 us
    all_gather x5, blocking collectives, gather(): x = lax.all_gather(x, 'pop', axis=0, axis_index_groups=strided, tiled=True)  77.4 us
    pallas_call x10, Pallas kernels, shards(): pl.pallas_call(ordered_kernel(len(ins), len(outs), len(common), functools...  50.3 us
    all_to_all x5, starting transfers between devices, exchange(): return lax.all_to_all(x, axis, split_axis=0, concat_axis=0, tiled=True)  36.3 us
    all_gather x5, blocking collectives, gather(): lax.all_gather(x, 'pop', axis=0, axis_index_groups=paired, tiled=True)  35.2 us
  transfers between devices with their start and end apart: 5, of which 0 were waited for; matrix products, arithmetic and copies ran while one was open for 0% of the time, Pallas kernels for 0%

profile of v7, /device:TPU:4, one launch (start us, length us, event | category | flops | bytes accessed | tf_op | source)
XLA Modules:
  0.0 296.1 jit_solution(11257241340628069373)
XLA Ops:
  0.0 1.3 select_reduce_fusion.delay_ref.refs_1_
  1.3 0.0 copy-start.6
  1.3 3.7 %shard_map.100 = (f32[8,32,128]{2,1,0:T(8,128)}, bf16[1,8,32,128]{3,2,1,0:T(8,128)(2,1)}, bf16[32,4,32,128]{3,2,1,0:T(8,128)(2,1)}, bf16[3,2,32,128]{3,2,1,0:T(8...) custom-call(s32[32]{0:T(128)} %select_reduce_fusion.delay_ref.refs_1, ...), custom_call_target="tpu_custom_call" | custom-call | tf_op jit(solution)/shard_map/pallas_call | solution.py:217
  5.1 0.0 copy-start
  5.1 0.0 copy-start.1
  5.1 0.0 copy-start.2
  5.1 0.0 copy-start.3
  5.1 0.0 copy-start.5
  5.1 0.0 copy-start.7
  5.1 0.0 copy-start.8
  5.1 7.7 %all-to-all-start = ((bf16[32,4,32,128]{3,2,1,0:T(8,128)(2,1)}), bf16[32,4,32,128]{3,2,1,0:T(8,128)(2,1)S(1)}, u32[]{:S(2)}, u32[]{:S(2)}) async-start(bf16[32,4,32,128]{3,2,1,0:T(8,128)(2,1)} %get-tuple-element.51), calls=%async_computation | async-start | bytes 2097152 | tf_op jit(solution)/shard_map/all_to_all | solution.py:237
  12.9 17.9 %all_gather.30 = bf16[4,8,32,128]{3,2,1,0:T(8,128)(2,1)S(1)} all-gather(bf16[1,8,32,128]{3,2,1,0:T(8,128)(2,1)} %get-tuple-element.50), channel_id=1, replica_groups={{0,2,4,6},{1,3,5,7},{8,10,12,14},{9,11,13,15},{16,18,20,22},{17,19,21,2..., dimensions={0}, use_global_device_ids=true | all-gather | bytes 327680 | tf_op jit(solution)/shard_map/all_gather | solution.py:243
  30.8 7.0 %all_gather.31 = bf16[8,8,32,128]{3,2,1,0:T(8,128)(2,1)S(1)} all-gather(bf16[4,8,32,128]{3,2,1,0:T(8,128)(2,1)S(1)} %all_gather.30), channel_id=1, replica_groups={{0,1},{2,3},{4,5},{6,7},{8,9},{10,11},{12,13},{14,15},{16,17},{18,19},{..., dimensions={0}, use_global_device_ids=true | all-gather | bytes 786432 | tf_op jit(solution)/shard_map/all_gather | solution.py:244
  37.8 1.4 slice_bitcast_fusion.refs_8_
  39.2 0.0 all-to-all-done.refs_5_
  39.2 0.0 copy-done.6
  39.2 0.0 copy-done
  39.2 0.0 copy-done.1
  39.2 0.0 copy-done.2
  39.2 0.0 copy-done.3
  39.2 0.0 copy-done.5
  39.3 0.0 copy-done.7
  39.3 0.0 copy-done.8
  39.3 0.0 copy-start.4
  39.3 4.9 %shard_map.101 = (f32[8,32,128]{2,1,0:T(8,128)S(1)}, bf16[8,8,32,128]{3,2,1,0:T(8,128)(2,1)S(1)}, bf16[3,2,32,128]{3,2,1,0:T(8,128)(2,1)S(1)}) custom-call(s32[13]{0:T(128)S(1)} %copy-done.7, s32[32]{0:T(128)S(1)} %copy-done.6, s32[8,12]{1,0:T(8,128)S(1)} %copy-done.2, s32[8,32]{1,0:T(8,128)S(1)} %copy-done.5, bf16[64,32,128]{2,1,0:T(8,128)(2,1)S(1)} %bitcast.22, ...), custom_call_target="tpu_custom_call" | custom-call | flops 369098752 | bytes 11534336 | tf_op jit(solution)/shard_map/pallas_call | solution.py:285
  44.2 19.3 %all_to_all.50 = bf16[8,8,32,128]{3,2,1,0:T(8,128)(2,1)S(1)} all-to-all(bf16[8,8,32,128]{3,2,1,0:T(8,128)(2,1)S(1)} %get-tuple-element.56), channel_id=1, replica_groups=mesh['area'=32,'pop'=8] {'pop'}, dimensions={0} | all-to-all | bytes 1048576 | tf_op jit(solution)/shard_map/all_to_all | solution.py:237
  63.5 0.0 copy-done.4
  63.5 5.0 %shard_map.102 = (f32[8,32,128]{2,1,0:T(8,128)S(1)}, bf16[1,8,32,128]{3,2,1,0:T(8,128)(2,1)S(1)}, bf16[3,2,32,128]{3,2,1,0:T(8,128)(2,1)S(1)}, bf16[32,4,32,128]{3,2,1,0:T(8,128)(2,1)}) custom-call(s32[13]{0:T(128)S(1)} %copy-done.7, s32[32]{0:T(128)S(1)} %copy-done.6, s32[8,12]{1,0:T(8,128)S(1)} %copy-done.2, s32[8,32]{1,0:T(8,128)S(1)} %copy-done.4, ...), custom_call_target="tpu_custom_call" | custom-call | flops 369098752 | bytes 11534336 | tf_op jit(solution)/shard_map/pallas_call | solution.py:285
  68.5 7.3 %all-to-all-start.2 = ((bf16[32,4,32,128]{3,2,1,0:T(8,128)(2,1)}), bf16[32,4,32,128]{3,2,1,0:T(8,128)(2,1)S(1)}, u32[]{:S(2)}, u32[]{:S(2)}) async-start(bf16[32,4,32,128]{3,2,1,0:T(8,128)(2,1)} %get-tuple-element.60), calls=%async_computation.2 | async-start | bytes 2097152 | tf_op jit(solution)/shard_map/all_to_all | solution.py:237
  75.9 14.9 %all_gather.32 = bf16[4,8,32,128]{3,2,1,0:T(8,128)(2,1)S(1)} all-gather(bf16[1,8,32,128]{3,2,1,0:T(8,128)(2,1)S(1)} %get-tuple-element.59), channel_id=1, replica_groups={{0,2,4,6},{1,3,5,7},{8,10,12,14},{9,11,13,15},{16,18,20,22},{17,19,21,2..., dimensions={0}, use_global_device_ids=true | all-gather | bytes 327680 | tf_op jit(solution)/shard_map/all_gather | solution.py:243
  90.8 7.0 %all_gather.33 = bf16[8,8,32,128]{3,2,1,0:T(8,128)(2,1)S(1)} all-gather(bf16[4,8,32,128]{3,2,1,0:T(8,128)(2,1)S(1)} %all_gather.32), channel_id=1, replica_groups={{0,1},{2,3},{4,5},{6,7},{8,9},{10,11},{12,13},{14,15},{16,17},{18,19},{..., dimensions={0}, use_global_device_ids=true | all-gather | bytes 786432 | tf_op jit(solution)/shard_map/all_gather | solution.py:244
  97.8 0.0 all-to-all-done.2.refs_5_
  97.8 4.9 %shard_map.103 = (f32[8,32,128]{2,1,0:T(8,128)S(1)}, bf16[8,8,32,128]{3,2,1,0:T(8,128)(2,1)S(1)}, bf16[3,2,32,128]{3,2,1,0:T(8,128)(2,1)S(1)}) custom-call(s32[13]{0:T(128)S(1)} %copy-done.7, s32[32]{0:T(128)S(1)} %copy-done.6, s32[8,12]{1,0:T(8,128)S(1)} %copy-done.2, s32[8,32]{1,0:T(8,128)S(1)} %copy-done.5, bf16[64,32,128]{2,1,0:T(8,128)(2,1)S(1)} %bitcast.23, ...), custom_call_target="tpu_custom_call" | custom-call | flops 369098752 | bytes 11534336 | tf_op jit(solution)/shard_map/pallas_call | solution.py:285
  102.8 17.4 %all_to_all.51 = bf16[8,8,32,128]{3,2,1,0:T(8,128)(2,1)S(1)} all-to-all(bf16[8,8,32,128]{3,2,1,0:T(8,128)(2,1)S(1)} %get-tuple-element.63), channel_id=1, replica_groups=mesh['area'=32,'pop'=8] {'pop'}, dimensions={0} | all-to-all | bytes 1048576 | tf_op jit(solution)/shard_map/all_to_all | solution.py:237
  120.1 5.0 %shard_map.104 = (f32[8,32,128]{2,1,0:T(8,128)S(1)}, bf16[1,8,32,128]{3,2,1,0:T(8,128)(2,1)S(1)}, bf16[3,2,32,128]{3,2,1,0:T(8,128)(2,1)S(1)}, bf16[32,4,32,128]{3,2,1,0:T(8,128)(2,1)}) custom-call(s32[13]{0:T(128)S(1)} %copy-done.7, s32[32]{0:T(128)S(1)} %copy-done.6, s32[8,12]{1,0:T(8,128)S(1)} %copy-done.2, s32[8,32]{1,0:T(8,128)S(1)} %copy-done.4, ...), custom_call_target="tpu_custom_call" | custom-call | flops 369098752 | bytes 11534336 | tf_op jit(solution)/shard_map/pallas_call | solution.py:285
  125.2 7.2 %all-to-all-start.4 = ((bf16[32,4,32,128]{3,2,1,0:T(8,128)(2,1)}), bf16[32,4,32,128]{3,2,1,0:T(8,128)(2,1)S(1)}, u32[]{:S(2)}, u32[]{:S(2)}) async-start(bf16[32,4,32,128]{3,2,1,0:T(8,128)(2,1)} %get-tuple-element.67), calls=%async_computation.4 | async-start | bytes 2097152 | tf_op jit(solution)/shard_map/all_to_all | solution.py:237
  132.3 14.8 %all_gather.34 = bf16[4,8,32,128]{3,2,1,0:T(8,128)(2,1)S(1)} all-gather(bf16[1,8,32,128]{3,2,1,0:T(8,128)(2,1)S(1)} %get-tuple-element.66), channel_id=1, replica_groups={{0,2,4,6},{1,3,5,7},{8,10,12,14},{9,11,13,15},{16,18,20,22},{17,19,21,2..., dimensions={0}, use_global_device_ids=true | all-gather | bytes 327680 | tf_op jit(solution)/shard_map/all_gather | solution.py:243
  147.1 7.0 %all_gather.35 = bf16[8,8,32,128]{3,2,1,0:T(8,128)(2,1)S(1)} all-gather(bf16[4,8,32,128]{3,2,1,0:T(8,128)(2,1)S(1)} %all_gather.34), channel_id=1, replica_groups={{0,1},{2,3},{4,5},{6,7},{8,9},{10,11},{12,13},{14,15},{16,17},{18,19},{..., dimensions={0}, use_global_device_ids=true | all-gather | bytes 786432 | tf_op jit(solution)/shard_map/all_gather | solution.py:244
  154.2 0.0 all-to-all-done.4.refs_5_
  154.2 4.9 %shard_map.105 = (f32[8,32,128]{2,1,0:T(8,128)S(1)}, bf16[8,8,32,128]{3,2,1,0:T(8,128)(2,1)S(1)}, bf16[3,2,32,128]{3,2,1,0:T(8,128)(2,1)S(1)}) custom-call(s32[13]{0:T(128)S(1)} %copy-done.7, s32[32]{0:T(128)S(1)} %copy-done.6, s32[8,12]{1,0:T(8,128)S(1)} %copy-done.2, s32[8,32]{1,0:T(8,128)S(1)} %copy-done.5, bf16[64,32,128]{2,1,0:T(8,128)(2,1)S(1)} %bitcast.24, ...), custom_call_target="tpu_custom_call" | custom-call | flops 369098752 | bytes 11534336 | tf_op jit(solution)/shard_map/pallas_call | solution.py:285
  159.1 17.9 %all_to_all.52 = bf16[8,8,32,128]{3,2,1,0:T(8,128)(2,1)S(1)} all-to-all(bf16[8,8,32,128]{3,2,1,0:T(8,128)(2,1)S(1)} %get-tuple-element.70), channel_id=1, replica_groups=mesh['area'=32,'pop'=8] {'pop'}, dimensions={0} | all-to-all | bytes 1048576 | tf_op jit(solution)/shard_map/all_to_all | solution.py:237
  177.0 5.0 %shard_map.106 = (f32[8,32,128]{2,1,0:T(8,128)S(1)}, bf16[1,8,32,128]{3,2,1,0:T(8,128)(2,1)S(1)}, bf16[3,2,32,128]{3,2,1,0:T(8,128)(2,1)S(1)}, bf16[32,4,32,128]{3,2,1,0:T(8,128)(2,1)}) custom-call(s32[13]{0:T(128)S(1)} %copy-done.7, s32[32]{0:T(128)S(1)} %copy-done.6, s32[8,12]{1,0:T(8,128)S(1)} %copy-done.2, s32[8,32]{1,0:T(8,128)S(1)} %copy-done.4, ...), custom_call_target="tpu_custom_call" | custom-call | flops 369098752 | bytes 11534336 | tf_op jit(solution)/shard_map/pallas_call | solution.py:285
  182.0 7.0 %all-to-all-start.6 = ((bf16[32,4,32,128]{3,2,1,0:T(8,128)(2,1)}), bf16[32,4,32,128]{3,2,1,0:T(8,128)(2,1)S(1)}, u32[]{:S(2)}, u32[]{:S(2)}) async-start(bf16[32,4,32,128]{3,2,1,0:T(8,128)(2,1)} %get-tuple-element.74), calls=%async_computation.6 | async-start | bytes 2097152 | tf_op jit(solution)/shard_map/all_to_all | solution.py:237
  189.1 14.9 %all_gather.36 = bf16[4,8,32,128]{3,2,1,0:T(8,128)(2,1)S(1)} all-gather(bf16[1,8,32,128]{3,2,1,0:T(8,128)(2,1)S(1)} %get-tuple-element.73), channel_id=1, replica_groups={{0,2,4,6},{1,3,5,7},{8,10,12,14},{9,11,13,15},{16,18,20,22},{17,19,21,2..., dimensions={0}, use_global_device_ids=true | all-gather | bytes 327680 | tf_op jit(solution)/shard_map/all_gather | solution.py:243
  204.0 7.0 %all_gather.37 = bf16[8,8,32,128]{3,2,1,0:T(8,128)(2,1)S(1)} all-gather(bf16[4,8,32,128]{3,2,1,0:T(8,128)(2,1)S(1)} %all_gather.36), channel_id=1, replica_groups={{0,1},{2,3},{4,5},{6,7},{8,9},{10,11},{12,13},{14,15},{16,17},{18,19},{..., dimensions={0}, use_global_device_ids=true | all-gather | bytes 786432 | tf_op jit(solution)/shard_map/all_gather | solution.py:244
  211.0 0.0 all-to-all-done.6.refs_5_
  211.0 4.9 %shard_map.107 = (f32[8,32,128]{2,1,0:T(8,128)S(1)}, bf16[8,8,32,128]{3,2,1,0:T(8,128)(2,1)S(1)}, bf16[3,2,32,128]{3,2,1,0:T(8,128)(2,1)S(1)}) custom-call(s32[13]{0:T(128)S(1)} %copy-done.7, s32[32]{0:T(128)S(1)} %copy-done.6, s32[8,12]{1,0:T(8,128)S(1)} %copy-done.2, s32[8,32]{1,0:T(8,128)S(1)} %copy-done.5, bf16[64,32,128]{2,1,0:T(8,128)(2,1)S(1)} %bitcast.25, ...), custom_call_target="tpu_custom_call" | custom-call | flops 369098752 | bytes 11534336 | tf_op jit(solution)/shard_map/pallas_call | solution.py:285
  216.0 17.7 %all_to_all.53 = bf16[8,8,32,128]{3,2,1,0:T(8,128)(2,1)S(1)} all-to-all(bf16[8,8,32,128]{3,2,1,0:T(8,128)(2,1)S(1)} %get-tuple-element.77), channel_id=1, replica_groups=mesh['area'=32,'pop'=8] {'pop'}, dimensions={0} | all-to-all | bytes 1048576 | tf_op jit(solution)/shard_map/all_to_all | solution.py:237
  233.6 5.0 %shard_map.108 = (f32[8,32,128]{2,1,0:T(8,128)S(1)}, bf16[1,8,32,128]{3,2,1,0:T(8,128)(2,1)S(1)}, bf16[3,2,32,128]{3,2,1,0:T(8,128)(2,1)S(1)}, bf16[32,4,32,128]{3,2,1,0:T(8,128)(2,1)}) custom-call(s32[13]{0:T(128)S(1)} %copy-done.7, s32[32]{0:T(128)S(1)} %copy-done.6, s32[8,12]{1,0:T(8,128)S(1)} %copy-done.2, s32[8,32]{1,0:T(8,128)S(1)} %copy-done.4, ...), custom_call_target="tpu_custom_call" | custom-call | flops 369098752 | bytes 11534336 | tf_op jit(solution)/shard_map/pallas_call | solution.py:285
  238.6 7.1 %all-to-all-start.8 = ((bf16[32,4,32,128]{3,2,1,0:T(8,128)(2,1)}), bf16[32,4,32,128]{3,2,1,0:T(8,128)(2,1)S(1)}, u32[]{:S(2)}, u32[]{:S(2)}) async-start(bf16[32,4,32,128]{3,2,1,0:T(8,128)(2,1)} %get-tuple-element.81), calls=%async_computation.8 | async-start | bytes 2097152 | tf_op jit(solution)/shard_map/all_to_all | solution.py:237
  245.7 14.8 %all_gather.38 = bf16[4,8,32,128]{3,2,1,0:T(8,128)(2,1)S(1)} all-gather(bf16[1,8,32,128]{3,2,1,0:T(8,128)(2,1)S(1)} %get-tuple-element.80), channel_id=1, replica_groups={{0,2,4,6},{1,3,5,7},{8,10,12,14},{9,11,13,15},{16,18,20,22},{17,19,21,2..., dimensions={0}, use_global_device_ids=true | all-gather | bytes 327680 | tf_op jit(solution)/shard_map/all_gather | solution.py:243
  260.6 7.0 %all_gather.39 = bf16[8,8,32,128]{3,2,1,0:T(8,128)(2,1)S(1)} all-gather(bf16[4,8,32,128]{3,2,1,0:T(8,128)(2,1)S(1)} %all_gather.38), channel_id=1, replica_groups={{0,1},{2,3},{4,5},{6,7},{8,9},{10,11},{12,13},{14,15},{16,17},{18,19},{..., dimensions={0}, use_global_device_ids=true | all-gather | bytes 786432 | tf_op jit(solution)/shard_map/all_gather | solution.py:244
  267.6 0.0 all-to-all-done.8.refs_5_
  267.6 4.9 %shard_map.109 = (f32[8,32,128]{2,1,0:T(8,128)S(1)}, bf16[8,8,32,128]{3,2,1,0:T(8,128)(2,1)S(1)}, bf16[3,2,32,128]{3,2,1,0:T(8,128)(2,1)S(1)}) custom-call(s32[13]{0:T(128)S(1)} %copy-done.7, s32[32]{0:T(128)S(1)} %copy-done.6, s32[8,12]{1,0:T(8,128)S(1)} %copy-done.2, s32[8,32]{1,0:T(8,128)S(1)} %copy-done.5, bf16[64,32,128]{2,1,0:T(8,128)(2,1)S(1)} %bitcast.21, ...), custom_call_target="tpu_custom_call" | custom-call | flops 369098752 | bytes 11534336 | tf_op jit(solution)/shard_map/pallas_call | solution.py:285
  272.6 17.8 %all_to_all.54 = bf16[8,8,32,128]{3,2,1,0:T(8,128)(2,1)S(1)} all-to-all(bf16[8,8,32,128]{3,2,1,0:T(8,128)(2,1)S(1)} %get-tuple-element.84), channel_id=1, replica_groups=mesh['area'=32,'pop'=8] {'pop'}, dimensions={0} | all-to-all | bytes 1048576 | tf_op jit(solution)/shard_map/all_to_all | solution.py:237
  290.4 5.6 %shard_map.110 = f32[8,32,128]{2,1,0:T(8,128)} custom-call(s32[13]{0:T(128)S(1)} %copy-done.7, s32[32]{0:T(128)S(1)} %copy-done.6, s32[8,12]{1,0:T(8,128)S(1)} %copy-done.2, s32[8,32]{1,0:T(8,128)S(1)} %copy-done.4, bf16[64,32,128]{2,1,0:T(8,128)(2,1)S(1)} %bitcast.26, bf16[32,4,32,128]{3,2,1,0:T(8,128)(2,1)S(1)} %all-to-all-done.8.refs_5_, ...), custom_call_target="tpu_custom_call" | custom-call | flops 369098752 | bytes 11534336 | tf_op jit(solution)/shard_map/pallas_call | solution.py:285
Async XLA Ops:
  1.3 37.9 %copy-start.6 = (s32[32]{0:T(128)S(1)}, s32[32]{0:T(128)}, u32[]{:S(2)}) copy-start(s32[32]{0:T(128)} %select_reduce_fusion.delay_ref.refs_1_) | copy-start | bytes 388
  5.1 34.2 %copy-start = (bf16[8,32,128]{2,1,0:T(8,128)(2,1)S(1)}, bf16[8,32,128]{2,1,0:T(8,128)(2,1)}, u32[]{:S(2)}) copy-start(bf16[8,32,128]{2,1,0:T(8,128)(2,1)} %get-tuple-element.52.refs_9_) | copy-start | bytes 196612
  5.1 34.2 %copy-start.1 = (f32[8,128]{1,0:T(8,128)S(1)}, f32[8,128]{1,0:T(8,128)}, u32[]{:S(2)}) copy-start(f32[8,128]{1,0:T(8,128)} %get-tuple-element.53.refs_10_) | copy-start | bytes 12292
  5.1 34.2 %copy-start.2 = (s32[8,12]{1,0:T(8,128)S(1)}, s32[8,12]{1,0:T(8,128)}, u32[]{:S(2)}) copy-start(s32[8,12]{1,0:T(8,128)} %get-tuple-element.47.refs_2_) | copy-start | bytes 1156
  5.1 34.2 %copy-start.3 = (f32[8,32,128]{2,1,0:T(8,128)S(1)}, f32[8,32,128]{2,1,0:T(8,128)}, u32[]{:S(2)}) copy-start(f32[8,32,128]{2,1,0:T(8,128)} %get-tuple-element.54.refs_11_) | copy-start | bytes 393220
  5.1 34.2 %copy-start.5 = (s32[8,32]{1,0:T(8,128)S(1)}, s32[8,32]{1,0:T(8,128)}, u32[]{:S(2)}) copy-start(s32[8,32]{1,0:T(8,128)} %get-tuple-element.49.refs_3_) | copy-start | bytes 3076
  5.1 34.2 %copy-start.7 = (s32[13]{0:T(128)S(1)}, s32[13]{0:T(128)}, u32[]{:S(2)}) copy-start(s32[13]{0:T(128)} %get-tuple-element.46.refs_0_) | copy-start | bytes 160
  5.1 34.2 %copy-start.8 = (bf16[3,2,32,128]{3,2,1,0:T(8,128)(2,1)S(1)}, bf16[3,2,32,128]{3,2,1,0:T(8,128)(2,1)}, u32[]{:S(2)}) copy-start(bf16[3,2,32,128]{3,2,1,0:T(8,128)(2,1)} %get-tuple-element.55.refs_12_) | copy-start | bytes 147460
  5.1 34.1 %all-to-all-start = ((bf16[32,4,32,128]{3,2,1,0:T(8,128)(2,1)}), bf16[32,4,32,128]{3,2,1,0:T(8,128)(2,1)S(1)}, u32[]{:S(2)}, u32[]{:S(2)}) async-start(bf16[32,4,32,128]{3,2,1,0:T(8,128)(2,1)} %get-tuple-element.51), calls=%async_computation | async-start | bytes 2097152 | tf_op jit(solution)/shard_map/all_to_all | solution.py:237
  39.3 24.2 %copy-start.4 = (s32[8,32]{1,0:T(8,128)S(1)}, s32[8,32]{1,0:T(8,128)}, u32[]{:S(2)}) copy-start(s32[8,32]{1,0:T(8,128)} %get-tuple-element.48.refs_3_) | copy-start | bytes 3076
  68.5 29.3 %all-to-all-start.2 = ((bf16[32,4,32,128]{3,2,1,0:T(8,128)(2,1)}), bf16[32,4,32,128]{3,2,1,0:T(8,128)(2,1)S(1)}, u32[]{:S(2)}, u32[]{:S(2)}) async-start(bf16[32,4,32,128]{3,2,1,0:T(8,128)(2,1)} %get-tuple-element.60), calls=%async_computation.2 | async-start | bytes 2097152 | tf_op jit(solution)/shard_map/all_to_all | solution.py:237
  125.2 29.0 %all-to-all-start.4 = ((bf16[32,4,32,128]{3,2,1,0:T(8,128)(2,1)}), bf16[32,4,32,128]{3,2,1,0:T(8,128)(2,1)S(1)}, u32[]{:S(2)}, u32[]{:S(2)}) async-start(bf16[32,4,32,128]{3,2,1,0:T(8,128)(2,1)} %get-tuple-element.67), calls=%async_computation.4 | async-start | bytes 2097152 | tf_op jit(solution)/shard_map/all_to_all | solution.py:237
  182.0 29.0 %all-to-all-start.6 = ((bf16[32,4,32,128]{3,2,1,0:T(8,128)(2,1)}), bf16[32,4,32,128]{3,2,1,0:T(8,128)(2,1)S(1)}, u32[]{:S(2)}, u32[]{:S(2)}) async-start(bf16[32,4,32,128]{3,2,1,0:T(8,128)(2,1)} %get-tuple-element.74), calls=%async_computation.6 | async-start | bytes 2097152 | tf_op jit(solution)/shard_map/all_to_all | solution.py:237
  238.6 29.0 %all-to-all-start.8 = ((bf16[32,4,32,128]{3,2,1,0:T(8,128)(2,1)}), bf16[32,4,32,128]{3,2,1,0:T(8,128)(2,1)S(1)}, u32[]{:S(2)}, u32[]{:S(2)}) async-start(bf16[32,4,32,128]{3,2,1,0:T(8,128)(2,1)} %get-tuple-element.81), calls=%async_computation.8 | async-start | bytes 2097152 | tf_op jit(solution)/shard_map/all_to_all | solution.py:237
